TPU v7x, 32 devices: a whole 2x2x4 slice. The times are simulated.
32 devices in a mesh: rep: 2 (over x), atom: 16 (over z, y, core).
Axes of the slice: x: 2, y: 2, z: 4, core: 2. Of those that a mesh axis runs over, the one named last changes fastest.
Arguments:
- features: bfloat16 [4096, 256], P(('rep', 'atom')), parts along dimension 0, may hold values from -6 to 6
- fractional: float32 [3, 4096], P(None, ('rep', 'atom')), parts along dimension 1, may hold values from 0 to 1, as said below
- distances: float32 [64, 4096], P(None, ('rep', 'atom')), parts along dimension 1, may hold values from 0.8 to 4.8
- neighbours: int32 [64, 4096], P(None, ('rep', 'atom')), parts along dimension 1, may hold values from 0 to 383
- edge_mask: int32 [64, 4096], P(None, ('rep', 'atom')), parts along dimension 1, may hold values 0 or 1
- wave_index: int32 [3, 2048], replicated, may hold values from -6 to 6
- w_rbf: bfloat16 [2, 64, 512], replicated, may hold values from -1.5 to 1.5
- w_filter: bfloat16 [2, 512, 256], replicated, may hold values from -0.25 to 0.25
- w_mixing: bfloat16 [2, 256, 256], replicated, may hold values from -0.375 to 0.375
- w_short: bfloat16 [2, 256, 256], replicated, may hold values from -0.375 to 0.375
- w_long: bfloat16 [2, 256, 256], replicated, may hold values from -0.375 to 0.375
Outputs:
- features_out: bfloat16 [4096, 256], P(('rep', 'atom')), parts along dimension 0
There are 2 independent parts, one for each index of `rep`. A program takes and returns all parts, laid end to end along the dimension named above; an argument that names none is the same for every part. Nothing has to cross between parts.
Inputs may be any that keep to these rules, and one draw needn't show every extreme that they name: neighbours[n, i] indexes the concatenation of the previous brick, atom i's own brick and the next brick, cyclic over the 16 bricks. `fractional`: atom i has its z coordinate within brick i // 128, that is between (i // 128) * 128 / 2048 and one brick further.
All inputs are finite; a program needn't handle non-finite values. No bound on the sum of `edge_mask` on one device may be relied on, other than what follows from the above.
Results may differ from a plain program's by a relative error of at most 0.01.
Values may be sent and summed in bfloat16 or wider, within the bound.
No kernel may reach another device: no remote copies, remote signals or barrier semaphores. Data moves between devices by JAX's collectives and lax.ppermute only.
A program may use at most 64 MiB of HBM per device.

v0:
```python
import functools
import math

import jax
import jax.numpy as jnp
from jax import lax
from jax.experimental import pallas as pl
from jax.experimental.pallas import tpu as pltpu
from jax.sharding import PartitionSpec as P


message_group = 16
reach = 6
orders = reach + 1
columns = 16
plane = (reach + 2) * columns
extra_rows = 16
limit = pltpu.CompilerParams(vmem_limit_bytes=20 << 20)
BF = jnp.bfloat16
F32 = jnp.float32


def dot(a, b):
    return jnp.dot(a, b, preferred_element_type=F32)


def dot_dims(a, b, ca, cb):
    return lax.dot_general(a, b, (((ca,), (cb,)), ((), ())), preferred_element_type=F32)


def turn_trig(turns):
    part = turns - jnp.round(turns)
    angle = part * (2.0 * math.pi)
    square = angle * angle
    cosine = jnp.full_like(square, 1.0 / math.factorial(20))
    for n in range(18, -2, -2):
        cosine = cosine * -square + 1.0 / math.factorial(n)
    sine = jnp.full_like(square, 1.0 / math.factorial(21))
    for n in range(19, -1, -2):
        sine = sine * -square + 1.0 / math.factorial(n)
    return cosine, sine * angle


def plane_phases(position):
    rows = position.shape[1]
    x, y = position[0:1], position[1:2]
    first = lax.broadcasted_iota(jnp.int32, (8, rows), 0).astype(F32)
    second = lax.broadcasted_iota(jnp.int32, (columns, rows), 0).astype(F32) - reach
    xc, xs = turn_trig(first * x)
    yc, ys = turn_trig(second * y)
    cosines, sines = [], []
    for a in range(plane // columns):
        pc, ps = xc[a : a + 1], xs[a : a + 1]
        cosines.append(pc * yc - ps * ys)
        sines.append(pc * ys + ps * yc)
    return jnp.concatenate(cosines, axis=0), jnp.concatenate(sines, axis=0)


def in_hbm(x):
    return pltpu.with_memory_space_constraint(x, pltpu.HBM)


VM = pl.BlockSpec(memory_space=pltpu.VMEM)
RAW = pl.BlockSpec(memory_space=pl.ANY)


def whole(x):
    return pl.BlockSpec(x.shape, lambda i: (0,) * len(x.shape))


def prepare_kernel(wave_ref, position_ref, own_ref, packed_ref, left_ref, zc_ref, zs_ref):
    rows = position_ref.shape[1]
    position = position_ref[...]
    top = position.astype(BF)
    rest = position - top.astype(F32)
    middle = rest.astype(BF)
    low = (rest - middle.astype(F32)).astype(BF)
    blank = jnp.zeros((extra_rows, 2 * rows), BF)
    packed_ref[:rows, :] = own_ref[...]
    packed_ref[rows:, :] = blank
    packed_ref[rows : rows + 3, :rows] = top
    packed_ref[rows : rows + 3, rows : 2 * rows] = middle
    packed_ref[rows + 3 : rows + 6, :rows] = low

    waves = wave_ref.shape[1]
    m0, m1, m2 = wave_ref[0:1, :], wave_ref[1:2, :], wave_ref[2:3, :]
    flip = jnp.logical_or(m0 < 0, jnp.logical_and(m0 == 0, m1 < 0))
    sign = jnp.where(flip, -1, 1)
    code = m0 * sign * columns + m1 * sign + reach
    height = m2 * sign
    row = lax.broadcasted_iota(jnp.int32, (plane, waves), 0)
    chosen = jnp.where(row == code, 1.0, 0.0).astype(BF)
    order = lax.broadcasted_iota(jnp.int32, (16, waves), 0)
    weight = jnp.where(order < 8, 1, jnp.where(height < 0, -1, 1)).astype(F32)
    picked = jnp.where(jnp.abs(height) == order % 8, weight, 0.0).astype(BF)
    count = dot_dims(picked, chosen, 1, 1)
    lane = lax.broadcasted_iota(jnp.int32, (16, plane), 1)
    k0 = (lane // columns).astype(F32)
    k1 = (lane % columns - reach).astype(F32)
    k2 = (lax.broadcasted_iota(jnp.int32, (16, plane), 0) % 8).astype(F32)
    strength = count / (1.0 + (k0 * k0 + k1 * k1 + k2 * k2) / 16.0)

    cosine, sine = plane_phases(position)
    cosine, sine = cosine.T, sine.T
    for m in range(orders):
        even = strength[m : m + 1]
        left_ref[m, :, :plane] = (cosine * even).astype(BF)
        left_ref[m, :, plane:] = (sine * even).astype(BF)
        if m:
            odd = strength[8 + m : 9 + m]
            left_ref[reach + m, :, :plane] = (sine * -odd).astype(BF)
            left_ref[reach + m, :, plane:] = (cosine * odd).astype(BF)
    zc, zs = turn_trig(position[2:3])
    zc_ref[...] = jnp.broadcast_to(zc, (rows, rows)).T
    zs_ref[...] = jnp.broadcast_to(zs, (rows, rows)).T


def prepare(wave_index, position, own):
    rows = position.shape[1]
    shapes = (
        jax.ShapeDtypeStruct((rows + extra_rows, own.shape[1]), BF),
        jax.ShapeDtypeStruct((2 * reach + 1, rows, 2 * plane), BF),
        jax.ShapeDtypeStruct((rows, rows), F32),
        jax.ShapeDtypeStruct((rows, rows), F32),
    )
    inputs = (wave_index, position, own)
    return pl.pallas_call(
        prepare_kernel,
        out_shape=shapes,
        grid=(1,),
        in_specs=[whole(x) for x in inputs],
        out_specs=tuple(whole(x) for x in shapes),
        compiler_params=limit,
        name="prepare",
    )(*[in_hbm(x) for x in inputs])


def coupling_kernel(places, rows, left_ref, zc_ref, zs_ref, *refs):
    count = max(p[0] for p in places) + 1
    packed, out_ref, right_ref, part_ref = refs[:count], refs[count], refs[count + 1], refs[count + 2]
    tile = 32
    for pair in range(0, len(places), 2):
        span = min(2, len(places) - pair)
        heights = []
        for side in range(span):
            which, start = places[pair + side]
            block = packed[which][start + rows : start + rows + extra_rows, :].astype(F32)
            position = (block[0:3, :rows] + block[0:3, rows : 2 * rows]) + block[3:6, :rows]
            cosine, sine = plane_phases(position)
            at = slice(side * rows, (side + 1) * rows)
            right_ref[:plane, at] = cosine.astype(BF)
            right_ref[plane:, at] = sine.astype(BF)
            heights.append(turn_trig(position[2:3]))
        wide = span * rows
        for m in range(2 * reach + 1):
            part_ref[m, :, :wide] = dot(left_ref[m], right_ref[:, :wide])
        for side in range(span):
            zc, zs = heights[side]
            at = slice(side * rows, (side + 1) * rows)
            for top in range(0, rows, tile):
                own = slice(top, top + tile)
                oc, os = zc_ref[own, :], zs_ref[own, :]
                c1 = oc * zc + os * zs
                s1 = os * zc - oc * zs
                twice = c1 + c1
                total = part_ref[0, own, at] + c1 * part_ref[1, own, at] + s1 * part_ref[reach + 1, own, at]
                c0, s0 = jnp.ones_like(c1), jnp.zeros_like(s1)
                for m in range(2, orders):
                    c0, c1 = c1, twice * c1 - c0
                    s0, s1 = s1, twice * s1 - s0
                    total = total + c1 * part_ref[m, own, at] + s1 * part_ref[reach + m, own, at]
                out_ref[own, pair * rows + side * rows : pair * rows + (side + 1) * rows] = total.astype(BF)


def coupling(prepared, arrays, places, rows):
    left, zc, zs = prepared
    return pl.pallas_call(
        functools.partial(coupling_kernel, tuple(places), rows),
        out_shape=jax.ShapeDtypeStruct((rows, len(places) * rows), BF),
        scratch_shapes=[
            pltpu.VMEM((2 * plane, 2 * rows), BF),
            pltpu.VMEM((2 * reach + 1, rows, 2 * rows), F32),
        ],
        in_specs=[pl.BlockSpec(memory_space=pltpu.VMEM)] * (3 + len(arrays)),
        out_specs=pl.BlockSpec(memory_space=pltpu.VMEM),
        name="coupling",
        compiler_params=limit,
    )(left, zc, zs, *arrays)


def coupling_of(prepared, arrays, places, blocks, rows):
    used = sorted({places[q][0] for q in blocks})
    spots = [(used.index(places[q][0]), places[q][1]) for q in blocks]
    return coupling(prepared, [arrays[n] for n in used], spots, rows)


def filter_kernel(layer, begin, fetch, distance_ref, rbf_ref, filter_ref, out_ref, *scratch):
    group, rows, _ = out_ref.shape
    at = slice(begin, begin + group)
    copies = []
    if fetch:
        sources = (distance_ref.at[at], rbf_ref.at[layer], filter_ref.at[layer])
        copies = [
            pltpu.make_async_copy(source, target, scratch[3].at[n])
            for n, (source, target) in enumerate(zip(sources, scratch))
        ]
        for copy in copies:
            copy.start()
        copies[0].wait()
        distance = scratch[0][...]
    else:
        distance = distance_ref[at, :]
    count = rbf_ref.shape[1]
    step = lax.broadcasted_iota(jnp.int32, (count, rows), 0).astype(F32)
    centers = 0.5 + 4.5 * step / (count - 1)
    pieces = []
    for s in range(group):
        offset = distance[s : s + 1, :] - centers
        pieces.append(jnp.exp(-4.0 * offset * offset).astype(BF))
    basis = jnp.concatenate(pieces, axis=1)
    if fetch:
        copies[1].wait()
    first = scratch[1][...] if fetch else rbf_ref[layer]
    half = dot_dims(basis, first * jnp.asarray(0.5, BF), 0, 0)
    inner = (half + half * jnp.tanh(half)).astype(BF)
    if fetch:
        copies[2].wait()
    second = scratch[2][...] if fetch else filter_ref[layer]
    out_ref[...] = dot(inner, second).astype(BF).reshape(out_ref.shape)


def filters_of(distances, w_rbf, w_filter, layer, begin, count, fetch):
    rows = distances.shape[1]
    width = w_filter.shape[2]
    inputs = (distances, w_rbf, w_filter)
    if fetch:
        inputs = tuple(in_hbm(x) for x in inputs)
        scratch = [
            pltpu.VMEM((count, rows), F32),
            pltpu.VMEM(w_rbf.shape[1:], BF),
            pltpu.VMEM(w_filter.shape[1:], BF),
            pltpu.SemaphoreType.DMA((3,)),
        ]
    else:
        scratch = []
    return pl.pallas_call(
        functools.partial(filter_kernel, layer, begin, fetch),
        out_shape=jax.ShapeDtypeStruct((count, rows, width), BF),
        in_specs=[RAW if fetch else VM] * 3,
        out_specs=VM,
        scratch_shapes=scratch,
        compiler_params=limit,
        name="filters",
    )(*inputs)


def message_kernel(index_ref, distance_ref, mask_ref, table_ref, *refs):
    filter_refs, out_ref = refs[:-1], refs[-1]
    slots, rows = index_ref.shape
    reachable, width = table_ref.shape
    group = message_group
    lane = lax.broadcasted_iota(jnp.int32, (rows, reachable), 1)
    total = jnp.zeros((rows, width), F32)
    per = slots // len(filter_refs)
    for begin in range(0, slots, group):
        at = slice(begin, begin + group)
        index = index_ref[at, :].astype(F32).T.astype(jnp.int32)
        cosine, _ = turn_trig(distance_ref[at, :] * 0.1)
        weight = (0.5 * (cosine + 1.0) * mask_ref[at, :].astype(F32)).T
        picks = [
            jnp.where(lane == index[:, s : s + 1], weight[:, s : s + 1], 0.0).astype(BF)
            for s in range(group)
        ]
        gathered = dot(jnp.concatenate(picks, axis=0), table_ref[...]).reshape(group, rows, width)
        where = begin % per
        factors = filter_refs[begin // per][where : where + group].astype(F32)
        total = total + jnp.sum(gathered * factors, axis=0)
    out_ref[...] = total.astype(BF)


def messages(neighbours, distances, edge_mask, table, filters):
    rows = neighbours.shape[1]
    width = table.shape[1]
    inputs = (neighbours, distances, edge_mask, table) + tuple(filters)
    return pl.pallas_call(
        message_kernel,
        out_shape=jax.ShapeDtypeStruct((rows, width), BF),
        in_specs=[VM] * len(inputs),
        out_specs=VM,
        compiler_params=limit,
        name="messages",
    )(*inputs)


def update_kernel(places, layer, before, after, own_ref, message_ref, mixing_ref, short_ref, long_ref, *refs):
    rows, width = own_ref.shape
    counts = sorted({p[0] for p in places})
    pairs = len({p[2] for p in places})
    matrices, states, out_ref = refs[:pairs], refs[pairs : pairs + len(counts)], refs[-1]
    total = jnp.zeros((rows, width), F32)
    for which, start, matrix, column in places:
        total = total + dot(
            matrices[matrix][:, column * rows : (column + 1) * rows], states[which][start : start + rows, :]
        )
    potential = dot((total * before).astype(BF), mixing_ref[layer]).astype(BF)
    field = (potential.astype(F32) * after).astype(BF)
    half = 0.5 * (dot(message_ref[...], short_ref[layer]) + dot(field, long_ref[layer]))
    out_ref[...] = (own_ref[...].astype(F32) + (half + half * jnp.tanh(half))).astype(BF)


def update(own, message, weights, layer, matrices, arrays, places, before, after):
    rows, width = own.shape
    return pl.pallas_call(
        functools.partial(update_kernel, tuple(places), layer, before, after),
        out_shape=jax.ShapeDtypeStruct((rows, width), BF),
        in_specs=[VM] * (5 + len(matrices) + len(arrays)),
        out_specs=VM,
        compiler_params=limit,
        name="update",
    )(own, message, *weights, *matrices, *arrays)


def swap(x, mask):
    count = lax.axis_size("atom")
    return lax.ppermute(x, "atom", [(i, i ^ mask) for i in range(count)])


def schedule(count):
    bits = [1 << n for n in range(count.bit_length() - 1)][::-1]
    stages, have = [], [0]
    if len(bits) >= 4:
        far, near, side, last = bits[0], bits[1], bits[2], bits[-1]
        first = [far + near, far, near, side]
        stages.append([(mask, [0]) for mask in first + [last]])
        stages.append([(side, first[:3]), (last, first)])
        stages.append([(last, [side + mask for mask in first[:3]])])
        have = [0] + first + [side + mask for mask in first[:3]]
        have = have + [q ^ last for q in have]
        bits = bits[3:-1]
    for bit in bits:
        stages.append([(bit, list(have))])
        have = have + [q ^ bit for q in have]
    return stages


def exchange(arrays, places, stage, size):
    arrays, places = list(arrays), dict(places)
    sends = []
    for mask, wanted in stage:
        parts = [
            lax.slice_in_dim(arrays[places[q][0]], places[q][1], places[q][1] + size, axis=0)
            for q in wanted
        ]
        sends.append(parts[0] if len(parts) == 1 else jnp.concatenate(parts, axis=0))
    fresh = {}
    for (mask, wanted), sent in zip(stage, sends):
        arrays.append(swap(sent, mask))
        for n, q in enumerate(wanted):
            fresh[q ^ mask] = (len(arrays) - 1, n * size)
    places.update(fresh)
    return arrays, places


def neighbour_table(own, close, even):
    count = lax.axis_size("atom")
    far = lax.ppermute(
        own, "atom", [(i, (i + (count - 1 if i % 2 == 0 else 1)) % count) for i in range(count)]
    )
    return jnp.concatenate([jnp.where(even, far, close), own, jnp.where(even, close, far)], axis=0)


def per_device(
    features,
    fractional,
    distances,
    neighbours,
    edge_mask,
    wave_index,
    w_rbf,
    w_filter,
    w_mixing,
    w_short,
    w_long,
):
    rows, _ = features.shape
    slots = neighbours.shape[0]
    bricks = lax.axis_size("atom")
    before = 1.0 / math.sqrt(rows * bricks)
    after = 4.0 / math.sqrt(wave_index.shape[1])
    even = lax.axis_index("atom") % 2 == 0
    stages = schedule(bricks)

    packed, *prepared = prepare(wave_index, fractional, features)
    split = slots // 2
    state = features
    matrices, order = [], []

    def couple(arrays, places):
        ready = [q for q in places if q not in order]
        matrices.append(coupling_of(prepared, arrays, places, ready, rows))
        order.extend(ready)

    for layer in range(w_rbf.shape[0]):
        block = state if layer else packed
        size = block.shape[0]
        arrays, places = exchange([block], {0: (0, 0)}, stages[0], size)
        close = arrays[places[1][0]][:rows] if 1 in places else swap(state, 1)
        table = neighbour_table(state, close, even)
        first = filters_of(distances, w_rbf, w_filter, layer, 0, split, layer == 0)
        second = filters_of(distances, w_rbf, w_filter, layer, split, slots - split, False)
        message = messages(neighbours, distances, edge_mask, table, (first, second))
        for stage in stages[1:]:
            if layer == 0:
                couple(arrays, places)
            arrays, places = exchange(arrays, places, stage, size)
        if layer == 0:
            couple(arrays, places)
        spots, at = [], 0
        for number, matrix in enumerate(matrices):
            for column in range(matrix.shape[1] // rows):
                spots.append(places[order[at]] + (number, column))
                at += 1
        weights = (w_mixing, w_short, w_long)
        state = update(
            state, message, weights, layer, matrices, arrays, spots, before, after
        )
    return state


def solution(mesh):
    along = P(None, ("rep", "atom"))
    in_specs = (P(("rep", "atom"), None), along, along, along, along) + (P(),) * 6
    return jax.shard_map(
        per_device, mesh=mesh, in_specs=in_specs, out_specs=P(("rep", "atom"), None), check_vma=False
    )
```

profile of v0, /device:TPU:0, one launch (start us, length us, event | category | flops | bytes accessed | tf_op | source)
XLA Modules:
  0.0 71.5 jit_solution(18278813648203838658)
XLA Ops:
  0.0 1.9 %prepare.1 = (bf16[144,256]{1,0:T(8,128)(2,1)}, bf16[13,128,256]{2,1,0:T(8,128)(2,1)S(1)}, f32[128,128]{1,0:T(8,128)S(1)}, f32[128,128]{1,0:T(8,128)S(1)}) custom-call(s32[3,2048]{1,0:T(4,128)} %wave_ref.1, f32[3,128]{1,0:T(4,128)} %position_ref.1, bf16[128,256]{1,0:T(8,128)(2,1)} %own_ref.3), custom_call_target="tpu_custom_call" | custom-call | tf_op jit(solution)/shard_map/prepare/pallas_call | solution.py:127
  1.9 0.6 copy-done.15
  2.5 0.6 copy-done.17
  3.2 5.1 %collective-permute-start.2 = (bf16[144,256]{1,0:T(8,128)(2,1)}, bf16[144,256]{1,0:T(8,128)(2,1)S(1)}, u32[]{:S(2)}, u32[]{:S(2)}) collective-permute-start(bf16[144,256]{1,0:T(8,128)(2,1)} %get-tuple-element.9.refs_0_.refs_3_), channel_id=1, source_target_pairs={{0,12},{1,13},{2,14},{3,15},{4,8},{5,9},{6,10},{7,11},{8,4},{9,5},... | collective-permute-start | bytes 221192 | tf_op jit(solution)/shard_map/ppermute | solution.py:325
  8.2 0.0 collective-permute-start.3
  8.2 0.6 collective-permute-start.4
  8.8 2.4 %collective-permute-done.2.refs_1_.refs_4_ = bf16[144,256]{1,0:T(8,128)(2,1)S(1)} collective-permute-done((bf16[144,256]{1,0:T(8,128)(2,1)}, bf16[144,256]{1,0:T(8,128)(2,1)S(1)}, u32[]{:S(2)}, u32[]{:S(2)}) %collective-permute-start.2) | collective-permute-done | bytes 73760 | tf_op jit(solution)/shard_map/ppermute | solution.py:325
  11.2 3.4 %collective-permute-done.3.refs_2_.refs_5_ = bf16[144,256]{1,0:T(8,128)(2,1)S(1)} collective-permute-done((bf16[144,256]{1,0:T(8,128)(2,1)}, bf16[144,256]{1,0:T(8,128)(2,1)S(1)}, u32[]{:S(2)}, u32[]{:S(2)}) %collective-permute-start.3) | collective-permute-done | bytes 73760 | tf_op jit(solution)/shard_map/ppermute | solution.py:325
  14.7 0.0 collective-permute-done.4.refs_3_.refs_6_
  14.7 0.7 %pad_maximum_fusion.2 = bf16[432,256]{1,0:T(8,128)(2,1)} fusion(bf16[144,256]{1,0:T(8,128)(2,1)S(1)} %collective-permute-done.4.refs_3_.refs_6_, bf16[144,256]{1,0:T(8,128)(2,1)S(1)} %collective-permute-done.3.refs_2_.refs_5_, bf16[144,256]{1,0:T(8,128)(2,1)S(1)} %collective-permute-done.2.refs_1_.refs_4_), kind=kLoop, calls=%fused_computation.2 | loop fusion | flops 663552 | bytes 442368 | tf_op jit(solution)/shard_map/concatenate | solution.py:354
  15.4 1.5 %collective-permute-start.6 = (bf16[432,256]{1,0:T(8,128)(2,1)}, bf16[432,256]{1,0:T(8,128)(2,1)}, u32[]{:S(2)}, u32[]{:S(2)}) collective-permute-start(bf16[432,256]{1,0:T(8,128)(2,1)} %pad_maximum_fusion.2), channel_id=1, source_target_pairs={{0,2},{1,3},{2,0},{3,1},{4,6},{5,7},{6,4},{7,5},{8,10},{9,11},{10,... | collective-permute-start | bytes 663560 | tf_op jit(solution)/shard_map/ppermute | solution.py:325
  16.9 0.5 collective-permute-start.5
  17.4 1.0 %collective-permute-start = (bf16[128,256]{1,0:T(8,128)(2,1)}, bf16[128,256]{1,0:T(8,128)(2,1)}, u32[]{:S(2)}, u32[]{:S(2)}) collective-permute-start(bf16[128,256]{1,0:T(8,128)(2,1)} %own_ref.3), channel_id=1, source_target_pairs={{0,15},{1,2},{2,1},{3,4},{4,3},{5,6},{6,5},{7,8},{8,7},{9,10},{10,... | collective-permute-start | bytes 196616 | tf_op jit(solution)/shard_map/ppermute | solution.py:366
  18.4 0.7 collective-permute-start.1
  19.1 3.6 %filters.4.refs_0_ = bf16[32,128,256]{2,1,0:T(8,128)(2,1)S(1)} custom-call(f32[64,128]{1,0:T(8,128)} %distance_ref.11, bf16[2,64,512]{2,1,0:T(8,128)(2,1)} %rbf_ref.7, bf16[2,512,256]{2,1,0:T(8,128)(2,1)} %filter_ref.7), custom_call_target="tpu_custom_call" | custom-call | tf_op jit(solution)/shard_map/filters/pallas_call | solution.py:246
  22.7 0.0 copy-start.20
  22.8 2.7 %filters.5.refs_1_ = bf16[32,128,256]{2,1,0:T(8,128)(2,1)S(1)} custom-call(f32[64,128]{1,0:T(8,128)S(1)} %copy-done.5, bf16[2,64,512]{2,1,0:T(8,128)(2,1)S(1)} %copy-done.3, bf16[2,512,256]{2,1,0:T(8,128)(2,1)S(1)} %copy-done.2), custom_call_target="tpu_custom_call" | custom-call | tf_op jit(solution)/shard_map/filters/pallas_call | solution.py:246
  25.5 1.4 %copy-done = bf16[32,128,256]{2,1,0:T(8,128)(2,1)} copy-done((bf16[32,128,256]{2,1,0:T(8,128)(2,1)}, bf16[32,128,256]{2,1,0:T(8,128)(2,1)S(1)}, u32[]{:S(2)}) %copy-start) | copy-done | bytes 2097176
  26.8 0.0 collective-permute-done.5.refs_4_.refs_7_
  26.8 1.0 %pad_maximum_fusion = bf16[576,256]{1,0:T(8,128)(2,1)S(1)} fusion(bf16[144,256]{1,0:T(8,128)(2,1)} %collective-permute-done.5.refs_4_.refs_7_, bf16[144,256]{1,0:T(8,128)(2,1)} %copy-done.10, bf16[144,256]{1,0:T(8,128)(2,1)} %copy-done.8, bf16[144,256]{1,0:T(8,128)(2,1)} %copy-done.6), kind=kLoop, calls=%fused_computation | loop fusion | flops 1179648 | bytes 589824 | tf_op jit(solution)/shard_map/concatenate | solution.py:354
  27.8 0.1 collective-permute-start.7
  27.9 0.0 collective-permute-done.6.refs_0_.refs_9_
  27.9 0.5 collective-permute-start.8
  28.4 0.0 collective-permute-done
  28.4 0.0 collective-permute-done.1.refs_5_.refs_8_
  28.4 0.9 %broadcast_select_fusion.3 = (bf16[128,256]{1,0:T(8,128)(2,1)S(1)}, bf16[128,256]{1,0:T(8,128)(2,1)S(1)}) fusion(bf16[128,256]{1,0:T(8,128)(2,1)} %collective-permute-done, pred[]{:T(512)S(6)} %eq.5, bf16[144,256]{1,0:T(8,128)(2,1)} %collective-permute-done.1.refs_5_.refs_8_), kind=kLoop, calls=%fused_computation.9 | loop fusion | flops 65536 | bytes 262145 | tf_op jit(solution)/shard_map/jit(_where)/select_n | solution.py:369
  29.3 0.9 %pad_maximum_fusion.3.table_ref = bf16[384,256]{1,0:T(8,128)(2,1)S(1)} fusion(bf16[128,256]{1,0:T(8,128)(2,1)S(1)} %get-tuple-element.14, bf16[128,256]{1,0:T(8,128)(2,1)} %own_ref.3, bf16[128,256]{1,0:T(8,128)(2,1)S(1)} %get-tuple-element.13), kind=kLoop, calls=%fused_computation.3 | loop fusion | flops 589824 | bytes 393216 | tf_op jit(solution)/shard_map/concatenate | solution.py:369
  30.2 1.6 %copy-done.1 = bf16[32,128,256]{2,1,0:T(8,128)(2,1)S(1)} copy-done((bf16[32,128,256]{2,1,0:T(8,128)(2,1)S(1)}, bf16[32,128,256]{2,1,0:T(8,128)(2,1)}, u32[]{:S(2)}) %copy-start.1) | copy-done | bytes 2097176
  31.8 0.8 %copy-done.21 = s32[64,128]{1,0:T(8,128)S(1)} copy-done((s32[64,128]{1,0:T(8,128)S(1)}, s32[64,128]{1,0:T(8,128)}, u32[]{:S(2)}) %copy-start.21) | copy-done | bytes 32792
  32.6 3.2 %messages.2.message_ref = bf16[128,256]{1,0:T(8,128)(2,1)S(1)} custom-call(s32[64,128]{1,0:T(8,128)S(1)} %copy-done.20, f32[64,128]{1,0:T(8,128)S(1)} %copy-done.5, s32[64,128]{1,0:T(8,128)S(1)} %copy-done.21, bf16[384,256]{1,0:T(8,128)(2,1)S(1)} %pad_maximum_fusion.3.table_ref, bf16[32,128,256]{2,1,0:T(8,128)(2,1)S(1)} %filters.4.refs_0_, ...), custom_call_target="tpu_custom_call" | custom-call | tf_op jit(solution)/shard_map/messages/pallas_call | solution.py:285
  35.8 0.0 copy-start.12
  35.8 0.0 copy-start.13
  35.9 0.0 copy-start.14
  35.9 0.0 copy-start.19
  35.9 2.4 %coupling.3.refs_0_ = bf16[128,768]{1,0:T(8,128)(2,1)S(1)} custom-call(bf16[13,128,256]{2,1,0:T(8,128)(2,1)S(1)} %get-tuple-element.10.left_ref, f32[128,128]{1,0:T(8,128)S(1)} %copy-done.16, f32[128,128]{1,0:T(8,128)S(1)} %copy-done.18, bf16[144,256]{1,0:T(8,128)(2,1)} %get-tuple-element.9.refs_0_.refs_3_, bf16[144,256]{1,0:T(8,128)(2,1)S(1)} %copy-done.7, ...), custom_call_target="tpu_custom_call" | custom-call | tf_op jit(solution)/shard_map/coupling/pallas_call | solution.py:177
  38.3 0.0 collective-permute-done.7.refs_1_.refs_10_
  38.3 2.7 %coupling.4.refs_1_ = bf16[128,896]{1,0:T(8,128)(2,1)S(1)} custom-call(bf16[13,128,256]{2,1,0:T(8,128)(2,1)S(1)} %get-tuple-element.10.left_ref, f32[128,128]{1,0:T(8,128)S(1)} %copy-done.16, f32[128,128]{1,0:T(8,128)S(1)} %copy-done.18, bf16[432,256]{1,0:T(8,128)(2,1)} %collective-permute-done.6.refs_0_.refs_9_, ...), custom_call_target="tpu_custom_call" | custom-call | tf_op jit(solution)/shard_map/coupling/pallas_call | solution.py:177
  41.0 0.0 copy-start.4
  41.0 0.0 collective-permute-done.8.refs_0_.refs_11_
  41.0 0.8 %coupling.5.refs_2_ = bf16[128,384]{1,0:T(8,128)(2,1)S(1)} custom-call(bf16[13,128,256]{2,1,0:T(8,128)(2,1)S(1)} %get-tuple-element.10.left_ref, f32[128,128]{1,0:T(8,128)S(1)} %copy-done.16, f32[128,128]{1,0:T(8,128)S(1)} %copy-done.18, bf16[432,256]{1,0:T(8,128)(2,1)S(1)} %collective-permute-done.8.refs_0_.refs_11_), custom_call_target="tpu_custom_call" | custom-call | tf_op jit(solution)/shard_map/coupling/pallas_call | solution.py:177
  41.9 1.8 %update.2.own_ref.refs_3_ = bf16[128,256]{1,0:T(8,128)(2,1)S(1)} custom-call(bf16[128,256]{1,0:T(8,128)(2,1)S(1)} %copy-done.19, bf16[128,256]{1,0:T(8,128)(2,1)S(1)} %messages.2.message_ref, bf16[2,256,256]{2,1,0:T(8,128)(2,1)S(1)} %copy-done.12, bf16[2,256,256]{2,1,0:T(8,128)(2,1)S(1)} %copy-done.13, bf16[2,256,256]{2,1,0:T(8,128)(2,1)S(1)} %copy-done.14, ...), custom_call_target="tpu_custom_call" | custom-call | tf_op jit(solution)/shard_map/update/pallas_call | solution.py:313
  43.7 2.7 %collective-permute-start.11 = (bf16[128,256]{1,0:T(8,128)(2,1)S(1)}, bf16[128,256]{1,0:T(8,128)(2,1)S(1)}, u32[]{:S(2)}, u32[]{:S(2)}) collective-permute-start(bf16[128,256]{1,0:T(8,128)(2,1)S(1)} %update.2.own_ref.refs_3_), channel_id=1, source_target_pairs={{0,12},{1,13},{2,14},{3,15},{4,8},{5,9},{6,10},{7,11},{8,4},{9,5},... | collective-permute-start | bytes 196616 | tf_op jit(solution)/shard_map/ppermute | solution.py:325
  46.5 0.0 collective-permute-start.12
  46.5 1.7 %collective-permute-start.13 = (bf16[128,256]{1,0:T(8,128)(2,1)S(1)}, bf16[128,256]{1,0:T(8,128)(2,1)S(1)}, u32[]{:S(2)}, u32[]{:S(2)}) collective-permute-start(bf16[128,256]{1,0:T(8,128)(2,1)S(1)} %update.2.own_ref.refs_3_), channel_id=1, source_target_pairs={{0,4},{1,5},{2,6},{3,7},{4,0},{5,1},{6,2},{7,3},{8,12},{9,13},{10,... | collective-permute-start | bytes 196616 | tf_op jit(solution)/shard_map/ppermute | solution.py:325
  48.2 2.3 %collective-permute-done.11.refs_4_ = bf16[128,256]{1,0:T(8,128)(2,1)S(1)} collective-permute-done((bf16[128,256]{1,0:T(8,128)(2,1)S(1)}, bf16[128,256]{1,0:T(8,128)(2,1)S(1)}, u32[]{:S(2)}, u32[]{:S(2)}) %collective-permute-start.11) | collective-permute-done | bytes 65568 | tf_op jit(solution)/shard_map/ppermute | solution.py:325
  50.5 2.2 %collective-permute-done.12.refs_5_ = bf16[128,256]{1,0:T(8,128)(2,1)S(1)} collective-permute-done((bf16[128,256]{1,0:T(8,128)(2,1)S(1)}, bf16[128,256]{1,0:T(8,128)(2,1)S(1)}, u32[]{:S(2)}, u32[]{:S(2)}) %collective-permute-start.12) | collective-permute-done | bytes 65568 | tf_op jit(solution)/shard_map/ppermute | solution.py:325
  52.8 0.0 collective-permute-done.13.refs_6_
  52.8 0.9 %collective-permute-start.15 = (bf16[384,256]{1,0:T(8,128)(2,1)S(1)}, bf16[384,256]{1,0:T(8,128)(2,1)S(1)}, u32[]{:S(2)}, u32[]{:S(2)}) collective-permute-start(bf16[384,256]{1,0:T(8,128)(2,1)S(1)} %pad_maximum_fusion.5), channel_id=1, source_target_pairs={{0,2},{1,3},{2,0},{3,1},{4,6},{5,7},{6,4},{7,5},{8,10},{9,11},{10,... | collective-permute-start | bytes 589832 | tf_op jit(solution)/shard_map/ppermute | solution.py:325
  53.7 1.2 %collective-permute-start.14 = (bf16[128,256]{1,0:T(8,128)(2,1)S(1)}, bf16[128,256]{1,0:T(8,128)(2,1)S(1)}, u32[]{:S(2)}, u32[]{:S(2)}) collective-permute-start(bf16[128,256]{1,0:T(8,128)(2,1)S(1)} %update.2.own_ref.refs_3_), channel_id=1, source_target_pairs={{0,2},{1,3},{2,0},{3,1},{4,6},{5,7},{6,4},{7,5},{8,10},{9,11},{10,... | collective-permute-start | bytes 196616 | tf_op jit(solution)/shard_map/ppermute | solution.py:325
  54.9 2.7 %filters.6.refs_0_ = bf16[32,128,256]{2,1,0:T(8,128)(2,1)S(1)} custom-call(f32[64,128]{1,0:T(8,128)S(1)} %copy-done.5, bf16[2,64,512]{2,1,0:T(8,128)(2,1)S(1)} %copy-done.4, bf16[2,512,256]{2,1,0:T(8,128)(2,1)S(1)} %copy-done.2), custom_call_target="tpu_custom_call" | custom-call | tf_op jit(solution)/shard_map/filters/pallas_call | solution.py:246
  57.6 0.0 copy-start.22
  57.6 2.7 %filters.7.refs_1_ = bf16[32,128,256]{2,1,0:T(8,128)(2,1)S(1)} custom-call(f32[64,128]{1,0:T(8,128)S(1)} %copy-done.5, bf16[2,64,512]{2,1,0:T(8,128)(2,1)S(1)} %copy-done.4, bf16[2,512,256]{2,1,0:T(8,128)(2,1)S(1)} %copy-done.2), custom_call_target="tpu_custom_call" | custom-call | tf_op jit(solution)/shard_map/filters/pallas_call | solution.py:246
  60.3 2.0 %collective-permute-start.9 = (bf16[128,256]{1,0:T(8,128)(2,1)S(1)}, bf16[128,256]{1,0:T(8,128)(2,1)S(1)}, u32[]{:S(2)}, u32[]{:S(2)}) collective-permute-start(bf16[128,256]{1,0:T(8,128)(2,1)S(1)} %update.2.own_ref.refs_3_), channel_id=1, source_target_pairs={{0,15},{1,2},{2,1},{3,4},{4,3},{5,6},{6,5},{7,8},{8,7},{9,10},{10,... | collective-permute-start | bytes 196616 | tf_op jit(solution)/shard_map/ppermute | solution.py:366
  62.3 0.0 collective-permute-start.10
  62.3 0.0 collective-permute-done.14.refs_7_
  62.3 0.6 collective-permute-start.16
  62.9 0.0 collective-permute-done.15.refs_9_
  62.9 0.1 collective-permute-start.17
  63.0 3.8 %collective-permute-done.9 = bf16[128,256]{1,0:T(8,128)(2,1)S(1)} collective-permute-done((bf16[128,256]{1,0:T(8,128)(2,1)S(1)}, bf16[128,256]{1,0:T(8,128)(2,1)S(1)}, u32[]{:S(2)}, u32[]{:S(2)}) %collective-permute-start.9) | collective-permute-done | bytes 65568 | tf_op jit(solution)/shard_map/ppermute | solution.py:366
  66.8 0.0 collective-permute-done.10.refs_8_
  66.8 3.2 %messages.3.message_ref = bf16[128,256]{1,0:T(8,128)(2,1)S(1)} custom-call(s32[64,128]{1,0:T(8,128)S(1)} %copy-done.20, f32[64,128]{1,0:T(8,128)S(1)} %copy-done.5, s32[64,128]{1,0:T(8,128)S(1)} %copy-done.22, bf16[384,256]{1,0:T(8,128)(2,1)S(1)} %pad_maximum_fusion.4.table_ref, bf16[32,128,256]{2,1,0:T(8,128)(2,1)S(1)} %filters.6.refs_0_, ...), custom_call_target="tpu_custom_call" | custom-call | tf_op jit(solution)/shard_map/messages/pallas_call | solution.py:285
  70.0 0.0 collective-permute-done.16.refs_10_
  70.0 0.0 collective-permute-done.17.refs_11_
  70.1 1.4 %update.3 = bf16[128,256]{1,0:T(8,128)(2,1)} custom-call(bf16[128,256]{1,0:T(8,128)(2,1)S(1)} %update.2.own_ref.refs_3_, bf16[128,256]{1,0:T(8,128)(2,1)S(1)} %messages.3.message_ref, bf16[2,256,256]{2,1,0:T(8,128)(2,1)S(1)} %copy-done.12, bf16[2,256,256]{2,1,0:T(8,128)(2,1)S(1)} %copy-done.13, bf16[2,256,256]{2,1,0:T(8,128)(2,1)S(1)} %copy-done.14, ...), custom_call_target="tpu_custom_call" | custom-call | tf_op jit(solution)/shard_map/update/pallas_call | solution.py:313
  (38 shorter events, 0.1 us)
Async XLA Ops:
  0.0 22.7 %copy-start.5 = (f32[64,128]{1,0:T(8,128)S(1)}, f32[64,128]{1,0:T(8,128)}, u32[]{:S(2)}) copy-start(f32[64,128]{1,0:T(8,128)} %distance_ref.11) | copy-start | bytes 98308
  0.0 22.7 %copy-start.2 = (bf16[2,512,256]{2,1,0:T(8,128)(2,1)S(1)}, bf16[2,512,256]{2,1,0:T(8,128)(2,1)}, u32[]{:S(2)}) copy-start(bf16[2,512,256]{2,1,0:T(8,128)(2,1)} %filter_ref.7) | copy-start | bytes 1572868
  1.9 0.6 copy-start.15
  2.5 0.6 copy-start.17
  3.2 8.1 %collective-permute-start.2 = (bf16[144,256]{1,0:T(8,128)(2,1)}, bf16[144,256]{1,0:T(8,128)(2,1)S(1)}, u32[]{:S(2)}, u32[]{:S(2)}) collective-permute-start(bf16[144,256]{1,0:T(8,128)(2,1)} %get-tuple-element.9.refs_0_.refs_3_), channel_id=1, source_target_pairs={{0,12},{1,13},{2,14},{3,15},{4,8},{5,9},{6,10},{7,11},{8,4},{9,5},... | collective-permute-start | bytes 221192 | tf_op jit(solution)/shard_map/ppermute | solution.py:325
  8.2 6.4 %collective-permute-start.3 = (bf16[144,256]{1,0:T(8,128)(2,1)}, bf16[144,256]{1,0:T(8,128)(2,1)S(1)}, u32[]{:S(2)}, u32[]{:S(2)}) collective-permute-start(bf16[144,256]{1,0:T(8,128)(2,1)} %get-tuple-element.9.refs_0_.refs_3_), channel_id=1, source_target_pairs={{0,8},{1,9},{2,10},{3,11},{4,12},{5,13},{6,14},{7,15},{8,0},{9,1},... | collective-permute-start | bytes 221192 | tf_op jit(solution)/shard_map/ppermute | solution.py:325
  8.2 6.4 %collective-permute-start.4 = (bf16[144,256]{1,0:T(8,128)(2,1)}, bf16[144,256]{1,0:T(8,128)(2,1)S(1)}, u32[]{:S(2)}, u32[]{:S(2)}) collective-permute-start(bf16[144,256]{1,0:T(8,128)(2,1)} %get-tuple-element.9.refs_0_.refs_3_), channel_id=1, source_target_pairs={{0,4},{1,5},{2,6},{3,7},{4,0},{5,1},{6,2},{7,3},{8,12},{9,13},{10,... | collective-permute-start | bytes 221192 | tf_op jit(solution)/shard_map/ppermute | solution.py:325
  11.2 3.5 %copy-start.6 = (bf16[144,256]{1,0:T(8,128)(2,1)}, bf16[144,256]{1,0:T(8,128)(2,1)S(1)}, u32[]{:S(2)}) copy-start(bf16[144,256]{1,0:T(8,128)(2,1)S(1)} %collective-permute-done.2.refs_1_.refs_4_) | copy-start | bytes 221188
  14.7 0.8 %copy-start.8 = (bf16[144,256]{1,0:T(8,128)(2,1)}, bf16[144,256]{1,0:T(8,128)(2,1)S(1)}, u32[]{:S(2)}) copy-start(bf16[144,256]{1,0:T(8,128)(2,1)S(1)} %collective-permute-done.3.refs_2_.refs_5_) | copy-start | bytes 221188
  14.7 2.3 %copy-start.10 = (bf16[144,256]{1,0:T(8,128)(2,1)}, bf16[144,256]{1,0:T(8,128)(2,1)S(1)}, u32[]{:S(2)}) copy-start(bf16[144,256]{1,0:T(8,128)(2,1)S(1)} %collective-permute-done.4.refs_3_.refs_6_) | copy-start | bytes 221188
  15.4 12.5 %collective-permute-start.6 = (bf16[432,256]{1,0:T(8,128)(2,1)}, bf16[432,256]{1,0:T(8,128)(2,1)}, u32[]{:S(2)}, u32[]{:S(2)}) collective-permute-start(bf16[432,256]{1,0:T(8,128)(2,1)} %pad_maximum_fusion.2), channel_id=1, source_target_pairs={{0,2},{1,3},{2,0},{3,1},{4,6},{5,7},{6,4},{7,5},{8,10},{9,11},{10,... | collective-permute-start | bytes 663560 | tf_op jit(solution)/shard_map/ppermute | solution.py:325
  16.9 9.9 %collective-permute-start.5 = (bf16[144,256]{1,0:T(8,128)(2,1)}, bf16[144,256]{1,0:T(8,128)(2,1)}, u32[]{:S(2)}, u32[]{:S(2)}) collective-permute-start(bf16[144,256]{1,0:T(8,128)(2,1)} %get-tuple-element.9.refs_0_.refs_3_), channel_id=1, source_target_pairs={{0,2},{1,3},{2,0},{3,1},{4,6},{5,7},{6,4},{7,5},{8,10},{9,11},{10,... | collective-permute-start | bytes 221192 | tf_op jit(solution)/shard_map/ppermute | solution.py:325
  17.4 11.0 %collective-permute-start = (bf16[128,256]{1,0:T(8,128)(2,1)}, bf16[128,256]{1,0:T(8,128)(2,1)}, u32[]{:S(2)}, u32[]{:S(2)}) collective-permute-start(bf16[128,256]{1,0:T(8,128)(2,1)} %own_ref.3), channel_id=1, source_target_pairs={{0,15},{1,2},{2,1},{3,4},{4,3},{5,6},{6,5},{7,8},{8,7},{9,10},{10,... | collective-permute-start | bytes 196616 | tf_op jit(solution)/shard_map/ppermute | solution.py:366
  18.4 10.0 %collective-permute-start.1 = (bf16[144,256]{1,0:T(8,128)(2,1)}, bf16[144,256]{1,0:T(8,128)(2,1)}, u32[]{:S(2)}, u32[]{:S(2)}) collective-permute-start(bf16[144,256]{1,0:T(8,128)(2,1)} %get-tuple-element.9.refs_0_.refs_3_), channel_id=1, source_target_pairs={{0,1},{1,0},{2,3},{3,2},{4,5},{5,4},{6,7},{7,6},{8,9},{9,8},{10,11... | collective-permute-start | bytes 221192 | tf_op jit(solution)/shard_map/ppermute | solution.py:325
  19.1 3.7 %copy-start.3 = (bf16[2,64,512]{2,1,0:T(8,128)(2,1)S(1)}, bf16[2,64,512]{2,1,0:T(8,128)(2,1)}, u32[]{:S(2)}) copy-start(bf16[2,64,512]{2,1,0:T(8,128)(2,1)} %rbf_ref.7) | copy-start | bytes 393220
  22.7 7.4 %copy-start.20 = (s32[64,128]{1,0:T(8,128)S(1)}, s32[64,128]{1,0:T(8,128)}, u32[]{:S(2)}) copy-start(s32[64,128]{1,0:T(8,128)} %index_ref.3) | copy-start | bytes 98308
  25.5 1.4 %copy-start = (bf16[32,128,256]{2,1,0:T(8,128)(2,1)}, bf16[32,128,256]{2,1,0:T(8,128)(2,1)S(1)}, u32[]{:S(2)}) copy-start(bf16[32,128,256]{2,1,0:T(8,128)(2,1)S(1)} %filters.5.refs_1_) | copy-start | bytes 6291460
  27.8 10.4 %collective-permute-start.7 = (bf16[576,256]{1,0:T(8,128)(2,1)S(1)}, bf16[576,256]{1,0:T(8,128)(2,1)S(1)}, u32[]{:S(2)}, u32[]{:S(2)}) collective-permute-start(bf16[576,256]{1,0:T(8,128)(2,1)S(1)} %pad_maximum_fusion), channel_id=1, source_target_pairs={{0,1},{1,0},{2,3},{3,2},{4,5},{5,4},{6,7},{7,6},{8,9},{9,8},{10,11... | collective-permute-start | bytes 884744 | tf_op jit(solution)/shard_map/ppermute | solution.py:325
  27.9 13.1 %collective-permute-start.8 = (bf16[432,256]{1,0:T(8,128)(2,1)}, bf16[432,256]{1,0:T(8,128)(2,1)S(1)}, u32[]{:S(2)}, u32[]{:S(2)}) collective-permute-start(bf16[432,256]{1,0:T(8,128)(2,1)} %collective-permute-done.6.refs_0_.refs_9_), channel_id=1, source_target_pairs={{0,1},{1,0},{2,3},{3,2},{4,5},{5,4},{6,7},{7,6},{8,9},{9,8},{10,11... | collective-permute-start | bytes 663560 | tf_op jit(solution)/shard_map/ppermute | solution.py:325
  30.2 1.6 %copy-start.1 = (bf16[32,128,256]{2,1,0:T(8,128)(2,1)S(1)}, bf16[32,128,256]{2,1,0:T(8,128)(2,1)}, u32[]{:S(2)}) copy-start(bf16[32,128,256]{2,1,0:T(8,128)(2,1)} %copy-done) | copy-start | bytes 6291460
  31.8 0.8 %copy-start.21 = (s32[64,128]{1,0:T(8,128)S(1)}, s32[64,128]{1,0:T(8,128)}, u32[]{:S(2)}) copy-start(s32[64,128]{1,0:T(8,128)} %mask_ref.3) | copy-start | bytes 98308
  32.5 3.2 %copy-start.7 = (bf16[144,256]{1,0:T(8,128)(2,1)S(1)}, bf16[144,256]{1,0:T(8,128)(2,1)}, u32[]{:S(2)}) copy-start(bf16[144,256]{1,0:T(8,128)(2,1)} %copy-done.6) | copy-start | bytes 221188
  32.5 3.3 %copy-start.9 = (bf16[144,256]{1,0:T(8,128)(2,1)S(1)}, bf16[144,256]{1,0:T(8,128)(2,1)}, u32[]{:S(2)}) copy-start(bf16[144,256]{1,0:T(8,128)(2,1)} %copy-done.8) | copy-start | bytes 221188
  32.5 3.3 %copy-start.11 = (bf16[144,256]{1,0:T(8,128)(2,1)S(1)}, bf16[144,256]{1,0:T(8,128)(2,1)}, u32[]{:S(2)}) copy-start(bf16[144,256]{1,0:T(8,128)(2,1)} %copy-done.10) | copy-start | bytes 221188
  32.5 3.3 %copy-start.16 = (f32[128,128]{1,0:T(8,128)S(1)}, f32[128,128]{1,0:T(8,128)}, u32[]{:S(2)}) copy-start(f32[128,128]{1,0:T(8,128)} %copy-done.15) | copy-start | bytes 196612
  32.6 3.3 %copy-start.18 = (f32[128,128]{1,0:T(8,128)S(1)}, f32[128,128]{1,0:T(8,128)}, u32[]{:S(2)}) copy-start(f32[128,128]{1,0:T(8,128)} %copy-done.17) | copy-start | bytes 196612
  35.8 6.0 %copy-start.12 = (bf16[2,256,256]{2,1,0:T(8,128)(2,1)S(1)}, bf16[2,256,256]{2,1,0:T(8,128)(2,1)}, u32[]{:S(2)}) copy-start(bf16[2,256,256]{2,1,0:T(8,128)(2,1)} %mixing_ref.3) | copy-start | bytes 786436
  35.8 6.0 %copy-start.13 = (bf16[2,256,256]{2,1,0:T(8,128)(2,1)S(1)}, bf16[2,256,256]{2,1,0:T(8,128)(2,1)}, u32[]{:S(2)}) copy-start(bf16[2,256,256]{2,1,0:T(8,128)(2,1)} %short_ref.3) | copy-start | bytes 786436
  35.9 6.0 %copy-start.14 = (bf16[2,256,256]{2,1,0:T(8,128)(2,1)S(1)}, bf16[2,256,256]{2,1,0:T(8,128)(2,1)}, u32[]{:S(2)}) copy-start(bf16[2,256,256]{2,1,0:T(8,128)(2,1)} %long_ref.3) | copy-start | bytes 786436
  35.9 6.0 %copy-start.19 = (bf16[128,256]{1,0:T(8,128)(2,1)S(1)}, bf16[128,256]{1,0:T(8,128)(2,1)}, u32[]{:S(2)}) copy-start(bf16[128,256]{1,0:T(8,128)(2,1)} %own_ref.3) | copy-start | bytes 196612
  41.0 13.8 %copy-start.4 = (bf16[2,64,512]{2,1,0:T(8,128)(2,1)S(1)}, bf16[2,64,512]{2,1,0:T(8,128)(2,1)}, u32[]{:S(2)}) copy-start(bf16[2,64,512]{2,1,0:T(8,128)(2,1)} %rbf_ref.7) | copy-start | bytes 393220
  43.7 6.8 %collective-permute-start.11 = (bf16[128,256]{1,0:T(8,128)(2,1)S(1)}, bf16[128,256]{1,0:T(8,128)(2,1)S(1)}, u32[]{:S(2)}, u32[]{:S(2)}) collective-permute-start(bf16[128,256]{1,0:T(8,128)(2,1)S(1)} %update.2.own_ref.refs_3_), channel_id=1, source_target_pairs={{0,12},{1,13},{2,14},{3,15},{4,8},{5,9},{6,10},{7,11},{8,4},{9,5},... | collective-permute-start | bytes 196616 | tf_op jit(solution)/shard_map/ppermute | solution.py:325
  46.5 6.3 %collective-permute-start.12 = (bf16[128,256]{1,0:T(8,128)(2,1)S(1)}, bf16[128,256]{1,0:T(8,128)(2,1)S(1)}, u32[]{:S(2)}, u32[]{:S(2)}) collective-permute-start(bf16[128,256]{1,0:T(8,128)(2,1)S(1)} %update.2.own_ref.refs_3_), channel_id=1, source_target_pairs={{0,8},{1,9},{2,10},{3,11},{4,12},{5,13},{6,14},{7,15},{8,0},{9,1},... | collective-permute-start | bytes 196616 | tf_op jit(solution)/shard_map/ppermute | solution.py:325
  46.5 6.3 %collective-permute-start.13 = (bf16[128,256]{1,0:T(8,128)(2,1)S(1)}, bf16[128,256]{1,0:T(8,128)(2,1)S(1)}, u32[]{:S(2)}, u32[]{:S(2)}) collective-permute-start(bf16[128,256]{1,0:T(8,128)(2,1)S(1)} %update.2.own_ref.refs_3_), channel_id=1, source_target_pairs={{0,4},{1,5},{2,6},{3,7},{4,0},{5,1},{6,2},{7,3},{8,12},{9,13},{10,... | collective-permute-start | bytes 196616 | tf_op jit(solution)/shard_map/ppermute | solution.py:325
  52.8 10.1 %collective-permute-start.15 = (bf16[384,256]{1,0:T(8,128)(2,1)S(1)}, bf16[384,256]{1,0:T(8,128)(2,1)S(1)}, u32[]{:S(2)}, u32[]{:S(2)}) collective-permute-start(bf16[384,256]{1,0:T(8,128)(2,1)S(1)} %pad_maximum_fusion.5), channel_id=1, source_target_pairs={{0,2},{1,3},{2,0},{3,1},{4,6},{5,7},{6,4},{7,5},{8,10},{9,11},{10,... | collective-permute-start | bytes 589832 | tf_op jit(solution)/shard_map/ppermute | solution.py:325
  53.7 8.6 %collective-permute-start.14 = (bf16[128,256]{1,0:T(8,128)(2,1)S(1)}, bf16[128,256]{1,0:T(8,128)(2,1)S(1)}, u32[]{:S(2)}, u32[]{:S(2)}) collective-permute-start(bf16[128,256]{1,0:T(8,128)(2,1)S(1)} %update.2.own_ref.refs_3_), channel_id=1, source_target_pairs={{0,2},{1,3},{2,0},{3,1},{4,6},{5,7},{6,4},{7,5},{8,10},{9,11},{10,... | collective-permute-start | bytes 196616 | tf_op jit(solution)/shard_map/ppermute | solution.py:325
  57.6 9.2 %copy-start.22 = (s32[64,128]{1,0:T(8,128)S(1)}, s32[64,128]{1,0:T(8,128)}, u32[]{:S(2)}) copy-start(s32[64,128]{1,0:T(8,128)} %mask_ref.3) | copy-start | bytes 98308
  60.3 6.5 %collective-permute-start.9 = (bf16[128,256]{1,0:T(8,128)(2,1)S(1)}, bf16[128,256]{1,0:T(8,128)(2,1)S(1)}, u32[]{:S(2)}, u32[]{:S(2)}) collective-permute-start(bf16[128,256]{1,0:T(8,128)(2,1)S(1)} %update.2.own_ref.refs_3_), channel_id=1, source_target_pairs={{0,15},{1,2},{2,1},{3,4},{4,3},{5,6},{6,5},{7,8},{8,7},{9,10},{10,... | collective-permute-start | bytes 196616 | tf_op jit(solution)/shard_map/ppermute | solution.py:366
  62.3 4.5 %collective-permute-start.10 = (bf16[128,256]{1,0:T(8,128)(2,1)S(1)}, bf16[128,256]{1,0:T(8,128)(2,1)S(1)}, u32[]{:S(2)}, u32[]{:S(2)}) collective-permute-start(bf16[128,256]{1,0:T(8,128)(2,1)S(1)} %update.2.own_ref.refs_3_), channel_id=1, source_target_pairs={{0,1},{1,0},{2,3},{3,2},{4,5},{5,4},{6,7},{7,6},{8,9},{9,8},{10,11... | collective-permute-start | bytes 196616 | tf_op jit(solution)/shard_map/ppermute | solution.py:325
  62.3 7.7 %collective-permute-start.16 = (bf16[512,256]{1,0:T(8,128)(2,1)S(1)}, bf16[512,256]{1,0:T(8,128)(2,1)S(1)}, u32[]{:S(2)}, u32[]{:S(2)}) collective-permute-start(bf16[512,256]{1,0:T(8,128)(2,1)S(1)} %pad_maximum_fusion.1), channel_id=1, source_target_pairs={{0,1},{1,0},{2,3},{3,2},{4,5},{5,4},{6,7},{7,6},{8,9},{9,8},{10,11... | collective-permute-start | bytes 786440 | tf_op jit(solution)/shard_map/ppermute | solution.py:325
  62.9 7.1 %collective-permute-start.17 = (bf16[384,256]{1,0:T(8,128)(2,1)S(1)}, bf16[384,256]{1,0:T(8,128)(2,1)S(1)}, u32[]{:S(2)}, u32[]{:S(2)}) collective-permute-start(bf16[384,256]{1,0:T(8,128)(2,1)S(1)} %collective-permute-done.15.refs_9_), channel_id=1, source_target_pairs={{0,1},{1,0},{2,3},{3,2},{4,5},{5,4},{6,7},{7,6},{8,9},{9,8},{10,11... | collective-permute-start | bytes 589832 | tf_op jit(solution)/shard_map/ppermute | solution.py:325
where the time goes:
time: 71.9 us; the launch traced here: 71.5 us
  Pallas kernels  29.2 us (41%)
  starting transfers between devices  19.1 us (27%)
  waiting for transfers between devices  14.2 us (20%)
  local copies, waits for them, and re-layouts  5.03 us (7%)
  other arithmetic  3.55 us (5%)
    ppermute x16, starting transfers between devices, swap(): return lax.ppermute(x, 'atom', [(i, i ^ mask) for i in range(count)])  16.1 us
    pallas_call x4, Pallas kernels, filters_of(): pl.pallas_call(functools.partial(filter_kernel, layer, begin, fetch), out...  11.7 us
    ppermute x16, waiting for transfers between devices, swap(): return lax.ppermute(x, 'atom', [(i, i ^ mask) for i in range(count)])  10.4 us
    pallas_call x2, Pallas kernels, messages(): pl.pallas_call(message_kernel, out_shape=jax.ShapeDtypeStruct((rows, widt...  6.44 us
    pallas_call x3, Pallas kernels, coupling(): pl.pallas_call(functools.partial(coupling_kernel, tuple(places), rows), o...  5.92 us
    unnamed x46, local copies, waits for them, and re-layouts  5.03 us
    ppermute x2, waiting for transfers between devices, neighbour_table(): lax.ppermute(own, 'atom', [(i, (i + (count - 1 if i % 2 == 0 else 1)) % c...  3.77 us
    pallas_call x2, Pallas kernels, update(): pl.pallas_call(functools.partial(update_kernel, tuple(places), layer, bef...  3.25 us
  transfers between devices with their start and end apart: 18, of which 5 were waited for; matrix products, arithmetic and copies ran while one was open for 4% of the time, Pallas kernels for 33%

commit v1 on v0

--- a/solution.py
+++ b/solution.py
@@ -32,11 +32,11 @@
     part = turns - jnp.round(turns)
     angle = part * (2.0 * math.pi)
     square = angle * angle
-    cosine = jnp.full_like(square, 1.0 / math.factorial(20))
-    for n in range(18, -2, -2):
+    cosine = jnp.full_like(square, 1.0 / math.factorial(18))
+    for n in range(16, -2, -2):
         cosine = cosine * -square + 1.0 / math.factorial(n)
-    sine = jnp.full_like(square, 1.0 / math.factorial(21))
-    for n in range(19, -1, -2):
+    sine = jnp.full_like(square, 1.0 / math.factorial(19))
+    for n in range(17, -1, -2):
         sine = sine * -square + 1.0 / math.factorial(n)
     return cosine, sine * angle
 
@@ -68,7 +68,13 @@
     return pl.BlockSpec(x.shape, lambda i: (0,) * len(x.shape))
 
 
-def prepare_kernel(wave_ref, position_ref, own_ref, packed_ref, left_ref, zc_ref, zs_ref):
+def prepare_kernel(
+    wave_ref, position_ref, own_ref, distance_ref, rbf_ref, filter_ref,
+    packed_ref, left_ref, zc_ref, zs_ref, distance_out, rbf_out, filter_out,
+):
+    distance_out[...] = distance_ref[...]
+    rbf_out[...] = rbf_ref[...]
+    filter_out[...] = filter_ref[...]
     rows = position_ref.shape[1]
     position = position_ref[...]
     top = position.astype(BF)
@@ -115,21 +121,24 @@
     zs_ref[...] = jnp.broadcast_to(zs, (rows, rows)).T
 
 
-def prepare(wave_index, position, own):
+def prepare(wave_index, position, own, distances, w_rbf, w_filter):
     rows = position.shape[1]
     shapes = (
         jax.ShapeDtypeStruct((rows + extra_rows, own.shape[1]), BF),
         jax.ShapeDtypeStruct((2 * reach + 1, rows, 2 * plane), BF),
         jax.ShapeDtypeStruct((rows, rows), F32),
         jax.ShapeDtypeStruct((rows, rows), F32),
+        jax.ShapeDtypeStruct(distances.shape, F32),
+        jax.ShapeDtypeStruct((1,) + w_rbf.shape[1:], BF),
+        jax.ShapeDtypeStruct((1,) + w_filter.shape[1:], BF),
     )
-    inputs = (wave_index, position, own)
+    inputs = (wave_index, position, own, distances, w_rbf, w_filter)
     return pl.pallas_call(
         prepare_kernel,
         out_shape=shapes,
         grid=(1,),
-        in_specs=[whole(x) for x in inputs],
-        out_specs=tuple(whole(x) for x in shapes),
+        in_specs=[whole(x) for x in inputs[:4]] + [whole(x) for x in shapes[-2:]],
+        out_specs=(VM,) * len(shapes),
         compiler_params=limit,
         name="prepare",
     )(*[in_hbm(x) for x in inputs])
@@ -163,12 +172,12 @@
                 c1 = oc * zc + os * zs
                 s1 = os * zc - oc * zs
                 twice = c1 + c1
-                total = part_ref[0, own, at] + c1 * part_ref[1, own, at] + s1 * part_ref[reach + 1, own, at]
-                c0, s0 = jnp.ones_like(c1), jnp.zeros_like(s1)
-                for m in range(2, orders):
-                    c0, c1 = c1, twice * c1 - c0
-                    s0, s1 = s1, twice * s1 - s0
-                    total = total + c1 * part_ref[m, own, at] + s1 * part_ref[reach + m, own, at]
+                even, odd = part_ref[reach, own, at], part_ref[2 * reach, own, at]
+                even_last, odd_last = 0.0, 0.0
+                for m in range(reach - 1, 0, -1):
+                    even, even_last = part_ref[m, own, at] + twice * even - even_last, even
+                    odd, odd_last = part_ref[reach + m, own, at] + twice * odd - odd_last, odd
+                total = part_ref[0, own, at] + c1 * even - even_last + s1 * odd
                 out_ref[own, pair * rows + side * rows : pair * rows + (side + 1) * rows] = total.astype(BF)
 
 
@@ -194,64 +203,36 @@
     return coupling(prepared, [arrays[n] for n in used], spots, rows)
 
 
-def filter_kernel(layer, begin, fetch, distance_ref, rbf_ref, filter_ref, out_ref, *scratch):
+def filter_kernel(layer, begin, distance_ref, rbf_ref, filter_ref, out_ref):
     group, rows, _ = out_ref.shape
-    at = slice(begin, begin + group)
-    copies = []
-    if fetch:
-        sources = (distance_ref.at[at], rbf_ref.at[layer], filter_ref.at[layer])
-        copies = [
-            pltpu.make_async_copy(source, target, scratch[3].at[n])
-            for n, (source, target) in enumerate(zip(sources, scratch))
-        ]
-        for copy in copies:
-            copy.start()
-        copies[0].wait()
-        distance = scratch[0][...]
-    else:
-        distance = distance_ref[at, :]
     count = rbf_ref.shape[1]
     step = lax.broadcasted_iota(jnp.int32, (count, rows), 0).astype(F32)
     centers = 0.5 + 4.5 * step / (count - 1)
     pieces = []
-    for s in range(group):
-        offset = distance[s : s + 1, :] - centers
+    for s in range(begin, begin + group):
+        offset = distance_ref[s : s + 1, :] - centers
         pieces.append(jnp.exp(-4.0 * offset * offset).astype(BF))
     basis = jnp.concatenate(pieces, axis=1)
-    if fetch:
-        copies[1].wait()
-    first = scratch[1][...] if fetch else rbf_ref[layer]
-    half = dot_dims(basis, first * jnp.asarray(0.5, BF), 0, 0)
+    half = dot_dims(basis, rbf_ref[layer] * jnp.asarray(0.5, BF), 0, 0)
     inner = (half + half * jnp.tanh(half)).astype(BF)
-    if fetch:
-        copies[2].wait()
-    second = scratch[2][...] if fetch else filter_ref[layer]
-    out_ref[...] = dot(inner, second).astype(BF).reshape(out_ref.shape)
-
-
-def filters_of(distances, w_rbf, w_filter, layer, begin, count, fetch):
+    out_ref[...] = dot(inner, filter_ref[layer]).astype(BF).reshape(out_ref.shape)
+
+
+def filters_of(distances, w_rbf, w_filter, layer, begin, count):
     rows = distances.shape[1]
     width = w_filter.shape[2]
-    inputs = (distances, w_rbf, w_filter)
-    if fetch:
-        inputs = tuple(in_hbm(x) for x in inputs)
-        scratch = [
-            pltpu.VMEM((count, rows), F32),
-            pltpu.VMEM(w_rbf.shape[1:], BF),
-            pltpu.VMEM(w_filter.shape[1:], BF),
-            pltpu.SemaphoreType.DMA((3,)),
-        ]
-    else:
-        scratch = []
-    return pl.pallas_call(
-        functools.partial(filter_kernel, layer, begin, fetch),
+    return pl.pallas_call(
+        functools.partial(filter_kernel, layer, begin),
         out_shape=jax.ShapeDtypeStruct((count, rows, width), BF),
-        in_specs=[RAW if fetch else VM] * 3,
+        in_specs=[VM] * 3,
         out_specs=VM,
-        scratch_shapes=scratch,
         compiler_params=limit,
         name="filters",
-    )(*inputs)
+    )(distances, w_rbf, w_filter)
+
+
+def code_of(index):
+    return jnp.where(index < 256, index, 255 - index).astype(F32).astype(BF)
 
 
 def message_kernel(index_ref, distance_ref, mask_ref, table_ref, *refs):
@@ -259,16 +240,16 @@
     slots, rows = index_ref.shape
     reachable, width = table_ref.shape
     group = message_group
-    lane = lax.broadcasted_iota(jnp.int32, (rows, reachable), 1)
+    lane = code_of(lax.broadcasted_iota(jnp.int32, (rows, reachable), 1))
     total = jnp.zeros((rows, width), F32)
     per = slots // len(filter_refs)
     for begin in range(0, slots, group):
         at = slice(begin, begin + group)
-        index = index_ref[at, :].astype(F32).T.astype(jnp.int32)
+        code = code_of(index_ref[at, :]).astype(F32).T.astype(BF)
         cosine, _ = turn_trig(distance_ref[at, :] * 0.1)
-        weight = (0.5 * (cosine + 1.0) * mask_ref[at, :].astype(F32)).T
+        weight = (0.5 * (cosine + 1.0) * mask_ref[at, :].astype(F32)).T.astype(BF)
         picks = [
-            jnp.where(lane == index[:, s : s + 1], weight[:, s : s + 1], 0.0).astype(BF)
+            jnp.where(lane == code[:, s : s + 1], weight[:, s : s + 1], jnp.zeros((), BF))
             for s in range(group)
         ]
         gathered = dot(jnp.concatenate(picks, axis=0), table_ref[...]).reshape(group, rows, width)
@@ -292,37 +273,70 @@
     )(*inputs)
 
 
-def update_kernel(places, layer, before, after, own_ref, message_ref, mixing_ref, short_ref, long_ref, *refs):
-    rows, width = own_ref.shape
-    counts = sorted({p[0] for p in places})
-    pairs = len({p[2] for p in places})
-    matrices, states, out_ref = refs[:pairs], refs[pairs : pairs + len(counts)], refs[-1]
-    total = jnp.zeros((rows, width), F32)
+def gathered_field(places, rows, matrices, states):
+    total = None
     for which, start, matrix, column in places:
-        total = total + dot(
+        part = dot(
             matrices[matrix][:, column * rows : (column + 1) * rows], states[which][start : start + rows, :]
         )
+        total = part if total is None else total + part
+    return total
+
+
+def partial_kernel(places, pairs, layer, message_ref, short_ref, *refs):
+    matrices, states, total_ref, close_ref = refs[:pairs], refs[pairs:-2], refs[-2], refs[-1]
+    total_ref[...] = gathered_field(places, message_ref.shape[0], matrices, states)
+    close_ref[...] = dot(message_ref[...], short_ref[layer])
+
+
+def partial_update(message, w_short, layer, matrices, arrays, places):
+    shape = jax.ShapeDtypeStruct(message.shape, F32)
+    return pl.pallas_call(
+        functools.partial(partial_kernel, tuple(places), len(matrices), layer),
+        out_shape=(shape, shape),
+        in_specs=[VM] * (2 + len(matrices) + len(arrays)),
+        out_specs=(VM, VM),
+        compiler_params=limit,
+        name="partial",
+    )(message, w_short, *matrices, *arrays)
+
+
+def update_kernel(places, pairs, begun, layer, before, after, own_ref, mixing_ref, long_ref, *refs):
+    rows, _ = own_ref.shape
+    head, matrices, states, out_ref = refs[:2], refs[2 : 2 + pairs], refs[2 + pairs : -1], refs[-1]
+    total = gathered_field(places, rows, matrices, states)
+    if begun:
+        total = total + head[0][...]
+        close = head[1][...]
+    else:
+        close = dot(head[0][...], head[1][layer])
     potential = dot((total * before).astype(BF), mixing_ref[layer]).astype(BF)
     field = (potential.astype(F32) * after).astype(BF)
-    half = 0.5 * (dot(message_ref[...], short_ref[layer]) + dot(field, long_ref[layer]))
+    half = 0.5 * (close + dot(field, long_ref[layer]))
     out_ref[...] = (own_ref[...].astype(F32) + (half + half * jnp.tanh(half))).astype(BF)
 
 
-def update(own, message, weights, layer, matrices, arrays, places, before, after):
-    rows, width = own.shape
-    return pl.pallas_call(
-        functools.partial(update_kernel, tuple(places), layer, before, after),
-        out_shape=jax.ShapeDtypeStruct((rows, width), BF),
+def update(own, head, begun, mixing, long, layer, matrices, arrays, places, before, after):
+    return pl.pallas_call(
+        functools.partial(update_kernel, tuple(places), len(matrices), begun, layer, before, after),
+        out_shape=jax.ShapeDtypeStruct(own.shape, BF),
         in_specs=[VM] * (5 + len(matrices) + len(arrays)),
         out_specs=VM,
         compiler_params=limit,
         name="update",
-    )(own, message, *weights, *matrices, *arrays)
-
-
-def swap(x, mask):
+    )(own, mixing, long, *head, *matrices, *arrays)
+
+
+def picked(spots, matrices, arrays):
+    rows = sorted({spot[2] for spot in spots})
+    used = sorted({spot[0] for spot in spots})
+    spots = [(used.index(a), s, rows.index(m), c) for a, s, m, c in spots]
+    return [matrices[m] for m in rows], [arrays[a] for a in used], spots
+
+
+def swap(x, even, odd):
     count = lax.axis_size("atom")
-    return lax.ppermute(x, "atom", [(i, i ^ mask) for i in range(count)])
+    return lax.ppermute(x, "atom", [(i, i ^ (odd if i % 2 else even)) for i in range(count)])
 
 
 def schedule(count):
@@ -330,15 +344,16 @@
     stages, have = [], [0]
     if len(bits) >= 4:
         far, near, side, last = bits[0], bits[1], bits[2], bits[-1]
-        first = [far + near, far, near, side]
-        stages.append([(mask, [0]) for mask in first + [last]])
-        stages.append([(side, first[:3]), (last, first)])
-        stages.append([(last, [side + mask for mask in first[:3]])])
-        have = [0] + first + [side + mask for mask in first[:3]]
-        have = have + [q ^ last for q in have]
+        first = [far + near, far, near]
+        second = [side + q for q in first]
+        early = first + [side]
+        stages.append([(mask, mask, [0], [mask]) for mask in early + [last]])
+        stages.append([(side, side, first, second), (last, last, early, [last + q for q in early])])
+        stages.append([(last, last, second, [last + q for q in second])])
+        have = [0] + [q for stage in stages for item in stage for q in item[3]]
         bits = bits[3:-1]
     for bit in bits:
-        stages.append([(bit, list(have))])
+        stages.append([(bit, bit, list(have), [q ^ bit for q in have])])
         have = have + [q ^ bit for q in have]
     return stages
 
@@ -346,18 +361,16 @@
 def exchange(arrays, places, stage, size):
     arrays, places = list(arrays), dict(places)
     sends = []
-    for mask, wanted in stage:
+    for _, _, wanted, _ in stage:
         parts = [
             lax.slice_in_dim(arrays[places[q][0]], places[q][1], places[q][1] + size, axis=0)
             for q in wanted
         ]
         sends.append(parts[0] if len(parts) == 1 else jnp.concatenate(parts, axis=0))
-    fresh = {}
-    for (mask, wanted), sent in zip(stage, sends):
-        arrays.append(swap(sent, mask))
-        for n, q in enumerate(wanted):
-            fresh[q ^ mask] = (len(arrays) - 1, n * size)
-    places.update(fresh)
+    for (even, odd, _, labels), sent in zip(stage, sends):
+        arrays.append(swap(sent, even, odd))
+        for n, q in enumerate(labels):
+            places[q] = (len(arrays) - 1, n * size)
     return arrays, places
 
 
@@ -390,39 +403,49 @@
     even = lax.axis_index("atom") % 2 == 0
     stages = schedule(bricks)
 
-    packed, *prepared = prepare(wave_index, fractional, features)
+    packed, *prepared, near_distances, first_rbf, first_filter = prepare(
+        wave_index, fractional, features, distances, w_rbf, w_filter
+    )
     split = slots // 2
     state = features
-    matrices, order = [], []
-
-    def couple(arrays, places):
-        ready = [q for q in places if q not in order]
-        matrices.append(coupling_of(prepared, arrays, places, ready, rows))
-        order.extend(ready)
+    matrices, where = [], {}
+
+    def couple(arrays, places, keep=0):
+        ready = [q for q in places if q not in where]
+        ready = ready[: len(ready) - keep]
+        matrix = coupling_of(prepared, arrays, places, ready, rows)
+        where.update({q: (len(matrices), n) for n, q in enumerate(ready)})
+        matrices.append(matrix)
 
     for layer in range(w_rbf.shape[0]):
         block = state if layer else packed
         size = block.shape[0]
         arrays, places = exchange([block], {0: (0, 0)}, stages[0], size)
-        close = arrays[places[1][0]][:rows] if 1 in places else swap(state, 1)
+        close = arrays[places[1][0]][:rows] if 1 in places else swap(state, 1, 1)
         table = neighbour_table(state, close, even)
-        first = filters_of(distances, w_rbf, w_filter, layer, 0, split, layer == 0)
-        second = filters_of(distances, w_rbf, w_filter, layer, split, slots - split, False)
-        message = messages(neighbours, distances, edge_mask, table, (first, second))
+        if layer:
+            edge = (distances, w_rbf, w_filter, layer)
+        else:
+            edge = (near_distances, first_rbf, first_filter, 0)
+        first = filters_of(*edge, 0, split)
+        second = filters_of(*edge, split, slots - split)
+        message = messages(neighbours, edge[0], edge_mask, table, (first, second))
         for stage in stages[1:]:
             if layer == 0:
                 couple(arrays, places)
+            early = list(places)
             arrays, places = exchange(arrays, places, stage, size)
         if layer == 0:
             couple(arrays, places)
-        spots, at = [], 0
-        for number, matrix in enumerate(matrices):
-            for column in range(matrix.shape[1] // rows):
-                spots.append(places[order[at]] + (number, column))
-                at += 1
-        weights = (w_mixing, w_short, w_long)
+            early = []
+        spot = {q: places[q] + where[q] for q in places}
+        head, late = (message, w_short), [q for q in places if q not in early]
+        if early:
+            used, held, spots = picked([spot[q] for q in early], matrices, arrays)
+            head = partial_update(message, w_short, layer, used, held, spots)
+        used, held, spots = picked([spot[q] for q in late], matrices, arrays)
         state = update(
-            state, message, weights, layer, matrices, arrays, spots, before, after
+            state, head, bool(early), w_mixing, w_long, layer, used, held, spots, before, after
         )
     return state
 

time: 71.9 us -> 71.3 us (level)
  local copies, waits for them, and re-layouts: 5.03 us -> 7.24 us
  Pallas kernels: 29.2 us -> 27.5 us
  other arithmetic: 3.55 us -> 2.55 us
    unnamed x46 -> x38, local copies, waits for them, and re-layouts: 5.03 us -> 7.24 us
    concatenate x4, other arithmetic: 1.78 us -> 0.78 us  [exchange(): jnp.concatenate(parts, axis=0)]
    pallas_call x6 -> x7, Pallas kernels: 15 us -> 14.1 us  [the longest x4 10.8 us: filters_of(): pl.pallas_call(functools.partial(filter_kernel, layer, begin), out_shape=...]
    pallas_call x2, Pallas kernels: 6.44 us -> 5.58 us  [messages(): pl.pallas_call(message_kernel, out_shape=jax.ShapeDtypeStruct((rows, widt...]
  transfers between devices with their start and end apart: 18 -> 18, of which waited for: 5 -> 5; matrix products, arithmetic and copies ran while one was open for 4% -> 3% of each run, Pallas kernels for 33% -> 30%
where the time goes in v1:
time: 71.3 us; the launch traced here: 70.8 us
  Pallas kernels  27.5 us (39%)
  starting transfers between devices  19.1 us (27%)
  waiting for transfers between devices  14.2 us (20%)
  local copies, waits for them, and re-layouts  7.24 us (10%)
  other arithmetic  2.55 us (4%)
    ppermute x16, starting transfers between devices, swap(): lax.ppermute(x, 'atom', [(i, i ^ (odd if i % 2 else even)) for i in range...  16.1 us
    pallas_call x4, Pallas kernels, filters_of(): pl.pallas_call(functools.partial(filter_kernel, layer, begin), out_shape=...  10.8 us
    ppermute x16, waiting for transfers between devices, swap(): lax.ppermute(x, 'atom', [(i, i ^ (odd if i % 2 else even)) for i in range...  10.4 us
    unnamed x38, local copies, waits for them, and re-layouts  7.24 us
    pallas_call x3, Pallas kernels, coupling(): pl.pallas_call(functools.partial(coupling_kernel, tuple(places), rows), o...  5.71 us
    pallas_call x2, Pallas kernels, messages(): pl.pallas_call(message_kernel, out_shape=jax.ShapeDtypeStruct((rows, widt...  5.58 us
    ppermute x2, waiting for transfers between devices, neighbour_table(): lax.ppermute(own, 'atom', [(i, (i + (count - 1 if i % 2 == 0 else 1)) % c...  3.74 us
    ppermute x2, starting transfers between devices, neighbour_table(): lax.ppermute(own, 'atom', [(i, (i + (count - 1 if i % 2 == 0 else 1)) % c...  3 us
  transfers between devices with their start and end apart: 18, of which 5 were waited for; matrix products, arithmetic and copies ran while one was open for 3% of the time, Pallas kernels for 30%

profile of v1, /device:TPU:0, one launch (start us, length us, event | category | flops | bytes accessed | tf_op | source)
XLA Modules:
  0.0 70.8 jit_solution(929967934877259064)
XLA Ops:
  0.0 2.1 %prepare.1 = (bf16[144,256]{1,0:T(8,128)(2,1)}, bf16[13,128,256]{2,1,0:T(8,128)(2,1)S(1)}, f32[128,128]{1,0:T(8,128)S(1)}, f32[128,128]{1,0:T(8,128)S(1)}, f32[6...) custom-call(s32[3,2048]{1,0:T(4,128)} %wave_ref.1, f32[3,128]{1,0:T(4,128)} %position_ref.1, ...), custom_call_target="tpu_custom_call" | custom-call | tf_op jit(solution)/shard_map/prepare/pallas_call | solution.py:136
  2.1 0.6 copy-done.7
  2.7 0.6 copy-done.9
  3.3 0.6 copy-done.13
  4.0 5.1 %collective-permute-start.2 = (bf16[144,256]{1,0:T(8,128)(2,1)}, bf16[144,256]{1,0:T(8,128)(2,1)S(1)}, u32[]{:S(2)}, u32[]{:S(2)}) collective-permute-start(bf16[144,256]{1,0:T(8,128)(2,1)} %get-tuple-element.15.refs_0_.refs_5_), channel_id=1, source_target_pairs={{0,12},{1,13},{2,14},{3,15},{4,8},{5,9},{6,10},{7,11},{8,4},{9,5},... | collective-permute-start | bytes 221192 | tf_op jit(solution)/shard_map/ppermute | solution.py:339
  9.0 0.0 collective-permute-start.3
  9.0 0.6 collective-permute-start.4
  9.6 2.4 %collective-permute-done.2.refs_1_.refs_6_ = bf16[144,256]{1,0:T(8,128)(2,1)S(1)} collective-permute-done((bf16[144,256]{1,0:T(8,128)(2,1)}, bf16[144,256]{1,0:T(8,128)(2,1)S(1)}, u32[]{:S(2)}, u32[]{:S(2)}) %collective-permute-start.2) | collective-permute-done | bytes 73760 | tf_op jit(solution)/shard_map/ppermute | solution.py:339
  12.0 3.4 %collective-permute-done.3.refs_2_.refs_7_ = bf16[144,256]{1,0:T(8,128)(2,1)S(1)} collective-permute-done((bf16[144,256]{1,0:T(8,128)(2,1)}, bf16[144,256]{1,0:T(8,128)(2,1)S(1)}, u32[]{:S(2)}, u32[]{:S(2)}) %collective-permute-start.3) | collective-permute-done | bytes 73760 | tf_op jit(solution)/shard_map/ppermute | solution.py:339
  15.5 0.0 collective-permute-done.4.refs_3_.refs_8_
  15.5 0.7 %pad_maximum_fusion.2 = bf16[432,256]{1,0:T(8,128)(2,1)} fusion(bf16[144,256]{1,0:T(8,128)(2,1)S(1)} %collective-permute-done.4.refs_3_.refs_8_, bf16[144,256]{1,0:T(8,128)(2,1)S(1)} %collective-permute-done.3.refs_2_.refs_7_, bf16[144,256]{1,0:T(8,128)(2,1)S(1)} %collective-permute-done.2.refs_1_.refs_6_), kind=kLoop, calls=%fused_computation.2 | loop fusion | flops 663552 | bytes 442368 | tf_op jit(solution)/shard_map/concatenate | solution.py:369
  16.2 1.5 %collective-permute-start.6 = (bf16[432,256]{1,0:T(8,128)(2,1)}, bf16[432,256]{1,0:T(8,128)(2,1)}, u32[]{:S(2)}, u32[]{:S(2)}) collective-permute-start(bf16[432,256]{1,0:T(8,128)(2,1)} %pad_maximum_fusion.2), channel_id=1, source_target_pairs={{0,2},{1,3},{2,0},{3,1},{4,6},{5,7},{6,4},{7,5},{8,10},{9,11},{10,... | collective-permute-start | bytes 663560 | tf_op jit(solution)/shard_map/ppermute | solution.py:339
  17.7 0.5 collective-permute-start.5
  18.2 1.0 %collective-permute-start = (bf16[128,256]{1,0:T(8,128)(2,1)}, bf16[128,256]{1,0:T(8,128)(2,1)}, u32[]{:S(2)}, u32[]{:S(2)}) collective-permute-start(bf16[128,256]{1,0:T(8,128)(2,1)} %own_ref.3), channel_id=1, source_target_pairs={{0,15},{1,2},{2,1},{3,4},{4,3},{5,6},{6,5},{7,8},{8,7},{9,10},{10,... | collective-permute-start | bytes 196616 | tf_op jit(solution)/shard_map/ppermute | solution.py:379
  19.2 0.7 collective-permute-start.1
  19.9 0.8 %copy-done.14 = bf16[1,64,512]{2,1,0:T(8,128)(2,1)S(1)} copy-done((bf16[1,64,512]{2,1,0:T(8,128)(2,1)S(1)}, bf16[1,64,512]{2,1,0:T(8,128)(2,1)}, u32[]{:S(2)}) %copy-start.14) | copy-done | bytes 65560
  20.7 2.7 %filters.4.refs_0_ = bf16[32,128,256]{2,1,0:T(8,128)(2,1)S(1)} custom-call(f32[64,128]{1,0:T(8,128)S(1)} %get-tuple-element.14.distance_ref, bf16[1,64,512]{2,1,0:T(8,128)(2,1)S(1)} %copy-done.14, bf16[1,512,256]{2,1,0:T(8,128)(2,1)S(1)} %get-tuple-element.17.filter_ref), custom_call_target="tpu_custom_call" | custom-call | tf_op jit(solution)/shard_map/filters/pallas_call | solution.py:224
  23.4 2.7 %filters.5.refs_1_ = bf16[32,128,256]{2,1,0:T(8,128)(2,1)S(1)} custom-call(f32[64,128]{1,0:T(8,128)S(1)} %get-tuple-element.14.distance_ref, bf16[1,64,512]{2,1,0:T(8,128)(2,1)S(1)} %copy-done.15, bf16[1,512,256]{2,1,0:T(8,128)(2,1)S(1)} %get-tuple-element.17.filter_ref), custom_call_target="tpu_custom_call" | custom-call | tf_op jit(solution)/shard_map/filters/pallas_call | solution.py:224
  26.1 1.3 %copy-done = bf16[32,128,256]{2,1,0:T(8,128)(2,1)} copy-done((bf16[32,128,256]{2,1,0:T(8,128)(2,1)}, bf16[32,128,256]{2,1,0:T(8,128)(2,1)S(1)}, u32[]{:S(2)}) %copy-start) | copy-done | bytes 2097176
  27.5 0.0 collective-permute-done.5.refs_4_.refs_9_
  27.5 0.1 collective-permute-start.7
  27.6 0.0 collective-permute-done.6.refs_0_.refs_11_
  27.6 0.5 collective-permute-start.8
  28.1 0.0 collective-permute-done
  28.1 0.9 %broadcast_select_fusion.3 = (bf16[128,256]{1,0:T(8,128)(2,1)S(1)}, bf16[128,256]{1,0:T(8,128)(2,1)S(1)}) fusion(bf16[128,256]{1,0:T(8,128)(2,1)} %collective-permute-done, pred[]{:T(512)S(6)} %eq.5, bf16[144,256]{1,0:T(8,128)(2,1)} %collective-permute-done.1.refs_5_.refs_10_), kind=kLoop, calls=%fused_computation.9 | loop fusion | flops 65536 | bytes 262145 | tf_op jit(solution)/shard_map/jit(_where)/select_n | solution.py:382
  29.0 0.9 %pad_maximum_fusion.3.table_ref = bf16[384,256]{1,0:T(8,128)(2,1)S(1)} fusion(bf16[128,256]{1,0:T(8,128)(2,1)S(1)} %get-tuple-element.24, bf16[128,256]{1,0:T(8,128)(2,1)} %own_ref.3, bf16[128,256]{1,0:T(8,128)(2,1)S(1)} %get-tuple-element.23), kind=kLoop, calls=%fused_computation.3 | loop fusion | flops 589824 | bytes 393216 | tf_op jit(solution)/shard_map/concatenate | solution.py:382
  29.9 1.6 %copy-done.1 = bf16[32,128,256]{2,1,0:T(8,128)(2,1)S(1)} copy-done((bf16[32,128,256]{2,1,0:T(8,128)(2,1)S(1)}, bf16[32,128,256]{2,1,0:T(8,128)(2,1)}, u32[]{:S(2)}) %copy-start.1) | copy-done | bytes 2097176
  31.4 0.8 %copy-done.16 = s32[64,128]{1,0:T(8,128)S(1)} copy-done((s32[64,128]{1,0:T(8,128)S(1)}, s32[64,128]{1,0:T(8,128)}, u32[]{:S(2)}) %copy-start.16) | copy-done | bytes 32792
  32.2 0.8 %copy-done.17 = s32[64,128]{1,0:T(8,128)S(1)} copy-done((s32[64,128]{1,0:T(8,128)S(1)}, s32[64,128]{1,0:T(8,128)}, u32[]{:S(2)}) %copy-start.17) | copy-done | bytes 32792
  33.0 2.8 %messages.2.refs_0_ = bf16[128,256]{1,0:T(8,128)(2,1)S(1)} custom-call(s32[64,128]{1,0:T(8,128)S(1)} %copy-done.16, f32[64,128]{1,0:T(8,128)S(1)} %get-tuple-element.14.distance_ref, s32[64,128]{1,0:T(8,128)S(1)} %copy-done.17, bf16[384,256]{1,0:T(8,128)(2,1)S(1)} %pad_maximum_fusion.3.table_ref, bf16[32,128,256]{2,1,0:T(8,128)(2,1)S(1)} %filters.4.refs_0_, ...), custom_call_target="tpu_custom_call" | custom-call | tf_op jit(solution)/shard_map/messages/pallas_call | solution.py:266
  35.8 0.0 copy-start.4
  35.8 0.0 copy-start.5
  35.8 0.0 copy-start.6
  35.8 0.0 copy-start.11
  35.8 2.2 %coupling.3.refs_2_.refs_0_ = bf16[128,768]{1,0:T(8,128)(2,1)S(1)} custom-call(bf16[13,128,256]{2,1,0:T(8,128)(2,1)S(1)} %get-tuple-element.18.left_ref, f32[128,128]{1,0:T(8,128)S(1)} %copy-done.8, f32[128,128]{1,0:T(8,128)S(1)} %copy-done.10, bf16[144,256]{1,0:T(8,128)(2,1)} %get-tuple-element.15.refs_0_.refs_5_, ...), custom_call_target="tpu_custom_call" | custom-call | tf_op jit(solution)/shard_map/coupling/pallas_call | solution.py:186
  38.1 2.5 %coupling.4.refs_3_.refs_1_ = bf16[128,896]{1,0:T(8,128)(2,1)S(1)} custom-call(bf16[13,128,256]{2,1,0:T(8,128)(2,1)S(1)} %get-tuple-element.18.left_ref, f32[128,128]{1,0:T(8,128)S(1)} %copy-done.8, f32[128,128]{1,0:T(8,128)S(1)} %copy-done.10, bf16[432,256]{1,0:T(8,128)(2,1)} %collective-permute-done.6.refs_0_.refs_11_, ...), custom_call_target="tpu_custom_call" | custom-call | tf_op jit(solution)/shard_map/coupling/pallas_call | solution.py:186
  40.6 0.0 copy-start.2
  40.6 0.0 copy-start.3
  40.6 0.0 copy-start.12
  40.6 1.0 %coupling.5.refs_4_.refs_2_ = bf16[128,384]{1,0:T(8,128)(2,1)S(1)} custom-call(bf16[13,128,256]{2,1,0:T(8,128)(2,1)S(1)} %get-tuple-element.18.left_ref, f32[128,128]{1,0:T(8,128)S(1)} %copy-done.8, f32[128,128]{1,0:T(8,128)S(1)} %copy-done.10, bf16[432,256]{1,0:T(8,128)(2,1)S(1)} %collective-permute-done.8.refs_0_.refs_13_), custom_call_target="tpu_custom_call" | custom-call | tf_op jit(solution)/shard_map/coupling/pallas_call | solution.py:186
  41.6 1.8 %update.2.refs_2_.own_ref = bf16[128,256]{1,0:T(8,128)(2,1)S(1)} custom-call(bf16[128,256]{1,0:T(8,128)(2,1)S(1)} %copy-done.11, bf16[2,256,256]{2,1,0:T(8,128)(2,1)S(1)} %copy-done.5, bf16[2,256,256]{2,1,0:T(8,128)(2,1)S(1)} %copy-done.6, bf16[128,256]{1,0:T(8,128)(2,1)S(1)} %messages.2.refs_0_, bf16[2,256,256]{2,1,0:T(8,128)(2,1)S(1)} %copy-done.4, ...), custom_call_target="tpu_custom_call" | custom-call | tf_op jit(solution)/shard_map/update/pallas_call | solution.py:320
  43.4 2.7 %collective-permute-start.11 = (bf16[128,256]{1,0:T(8,128)(2,1)S(1)}, bf16[128,256]{1,0:T(8,128)(2,1)S(1)}, u32[]{:S(2)}, u32[]{:S(2)}) collective-permute-start(bf16[128,256]{1,0:T(8,128)(2,1)S(1)} %update.2.refs_2_.own_ref), channel_id=1, source_target_pairs={{0,12},{1,13},{2,14},{3,15},{4,8},{5,9},{6,10},{7,11},{8,4},{9,5},... | collective-permute-start | bytes 196616 | tf_op jit(solution)/shard_map/ppermute | solution.py:339
  46.2 0.0 collective-permute-start.12
  46.2 1.7 %collective-permute-start.13 = (bf16[128,256]{1,0:T(8,128)(2,1)S(1)}, bf16[128,256]{1,0:T(8,128)(2,1)S(1)}, u32[]{:S(2)}, u32[]{:S(2)}) collective-permute-start(bf16[128,256]{1,0:T(8,128)(2,1)S(1)} %update.2.refs_2_.own_ref), channel_id=1, source_target_pairs={{0,4},{1,5},{2,6},{3,7},{4,0},{5,1},{6,2},{7,3},{8,12},{9,13},{10,... | collective-permute-start | bytes 196616 | tf_op jit(solution)/shard_map/ppermute | solution.py:339
  47.9 2.3 %collective-permute-done.11.refs_3_ = bf16[128,256]{1,0:T(8,128)(2,1)S(1)} collective-permute-done((bf16[128,256]{1,0:T(8,128)(2,1)S(1)}, bf16[128,256]{1,0:T(8,128)(2,1)S(1)}, u32[]{:S(2)}, u32[]{:S(2)}) %collective-permute-start.11) | collective-permute-done | bytes 65568 | tf_op jit(solution)/shard_map/ppermute | solution.py:339
  50.2 2.2 %collective-permute-done.12.refs_4_ = bf16[128,256]{1,0:T(8,128)(2,1)S(1)} collective-permute-done((bf16[128,256]{1,0:T(8,128)(2,1)S(1)}, bf16[128,256]{1,0:T(8,128)(2,1)S(1)}, u32[]{:S(2)}, u32[]{:S(2)}) %collective-permute-start.12) | collective-permute-done | bytes 65568 | tf_op jit(solution)/shard_map/ppermute | solution.py:339
  52.4 0.0 collective-permute-done.13.refs_5_
  52.4 1.0 %collective-permute-start.15 = (bf16[384,256]{1,0:T(8,128)(2,1)S(1)}, bf16[384,256]{1,0:T(8,128)(2,1)S(1)}, u32[]{:S(2)}, u32[]{:S(2)}) collective-permute-start(bf16[384,256]{1,0:T(8,128)(2,1)S(1)} %pad_maximum_fusion.5), channel_id=1, source_target_pairs={{0,2},{1,3},{2,0},{3,1},{4,6},{5,7},{6,4},{7,5},{8,10},{9,11},{10,... | collective-permute-start | bytes 589832 | tf_op jit(solution)/shard_map/ppermute | solution.py:339
  53.4 1.1 %collective-permute-start.14 = (bf16[128,256]{1,0:T(8,128)(2,1)S(1)}, bf16[128,256]{1,0:T(8,128)(2,1)S(1)}, u32[]{:S(2)}, u32[]{:S(2)}) collective-permute-start(bf16[128,256]{1,0:T(8,128)(2,1)S(1)} %update.2.refs_2_.own_ref), channel_id=1, source_target_pairs={{0,2},{1,3},{2,0},{3,1},{4,6},{5,7},{6,4},{7,5},{8,10},{9,11},{10,... | collective-permute-start | bytes 196616 | tf_op jit(solution)/shard_map/ppermute | solution.py:339
  54.5 2.7 %filters.6.refs_0_ = bf16[32,128,256]{2,1,0:T(8,128)(2,1)S(1)} custom-call(f32[64,128]{1,0:T(8,128)S(1)} %copy-done.12, bf16[2,64,512]{2,1,0:T(8,128)(2,1)S(1)} %copy-done.3, bf16[2,512,256]{2,1,0:T(8,128)(2,1)S(1)} %copy-done.2), custom_call_target="tpu_custom_call" | custom-call | tf_op jit(solution)/shard_map/filters/pallas_call | solution.py:224
  57.3 0.0 copy-start.18
  57.3 2.7 %filters.7.refs_1_ = bf16[32,128,256]{2,1,0:T(8,128)(2,1)S(1)} custom-call(f32[64,128]{1,0:T(8,128)S(1)} %copy-done.12, bf16[2,64,512]{2,1,0:T(8,128)(2,1)S(1)} %copy-done.3, bf16[2,512,256]{2,1,0:T(8,128)(2,1)S(1)} %copy-done.2), custom_call_target="tpu_custom_call" | custom-call | tf_op jit(solution)/shard_map/filters/pallas_call | solution.py:224
  60.0 2.0 %collective-permute-start.9 = (bf16[128,256]{1,0:T(8,128)(2,1)S(1)}, bf16[128,256]{1,0:T(8,128)(2,1)S(1)}, u32[]{:S(2)}, u32[]{:S(2)}) collective-permute-start(bf16[128,256]{1,0:T(8,128)(2,1)S(1)} %update.2.refs_2_.own_ref), channel_id=1, source_target_pairs={{0,15},{1,2},{2,1},{3,4},{4,3},{5,6},{6,5},{7,8},{8,7},{9,10},{10,... | collective-permute-start | bytes 196616 | tf_op jit(solution)/shard_map/ppermute | solution.py:379
  62.0 0.0 collective-permute-start.10
  62.0 0.0 collective-permute-done.14.refs_6_
  62.0 0.6 collective-permute-start.16
  62.6 0.0 collective-permute-done.15.refs_8_
  62.6 0.1 collective-permute-start.17
  62.7 3.7 %collective-permute-done.9 = bf16[128,256]{1,0:T(8,128)(2,1)S(1)} collective-permute-done((bf16[128,256]{1,0:T(8,128)(2,1)S(1)}, bf16[128,256]{1,0:T(8,128)(2,1)S(1)}, u32[]{:S(2)}, u32[]{:S(2)}) %collective-permute-start.9) | collective-permute-done | bytes 65568 | tf_op jit(solution)/shard_map/ppermute | solution.py:379
  66.5 2.8 %messages.3.message_ref = bf16[128,256]{1,0:T(8,128)(2,1)S(1)} custom-call(s32[64,128]{1,0:T(8,128)S(1)} %copy-done.16, f32[64,128]{1,0:T(8,128)S(1)} %copy-done.12, s32[64,128]{1,0:T(8,128)S(1)} %copy-done.18, bf16[384,256]{1,0:T(8,128)(2,1)S(1)} %pad_maximum_fusion.4.table_ref, bf16[32,128,256]{2,1,0:T(8,128)(2,1)S(1)} %filters.6.refs_0_, ...), custom_call_target="tpu_custom_call" | custom-call | tf_op jit(solution)/shard_map/messages/pallas_call | solution.py:266
  69.3 0.0 collective-permute-done.16.refs_9_
  69.3 0.4 partial.1
  69.7 0.0 collective-permute-done.17.refs_3_
  69.7 1.1 %update.3 = bf16[128,256]{1,0:T(8,128)(2,1)} custom-call(bf16[128,256]{1,0:T(8,128)(2,1)S(1)} %update.2.refs_2_.own_ref, bf16[2,256,256]{2,1,0:T(8,128)(2,1)S(1)} %copy-done.5, bf16[2,256,256]{2,1,0:T(8,128)(2,1)S(1)} %copy-done.6, f32[128,256]{1,0:T(8,128)S(1)} %get-tuple-element.21.refs_0_, f32[128,256]{1,0:T(8,128)S(1)} %get-tuple-element.22.refs_1_, ...), custom_call_target="tpu_custom_call" | custom-call | tf_op jit(solution)/shard_map/update/pallas_call | solution.py:320
  (31 shorter events, 0.1 us)
Async XLA Ops:
  2.1 0.6 copy-start.7
  2.7 0.6 copy-start.9
  3.3 0.6 copy-start.13
  4.0 8.1 %collective-permute-start.2 = (bf16[144,256]{1,0:T(8,128)(2,1)}, bf16[144,256]{1,0:T(8,128)(2,1)S(1)}, u32[]{:S(2)}, u32[]{:S(2)}) collective-permute-start(bf16[144,256]{1,0:T(8,128)(2,1)} %get-tuple-element.15.refs_0_.refs_5_), channel_id=1, source_target_pairs={{0,12},{1,13},{2,14},{3,15},{4,8},{5,9},{6,10},{7,11},{8,4},{9,5},... | collective-permute-start | bytes 221192 | tf_op jit(solution)/shard_map/ppermute | solution.py:339
  9.0 6.4 %collective-permute-start.3 = (bf16[144,256]{1,0:T(8,128)(2,1)}, bf16[144,256]{1,0:T(8,128)(2,1)S(1)}, u32[]{:S(2)}, u32[]{:S(2)}) collective-permute-start(bf16[144,256]{1,0:T(8,128)(2,1)} %get-tuple-element.15.refs_0_.refs_5_), channel_id=1, source_target_pairs={{0,8},{1,9},{2,10},{3,11},{4,12},{5,13},{6,14},{7,15},{8,0},{9,1},... | collective-permute-start | bytes 221192 | tf_op jit(solution)/shard_map/ppermute | solution.py:339
  9.0 6.4 %collective-permute-start.4 = (bf16[144,256]{1,0:T(8,128)(2,1)}, bf16[144,256]{1,0:T(8,128)(2,1)S(1)}, u32[]{:S(2)}, u32[]{:S(2)}) collective-permute-start(bf16[144,256]{1,0:T(8,128)(2,1)} %get-tuple-element.15.refs_0_.refs_5_), channel_id=1, source_target_pairs={{0,4},{1,5},{2,6},{3,7},{4,0},{5,1},{6,2},{7,3},{8,12},{9,13},{10,... | collective-permute-start | bytes 221192 | tf_op jit(solution)/shard_map/ppermute | solution.py:339
  16.2 11.4 %collective-permute-start.6 = (bf16[432,256]{1,0:T(8,128)(2,1)}, bf16[432,256]{1,0:T(8,128)(2,1)}, u32[]{:S(2)}, u32[]{:S(2)}) collective-permute-start(bf16[432,256]{1,0:T(8,128)(2,1)} %pad_maximum_fusion.2), channel_id=1, source_target_pairs={{0,2},{1,3},{2,0},{3,1},{4,6},{5,7},{6,4},{7,5},{8,10},{9,11},{10,... | collective-permute-start | bytes 663560 | tf_op jit(solution)/shard_map/ppermute | solution.py:339
  17.7 9.8 %collective-permute-start.5 = (bf16[144,256]{1,0:T(8,128)(2,1)}, bf16[144,256]{1,0:T(8,128)(2,1)S(1)}, u32[]{:S(2)}, u32[]{:S(2)}) collective-permute-start(bf16[144,256]{1,0:T(8,128)(2,1)} %get-tuple-element.15.refs_0_.refs_5_), channel_id=1, source_target_pairs={{0,2},{1,3},{2,0},{3,1},{4,6},{5,7},{6,4},{7,5},{8,10},{9,11},{10,... | collective-permute-start | bytes 221192 | tf_op jit(solution)/shard_map/ppermute | solution.py:339
  18.2 9.9 %collective-permute-start = (bf16[128,256]{1,0:T(8,128)(2,1)}, bf16[128,256]{1,0:T(8,128)(2,1)}, u32[]{:S(2)}, u32[]{:S(2)}) collective-permute-start(bf16[128,256]{1,0:T(8,128)(2,1)} %own_ref.3), channel_id=1, source_target_pairs={{0,15},{1,2},{2,1},{3,4},{4,3},{5,6},{6,5},{7,8},{8,7},{9,10},{10,... | collective-permute-start | bytes 196616 | tf_op jit(solution)/shard_map/ppermute | solution.py:379
  19.2 8.9 %collective-permute-start.1 = (bf16[144,256]{1,0:T(8,128)(2,1)}, bf16[144,256]{1,0:T(8,128)(2,1)}, u32[]{:S(2)}, u32[]{:S(2)}) collective-permute-start(bf16[144,256]{1,0:T(8,128)(2,1)} %get-tuple-element.15.refs_0_.refs_5_), channel_id=1, source_target_pairs={{0,1},{1,0},{2,3},{3,2},{4,5},{5,4},{6,7},{7,6},{8,9},{9,8},{10,11... | collective-permute-start | bytes 221192 | tf_op jit(solution)/shard_map/ppermute | solution.py:339
  19.9 0.8 %copy-start.14 = (bf16[1,64,512]{2,1,0:T(8,128)(2,1)S(1)}, bf16[1,64,512]{2,1,0:T(8,128)(2,1)}, u32[]{:S(2)}) copy-start(bf16[1,64,512]{2,1,0:T(8,128)(2,1)} %copy-done.13) | copy-start | bytes 196612
  20.7 2.7 %copy-start.15 = (bf16[1,64,512]{2,1,0:T(8,128)(2,1)S(1)}, bf16[1,64,512]{2,1,0:T(8,128)(2,1)}, u32[]{:S(2)}) copy-start(bf16[1,64,512]{2,1,0:T(8,128)(2,1)} %copy-done.13) | copy-start | bytes 196612
  26.1 1.4 %copy-start = (bf16[32,128,256]{2,1,0:T(8,128)(2,1)}, bf16[32,128,256]{2,1,0:T(8,128)(2,1)S(1)}, u32[]{:S(2)}) copy-start(bf16[32,128,256]{2,1,0:T(8,128)(2,1)S(1)} %filters.5.refs_1_) | copy-start | bytes 6291460
  27.5 10.6 %collective-permute-start.7 = (bf16[576,256]{1,0:T(8,128)(2,1)S(1)}, bf16[576,256]{1,0:T(8,128)(2,1)S(1)}, u32[]{:S(2)}, u32[]{:S(2)}) collective-permute-start(bf16[576,256]{1,0:T(8,128)(2,1)S(1)} %pad_maximum_fusion), channel_id=1, source_target_pairs={{0,1},{1,0},{2,3},{3,2},{4,5},{5,4},{6,7},{7,6},{8,9},{9,8},{10,11... | collective-permute-start | bytes 884744 | tf_op jit(solution)/shard_map/ppermute | solution.py:339
  27.6 13.0 %collective-permute-start.8 = (bf16[432,256]{1,0:T(8,128)(2,1)}, bf16[432,256]{1,0:T(8,128)(2,1)S(1)}, u32[]{:S(2)}, u32[]{:S(2)}) collective-permute-start(bf16[432,256]{1,0:T(8,128)(2,1)} %collective-permute-done.6.refs_0_.refs_11_), channel_id=1, source_target_pairs={{0,1},{1,0},{2,3},{3,2},{4,5},{5,4},{6,7},{7,6},{8,9},{9,8},{10,11... | collective-permute-start | bytes 663560 | tf_op jit(solution)/shard_map/ppermute | solution.py:339
  29.8 1.6 %copy-start.1 = (bf16[32,128,256]{2,1,0:T(8,128)(2,1)S(1)}, bf16[32,128,256]{2,1,0:T(8,128)(2,1)}, u32[]{:S(2)}) copy-start(bf16[32,128,256]{2,1,0:T(8,128)(2,1)} %copy-done) | copy-start | bytes 6291460
  31.4 0.8 %copy-start.16 = (s32[64,128]{1,0:T(8,128)S(1)}, s32[64,128]{1,0:T(8,128)}, u32[]{:S(2)}) copy-start(s32[64,128]{1,0:T(8,128)} %index_ref.3) | copy-start | bytes 98308
  32.2 0.8 %copy-start.17 = (s32[64,128]{1,0:T(8,128)S(1)}, s32[64,128]{1,0:T(8,128)}, u32[]{:S(2)}) copy-start(s32[64,128]{1,0:T(8,128)} %mask_ref.3) | copy-start | bytes 98308
  33.0 2.8 %copy-start.8 = (f32[128,128]{1,0:T(8,128)S(1)}, f32[128,128]{1,0:T(8,128)}, u32[]{:S(2)}) copy-start(f32[128,128]{1,0:T(8,128)} %copy-done.7) | copy-start | bytes 196612
  33.0 2.8 %copy-start.10 = (f32[128,128]{1,0:T(8,128)S(1)}, f32[128,128]{1,0:T(8,128)}, u32[]{:S(2)}) copy-start(f32[128,128]{1,0:T(8,128)} %copy-done.9) | copy-start | bytes 196612
  35.8 5.8 %copy-start.4 = (bf16[2,256,256]{2,1,0:T(8,128)(2,1)S(1)}, bf16[2,256,256]{2,1,0:T(8,128)(2,1)}, u32[]{:S(2)}) copy-start(bf16[2,256,256]{2,1,0:T(8,128)(2,1)} %short_ref.1) | copy-start | bytes 786436
  35.8 5.8 %copy-start.5 = (bf16[2,256,256]{2,1,0:T(8,128)(2,1)S(1)}, bf16[2,256,256]{2,1,0:T(8,128)(2,1)}, u32[]{:S(2)}) copy-start(bf16[2,256,256]{2,1,0:T(8,128)(2,1)} %mixing_ref.3) | copy-start | bytes 786436
  35.8 5.8 %copy-start.6 = (bf16[2,256,256]{2,1,0:T(8,128)(2,1)S(1)}, bf16[2,256,256]{2,1,0:T(8,128)(2,1)}, u32[]{:S(2)}) copy-start(bf16[2,256,256]{2,1,0:T(8,128)(2,1)} %long_ref.3) | copy-start | bytes 786436
  35.8 5.8 %copy-start.11 = (bf16[128,256]{1,0:T(8,128)(2,1)S(1)}, bf16[128,256]{1,0:T(8,128)(2,1)}, u32[]{:S(2)}) copy-start(bf16[128,256]{1,0:T(8,128)(2,1)} %own_ref.3) | copy-start | bytes 196612
  40.6 14.0 %copy-start.2 = (bf16[2,512,256]{2,1,0:T(8,128)(2,1)S(1)}, bf16[2,512,256]{2,1,0:T(8,128)(2,1)}, u32[]{:S(2)}) copy-start(bf16[2,512,256]{2,1,0:T(8,128)(2,1)} %filter_ref.5) | copy-start | bytes 1572868
  40.6 14.0 %copy-start.3 = (bf16[2,64,512]{2,1,0:T(8,128)(2,1)S(1)}, bf16[2,64,512]{2,1,0:T(8,128)(2,1)}, u32[]{:S(2)}) copy-start(bf16[2,64,512]{2,1,0:T(8,128)(2,1)} %rbf_ref.5) | copy-start | bytes 393220
  40.6 14.0 %copy-start.12 = (f32[64,128]{1,0:T(8,128)S(1)}, f32[64,128]{1,0:T(8,128)}, u32[]{:S(2)}) copy-start(f32[64,128]{1,0:T(8,128)} %distance_ref.7) | copy-start | bytes 98308
  43.4 6.7 %collective-permute-start.11 = (bf16[128,256]{1,0:T(8,128)(2,1)S(1)}, bf16[128,256]{1,0:T(8,128)(2,1)S(1)}, u32[]{:S(2)}, u32[]{:S(2)}) collective-permute-start(bf16[128,256]{1,0:T(8,128)(2,1)S(1)} %update.2.refs_2_.own_ref), channel_id=1, source_target_pairs={{0,12},{1,13},{2,14},{3,15},{4,8},{5,9},{6,10},{7,11},{8,4},{9,5},... | collective-permute-start | bytes 196616 | tf_op jit(solution)/shard_map/ppermute | solution.py:339
  46.2 6.3 %collective-permute-start.12 = (bf16[128,256]{1,0:T(8,128)(2,1)S(1)}, bf16[128,256]{1,0:T(8,128)(2,1)S(1)}, u32[]{:S(2)}, u32[]{:S(2)}) collective-permute-start(bf16[128,256]{1,0:T(8,128)(2,1)S(1)} %update.2.refs_2_.own_ref), channel_id=1, source_target_pairs={{0,8},{1,9},{2,10},{3,11},{4,12},{5,13},{6,14},{7,15},{8,0},{9,1},... | collective-permute-start | bytes 196616 | tf_op jit(solution)/shard_map/ppermute | solution.py:339
  46.2 6.3 %collective-permute-start.13 = (bf16[128,256]{1,0:T(8,128)(2,1)S(1)}, bf16[128,256]{1,0:T(8,128)(2,1)S(1)}, u32[]{:S(2)}, u32[]{:S(2)}) collective-permute-start(bf16[128,256]{1,0:T(8,128)(2,1)S(1)} %update.2.refs_2_.own_ref), channel_id=1, source_target_pairs={{0,4},{1,5},{2,6},{3,7},{4,0},{5,1},{6,2},{7,3},{8,12},{9,13},{10,... | collective-permute-start | bytes 196616 | tf_op jit(solution)/shard_map/ppermute | solution.py:339
  52.4 10.2 %collective-permute-start.15 = (bf16[384,256]{1,0:T(8,128)(2,1)S(1)}, bf16[384,256]{1,0:T(8,128)(2,1)S(1)}, u32[]{:S(2)}, u32[]{:S(2)}) collective-permute-start(bf16[384,256]{1,0:T(8,128)(2,1)S(1)} %pad_maximum_fusion.5), channel_id=1, source_target_pairs={{0,2},{1,3},{2,0},{3,1},{4,6},{5,7},{6,4},{7,5},{8,10},{9,11},{10,... | collective-permute-start | bytes 589832 | tf_op jit(solution)/shard_map/ppermute | solution.py:339
  53.4 8.6 %collective-permute-start.14 = (bf16[128,256]{1,0:T(8,128)(2,1)S(1)}, bf16[128,256]{1,0:T(8,128)(2,1)S(1)}, u32[]{:S(2)}, u32[]{:S(2)}) collective-permute-start(bf16[128,256]{1,0:T(8,128)(2,1)S(1)} %update.2.refs_2_.own_ref), channel_id=1, source_target_pairs={{0,2},{1,3},{2,0},{3,1},{4,6},{5,7},{6,4},{7,5},{8,10},{9,11},{10,... | collective-permute-start | bytes 196616 | tf_op jit(solution)/shard_map/ppermute | solution.py:339
  57.3 9.2 %copy-start.18 = (s32[64,128]{1,0:T(8,128)S(1)}, s32[64,128]{1,0:T(8,128)}, u32[]{:S(2)}) copy-start(s32[64,128]{1,0:T(8,128)} %mask_ref.3) | copy-start | bytes 98308
  60.0 6.5 %collective-permute-start.9 = (bf16[128,256]{1,0:T(8,128)(2,1)S(1)}, bf16[128,256]{1,0:T(8,128)(2,1)S(1)}, u32[]{:S(2)}, u32[]{:S(2)}) collective-permute-start(bf16[128,256]{1,0:T(8,128)(2,1)S(1)} %update.2.refs_2_.own_ref), channel_id=1, source_target_pairs={{0,15},{1,2},{2,1},{3,4},{4,3},{5,6},{6,5},{7,8},{8,7},{9,10},{10,... | collective-permute-start | bytes 196616 | tf_op jit(solution)/shard_map/ppermute | solution.py:379
  62.0 4.4 %collective-permute-start.10 = (bf16[128,256]{1,0:T(8,128)(2,1)S(1)}, bf16[128,256]{1,0:T(8,128)(2,1)S(1)}, u32[]{:S(2)}, u32[]{:S(2)}) collective-permute-start(bf16[128,256]{1,0:T(8,128)(2,1)S(1)} %update.2.refs_2_.own_ref), channel_id=1, source_target_pairs={{0,1},{1,0},{2,3},{3,2},{4,5},{5,4},{6,7},{7,6},{8,9},{9,8},{10,11... | collective-permute-start | bytes 196616 | tf_op jit(solution)/shard_map/ppermute | solution.py:339
  62.0 7.3 %collective-permute-start.16 = (bf16[512,256]{1,0:T(8,128)(2,1)S(1)}, bf16[512,256]{1,0:T(8,128)(2,1)S(1)}, u32[]{:S(2)}, u32[]{:S(2)}) collective-permute-start(bf16[512,256]{1,0:T(8,128)(2,1)S(1)} %pad_maximum_fusion.1), channel_id=1, source_target_pairs={{0,1},{1,0},{2,3},{3,2},{4,5},{5,4},{6,7},{7,6},{8,9},{9,8},{10,11... | collective-permute-start | bytes 786440 | tf_op jit(solution)/shard_map/ppermute | solution.py:339
  62.6 7.1 %collective-permute-start.17 = (bf16[384,256]{1,0:T(8,128)(2,1)S(1)}, bf16[384,256]{1,0:T(8,128)(2,1)S(1)}, u32[]{:S(2)}, u32[]{:S(2)}) collective-permute-start(bf16[384,256]{1,0:T(8,128)(2,1)S(1)} %collective-permute-done.15.refs_8_), channel_id=1, source_target_pairs={{0,1},{1,0},{2,3},{3,2},{4,5},{5,4},{6,7},{7,6},{8,9},{9,8},{10,11... | collective-permute-start | bytes 589832 | tf_op jit(solution)/shard_map/ppermute | solution.py:339

commit v2 on v1

--- a/solution.py
+++ b/solution.py
@@ -10,6 +10,7 @@
 
 
 message_group = 16
+filter_group = 8
 reach = 6
 orders = reach + 1
 columns = 16
@@ -203,26 +204,35 @@
     return coupling(prepared, [arrays[n] for n in used], spots, rows)
 
 
-def filter_kernel(layer, begin, distance_ref, rbf_ref, filter_ref, out_ref):
-    group, rows, _ = out_ref.shape
-    count = rbf_ref.shape[1]
+def centers_of(count, rows):
     step = lax.broadcasted_iota(jnp.int32, (count, rows), 0).astype(F32)
-    centers = 0.5 + 4.5 * step / (count - 1)
+    return 0.5 + 4.5 * step / (count - 1)
+
+
+def filters_at(distance_ref, begin, count, centers, first, second):
     pieces = []
-    for s in range(begin, begin + group):
+    for s in range(begin, begin + count):
         offset = distance_ref[s : s + 1, :] - centers
         pieces.append(jnp.exp(-4.0 * offset * offset).astype(BF))
-    basis = jnp.concatenate(pieces, axis=1)
-    half = dot_dims(basis, rbf_ref[layer] * jnp.asarray(0.5, BF), 0, 0)
+    half = dot_dims(jnp.concatenate(pieces, axis=1), first, 0, 0)
     inner = (half + half * jnp.tanh(half)).astype(BF)
-    out_ref[...] = dot(inner, filter_ref[layer]).astype(BF).reshape(out_ref.shape)
-
-
-def filters_of(distances, w_rbf, w_filter, layer, begin, count):
+    return dot(inner, second).reshape(count, centers.shape[1], second.shape[1])
+
+
+def filter_kernel(layer, distance_ref, rbf_ref, filter_ref, out_ref):
+    group, rows, _ = out_ref.shape
+    centers = centers_of(rbf_ref.shape[1], rows)
+    first = rbf_ref[layer] * jnp.asarray(0.5, BF)
+    for chunk in range(0, group, filter_group):
+        made = filters_at(distance_ref, chunk, filter_group, centers, first, filter_ref[layer])
+        out_ref[chunk : chunk + filter_group] = made.astype(BF)
+
+
+def filters_of(distances, w_rbf, w_filter, layer, count):
     rows = distances.shape[1]
     width = w_filter.shape[2]
     return pl.pallas_call(
-        functools.partial(filter_kernel, layer, begin),
+        functools.partial(filter_kernel, layer),
         out_shape=jax.ShapeDtypeStruct((count, rows, width), BF),
         in_specs=[VM] * 3,
         out_specs=VM,
@@ -235,15 +245,20 @@
     return jnp.where(index < 256, index, 255 - index).astype(F32).astype(BF)
 
 
-def message_kernel(index_ref, distance_ref, mask_ref, table_ref, *refs):
-    filter_refs, out_ref = refs[:-1], refs[-1]
+def message_kernel(
+    layer, index_ref, distance_ref, mask_ref, table_ref, rbf_ref, filter_ref, ready_ref, out_ref
+):
     slots, rows = index_ref.shape
     reachable, width = table_ref.shape
+    ready = ready_ref.shape[0]
+    lane = code_of(lax.broadcasted_iota(jnp.int32, (rows, reachable), 1))
+    centers = centers_of(rbf_ref.shape[1], rows)
+    first = rbf_ref[layer] * jnp.asarray(0.5, BF)
+    total = jnp.zeros((rows, width), F32)
     group = message_group
-    lane = code_of(lax.broadcasted_iota(jnp.int32, (rows, reachable), 1))
-    total = jnp.zeros((rows, width), F32)
-    per = slots // len(filter_refs)
-    for begin in range(0, slots, group):
+    starts = [n for pair in zip(range(0, ready, group), range(ready, slots, group)) for n in pair]
+    starts += [n for n in range(0, slots, group) if n not in starts]
+    for begin in starts:
         at = slice(begin, begin + group)
         code = code_of(index_ref[at, :]).astype(F32).T.astype(BF)
         cosine, _ = turn_trig(distance_ref[at, :] * 0.1)
@@ -253,19 +268,19 @@
             for s in range(group)
         ]
         gathered = dot(jnp.concatenate(picks, axis=0), table_ref[...]).reshape(group, rows, width)
-        where = begin % per
-        factors = filter_refs[begin // per][where : where + group].astype(F32)
+        if begin < ready:
+            factors = ready_ref[at].astype(F32)
+        else:
+            factors = filters_at(distance_ref, begin, group, centers, first, filter_ref[layer])
         total = total + jnp.sum(gathered * factors, axis=0)
     out_ref[...] = total.astype(BF)
 
 
-def messages(neighbours, distances, edge_mask, table, filters):
-    rows = neighbours.shape[1]
-    width = table.shape[1]
-    inputs = (neighbours, distances, edge_mask, table) + tuple(filters)
-    return pl.pallas_call(
-        message_kernel,
-        out_shape=jax.ShapeDtypeStruct((rows, width), BF),
+def messages(neighbours, distances, edge_mask, table, w_rbf, w_filter, layer, ready):
+    inputs = (neighbours, distances, edge_mask, table, w_rbf, w_filter, ready)
+    return pl.pallas_call(
+        functools.partial(message_kernel, layer),
+        out_shape=jax.ShapeDtypeStruct((neighbours.shape[1], table.shape[1]), BF),
         in_specs=[VM] * len(inputs),
         out_specs=VM,
         compiler_params=limit,
@@ -339,16 +354,17 @@
     return lax.ppermute(x, "atom", [(i, i ^ (odd if i % 2 else even)) for i in range(count)])
 
 
-def schedule(count):
+def schedule(count, lean):
     bits = [1 << n for n in range(count.bit_length() - 1)][::-1]
     stages, have = [], [0]
     if len(bits) >= 4:
         far, near, side, last = bits[0], bits[1], bits[2], bits[-1]
         first = [far + near, far, near]
-        second = [side + q for q in first]
-        early = first + [side]
+        early = first if lean else first + [side]
+        sent = [0] + first if lean else first
+        second = [side + q for q in sent]
         stages.append([(mask, mask, [0], [mask]) for mask in early + [last]])
-        stages.append([(side, side, first, second), (last, last, early, [last + q for q in early])])
+        stages.append([(side, side, sent, second), (last, last, early, [last + q for q in early])])
         stages.append([(last, last, second, [last + q for q in second])])
         have = [0] + [q for stage in stages for item in stage for q in item[3]]
         bits = bits[3:-1]
@@ -401,24 +417,24 @@
     before = 1.0 / math.sqrt(rows * bricks)
     after = 4.0 / math.sqrt(wave_index.shape[1])
     even = lax.axis_index("atom") % 2 == 0
-    stages = schedule(bricks)
 
     packed, *prepared, near_distances, first_rbf, first_filter = prepare(
         wave_index, fractional, features, distances, w_rbf, w_filter
     )
-    split = slots // 2
     state = features
     matrices, where = [], {}
 
-    def couple(arrays, places, keep=0):
+    def couple(arrays, places):
         ready = [q for q in places if q not in where]
-        ready = ready[: len(ready) - keep]
+        if len(places) < bricks:
+            ready = ready[: len(ready) // 2 * 2]
         matrix = coupling_of(prepared, arrays, places, ready, rows)
         where.update({q: (len(matrices), n) for n, q in enumerate(ready)})
         matrices.append(matrix)
 
     for layer in range(w_rbf.shape[0]):
         block = state if layer else packed
+        stages = schedule(bricks, False)
         size = block.shape[0]
         arrays, places = exchange([block], {0: (0, 0)}, stages[0], size)
         close = arrays[places[1][0]][:rows] if 1 in places else swap(state, 1, 1)
@@ -427,9 +443,8 @@
             edge = (distances, w_rbf, w_filter, layer)
         else:
             edge = (near_distances, first_rbf, first_filter, 0)
-        first = filters_of(*edge, 0, split)
-        second = filters_of(*edge, split, slots - split)
-        message = messages(neighbours, edge[0], edge_mask, table, (first, second))
+        ready = filters_of(*edge, slots // 2)
+        message = messages(neighbours, edge[0], edge_mask, table, *edge[1:], ready)
         for stage in stages[1:]:
             if layer == 0:
                 couple(arrays, places)

time: 71.3 us -> 59.1 us (0.83)
  local copies, waits for them, and re-layouts: 7.24 us -> 0.05 us
  Pallas kernels: 27.5 us -> 22.3 us
  other arithmetic: 2.55 us -> 0.12 us
  waiting for transfers between devices: 14.2 us -> 16.4 us
    unnamed x38 -> x18, local copies, waits for them, and re-layouts: 7.24 us -> 0.05 us
    ppermute x16, waiting for transfers between devices: 10.4 us -> 14.8 us  [swap(): lax.ppermute(x, 'atom', [(i, i ^ (odd if i % 2 else even)) for i in range...]
    pallas_call x3, Pallas kernels: 5.71 us -> 3.37 us  [coupling(): pl.pallas_call(functools.partial(coupling_kernel, tuple(places), rows), o...]
    ppermute x2, waiting for transfers between devices: 3.74 us -> 1.61 us  [neighbour_table(): lax.ppermute(own, 'atom', [(i, (i + (count - 1 if i % 2 == 0 else 1)) % c...]
    pallas_call x6 -> x4, Pallas kernels: 16.4 us -> 14.9 us  [the longest x2 9.83 us: messages(): pl.pallas_call(functools.partial(message_kernel, layer), out_shape=jax.Sh...]
    select_n x2, other arithmetic: 0.9 us -> 0.03 us  [neighbour_table(): jnp.where(even, far, close)]
    concatenate x2, other arithmetic: 0.87 us -> 0.03 us  [neighbour_table(): jnp.concatenate([jnp.where(even, far, close), own, jnp.where(even, close,...]
    pallas_call x2, Pallas kernels: 2.91 us -> 2.09 us  [update(): pl.pallas_call(functools.partial(update_kernel, tuple(places), len(matric...]
  transfers between devices with their start and end apart: 18 -> 18, of which waited for: 5 -> 7; matrix products, arithmetic and copies ran while one was open for 3% -> 0% of each run, Pallas kernels for 30% -> 30%
where the time goes in v2:
time: 59.1 us; the launch traced here: 59 us
  Pallas kernels  22.3 us (38%)
  starting transfers between devices  19.8 us (34%)
  waiting for transfers between devices  16.4 us (28%)
    ppermute x16, starting transfers between devices, swap(): lax.ppermute(x, 'atom', [(i, i ^ (odd if i % 2 else even)) for i in range...  16.4 us
    ppermute x16, waiting for transfers between devices, swap(): lax.ppermute(x, 'atom', [(i, i ^ (odd if i % 2 else even)) for i in range...  14.8 us
    pallas_call x2, Pallas kernels, messages(): pl.pallas_call(functools.partial(message_kernel, layer), out_shape=jax.Sh...  9.83 us
    pallas_call x2, Pallas kernels, filters_of(): pl.pallas_call(functools.partial(filter_kernel, layer), out_shape=jax.Sha...  5.1 us
    ppermute x2, starting transfers between devices, neighbour_table(): lax.ppermute(own, 'atom', [(i, (i + (count - 1 if i % 2 == 0 else 1)) % c...  3.48 us
    pallas_call x3, Pallas kernels, coupling(): pl.pallas_call(functools.partial(coupling_kernel, tuple(places), rows), o...  3.37 us
    pallas_call x2, Pallas kernels, update(): pl.pallas_call(functools.partial(update_kernel, tuple(places), len(matric...  2.09 us
    ppermute x2, waiting for transfers between devices, neighbour_table(): lax.ppermute(own, 'atom', [(i, (i + (count - 1 if i % 2 == 0 else 1)) % c...  1.61 us
  transfers between devices with their start and end apart: 18, of which 7 were waited for; matrix products, arithmetic and copies ran while one was open for 0% of the time, Pallas kernels for 30%

profile of v2, /device:TPU:0, one launch (start us, length us, event | category | flops | bytes accessed | tf_op | source)
XLA Modules:
  0.0 59.0 jit_solution(18114755735294735226)
XLA Ops:
  0.0 1.5 %prepare.1 = (bf16[144,256]{1,0:T(8,128)(2,1)S(1)}, bf16[13,128,256]{2,1,0:T(8,128)(2,1)S(1)}, f32[128,128]{1,0:T(8,128)S(1)}, f32[128,128]{1,0:T(8,128)S(1)}, f...) custom-call(s32[3,2048]{1,0:T(4,128)} %wave_ref.1, f32[3,128]{1,0:T(4,128)} %position_ref.1, ...), custom_call_target="tpu_custom_call" | custom-call | tf_op jit(solution)/shard_map/prepare/pallas_call | solution.py:137
  1.5 0.0 copy-start.7
  1.6 0.0 copy-start.8
  1.6 5.1 %collective-permute-start.2 = (bf16[144,256]{1,0:T(8,128)(2,1)S(1)}, bf16[144,256]{1,0:T(8,128)(2,1)S(1)}, u32[]{:S(2)}, u32[]{:S(2)}) collective-permute-start(bf16[144,256]{1,0:T(8,128)(2,1)S(1)} %get-tuple-element.15.refs_0_.refs_5_), channel_id=1, source_target_pairs={{0,12},{1,13},{2,14},{3,15},{4,8},{5,9},{6,10},{7,11},{8,4},{9,5},... | collective-permute-start | bytes 221192 | tf_op jit(solution)/shard_map/ppermute | solution.py:354
  6.7 0.0 collective-permute-start.3
  6.7 0.6 %collective-permute-start.4 = (bf16[144,256]{1,0:T(8,128)(2,1)S(1)}, bf16[144,256]{1,0:T(8,128)(2,1)S(1)}, u32[]{:S(2)}, u32[]{:S(2)}) collective-permute-start(bf16[144,256]{1,0:T(8,128)(2,1)S(1)} %get-tuple-element.15.refs_0_.refs_5_), channel_id=1, source_target_pairs={{0,4},{1,5},{2,6},{3,7},{4,0},{5,1},{6,2},{7,3},{8,12},{9,13},{10,... | collective-permute-start | bytes 221192 | tf_op jit(solution)/shard_map/ppermute | solution.py:354
  7.4 2.0 %collective-permute-done.2.refs_1_.refs_6_ = bf16[144,256]{1,0:T(8,128)(2,1)S(1)} collective-permute-done((bf16[144,256]{1,0:T(8,128)(2,1)S(1)}, bf16[144,256]{1,0:T(8,128)(2,1)S(1)}, u32[]{:S(2)}, u32[]{:S(2)}) %collective-permute-start.2) | collective-permute-done | bytes 73760 | tf_op jit(solution)/shard_map/ppermute | solution.py:354
  9.4 3.5 %collective-permute-done.3.refs_2_.refs_7_ = bf16[144,256]{1,0:T(8,128)(2,1)S(1)} collective-permute-done((bf16[144,256]{1,0:T(8,128)(2,1)S(1)}, bf16[144,256]{1,0:T(8,128)(2,1)S(1)}, u32[]{:S(2)}, u32[]{:S(2)}) %collective-permute-start.3) | collective-permute-done | bytes 73760 | tf_op jit(solution)/shard_map/ppermute | solution.py:354
  12.9 0.0 collective-permute-done.4.refs_3_.refs_8_
  13.0 1.6 %collective-permute-start.6 = (bf16[432,256]{1,0:T(8,128)(2,1)S(1)}, bf16[432,256]{1,0:T(8,128)(2,1)S(1)}, u32[]{:S(2)}, u32[]{:S(2)}) collective-permute-start(bf16[432,256]{1,0:T(8,128)(2,1)S(1)} %pad_maximum_fusion.2), channel_id=1, source_target_pairs={{0,2},{1,3},{2,0},{3,1},{4,6},{5,7},{6,4},{7,5},{8,10},{9,11},{10,... | collective-permute-start | bytes 663560 | tf_op jit(solution)/shard_map/ppermute | solution.py:354
  14.5 0.5 collective-permute-start.5
  15.0 1.3 %collective-permute-start = (bf16[128,256]{1,0:T(8,128)(2,1)}, bf16[128,256]{1,0:T(8,128)(2,1)S(1)}, u32[]{:S(2)}, u32[]{:S(2)}) collective-permute-start(bf16[128,256]{1,0:T(8,128)(2,1)} %own_ref.3), channel_id=1, source_target_pairs={{0,15},{1,2},{2,1},{3,4},{4,3},{5,6},{6,5},{7,8},{8,7},{9,10},{10,... | collective-permute-start | bytes 196616 | tf_op jit(solution)/shard_map/ppermute | solution.py:395
  16.3 0.4 collective-permute-start.1
  16.7 2.5 %filters.2.ready_ref = bf16[32,128,256]{2,1,0:T(8,128)(2,1)S(1)} custom-call(f32[64,128]{1,0:T(8,128)S(1)} %get-tuple-element.14.distance_ref, bf16[1,64,512]{2,1,0:T(8,128)(2,1)S(1)} %get-tuple-element.16.rbf_ref, bf16[1,512,256]{2,1,0:T(8,128)(2,1)S(1)} %get-tuple-element.17.filter_ref), custom_call_target="tpu_custom_call" | custom-call | tf_op jit(solution)/shard_map/filters/pallas_call | solution.py:234
  19.2 2.8 %collective-permute-done.5.refs_4_.refs_9_ = bf16[144,256]{1,0:T(8,128)(2,1)S(1)} collective-permute-done((bf16[144,256]{1,0:T(8,128)(2,1)S(1)}, bf16[144,256]{1,0:T(8,128)(2,1)S(1)}, u32[]{:S(2)}, u32[]{:S(2)}) %collective-permute-start.5) | collective-permute-done | bytes 73760 | tf_op jit(solution)/shard_map/ppermute | solution.py:354
  22.1 0.1 collective-permute-start.7
  22.2 0.0 collective-permute-done.6.refs_0_.refs_11_
  22.2 0.5 collective-permute-start.8
  22.7 0.0 collective-permute-done
  22.7 0.0 collective-permute-done.1.refs_5_.refs_10_
  22.7 0.0 copy-done.5
  22.7 0.0 copy-done.7
  22.7 0.0 copy-done.8
  22.7 4.9 %messages.2.refs_0_ = bf16[128,256]{1,0:T(8,128)(2,1)S(1)} custom-call(s32[64,128]{1,0:T(8,128)S(1)} %copy-done.7, f32[64,128]{1,0:T(8,128)S(1)} %get-tuple-element.14.distance_ref, s32[64,128]{1,0:T(8,128)S(1)} %copy-done.8, bf16[384,256]{1,0:T(8,128)(2,1)S(1)} %pad_maximum_fusion.3.table_ref, bf16[1,64,512]{2,1,0:T(8,128)(2,1)S(1)} %get-tuple-element.16.rbf_ref, ...), custom_call_target="tpu_custom_call" | custom-call | tf_op jit(solution)/shard_map/messages/pallas_call | solution.py:281
  27.7 0.0 copy-start.2
  27.7 0.0 copy-start.3
  27.7 0.0 copy-start.4
  27.7 1.3 %coupling.3.refs_2_.refs_0_ = bf16[128,768]{1,0:T(8,128)(2,1)S(1)} custom-call(bf16[13,128,256]{2,1,0:T(8,128)(2,1)S(1)} %get-tuple-element.18.left_ref, f32[128,128]{1,0:T(8,128)S(1)} %get-tuple-element.19.zc_ref, f32[128,128]{1,0:T(8,128)S(1)} %get-tuple-element.20.zs_ref, bf16[144,256]{1,0:T(8,128)(2,1)S(1)} %get-tuple-element.15.refs_0_.refs_5_, ...), custom_call_target="tpu_custom_call" | custom-call | tf_op jit(solution)/shard_map/coupling/pallas_call | solution.py:187
  29.0 0.0 collective-permute-done.7.refs_1_.refs_0_.refs_12_
  29.0 1.3 %coupling.4.refs_3_.refs_1_ = bf16[128,768]{1,0:T(8,128)(2,1)S(1)} custom-call(bf16[13,128,256]{2,1,0:T(8,128)(2,1)S(1)} %get-tuple-element.18.left_ref, f32[128,128]{1,0:T(8,128)S(1)} %get-tuple-element.19.zc_ref, f32[128,128]{1,0:T(8,128)S(1)} %get-tuple-element.20.zs_ref, bf16[432,256]{1,0:T(8,128)(2,1)S(1)} %collective-permute-done.6.refs_0_.refs_11_, ...), custom_call_target="tpu_custom_call" | custom-call | tf_op jit(solution)/shard_map/coupling/pallas_call | solution.py:187
  30.2 0.0 copy-start
  30.2 0.0 copy-start.1
  30.3 0.0 copy-start.6
  30.3 0.0 collective-permute-done.8.refs_1_.refs_13_
  30.3 0.9 %coupling.5.refs_4_.refs_2_ = bf16[128,512]{1,0:T(8,128)(2,1)S(1)} custom-call(bf16[13,128,256]{2,1,0:T(8,128)(2,1)S(1)} %get-tuple-element.18.left_ref, f32[128,128]{1,0:T(8,128)S(1)} %get-tuple-element.19.zc_ref, f32[128,128]{1,0:T(8,128)S(1)} %get-tuple-element.20.zs_ref, bf16[576,256]{1,0:T(8,128)(2,1)S(1)} %collective-permute-done.7.refs_1_.refs_0_.refs_12_, ...), custom_call_target="tpu_custom_call" | custom-call | tf_op jit(solution)/shard_map/coupling/pallas_call | solution.py:187
  31.1 0.0 copy-done.2
  31.2 0.0 copy-done.3
  31.2 0.0 copy-done.4
  31.2 1.0 %update.2.refs_3_.own_ref = bf16[128,256]{1,0:T(8,128)(2,1)S(1)} custom-call(bf16[128,256]{1,0:T(8,128)(2,1)S(1)} %copy-done.5, bf16[2,256,256]{2,1,0:T(8,128)(2,1)S(1)} %copy-done.2, bf16[2,256,256]{2,1,0:T(8,128)(2,1)S(1)} %copy-done.3, bf16[128,256]{1,0:T(8,128)(2,1)S(1)} %messages.2.refs_0_, bf16[2,256,256]{2,1,0:T(8,128)(2,1)S(1)} %copy-done.4, ...), custom_call_target="tpu_custom_call" | custom-call | tf_op jit(solution)/shard_map/update/pallas_call | solution.py:335
  32.1 1.9 %collective-permute-start.11 = (bf16[128,256]{1,0:T(8,128)(2,1)S(1)}, bf16[128,256]{1,0:T(8,128)(2,1)S(1)}, u32[]{:S(2)}, u32[]{:S(2)}) collective-permute-start(bf16[128,256]{1,0:T(8,128)(2,1)S(1)} %update.2.refs_3_.own_ref), channel_id=1, source_target_pairs={{0,12},{1,13},{2,14},{3,15},{4,8},{5,9},{6,10},{7,11},{8,4},{9,5},... | collective-permute-start | bytes 196616 | tf_op jit(solution)/shard_map/ppermute | solution.py:354
  34.1 0.0 collective-permute-start.12
  34.1 2.5 %collective-permute-start.13 = (bf16[128,256]{1,0:T(8,128)(2,1)S(1)}, bf16[128,256]{1,0:T(8,128)(2,1)S(1)}, u32[]{:S(2)}, u32[]{:S(2)}) collective-permute-start(bf16[128,256]{1,0:T(8,128)(2,1)S(1)} %update.2.refs_3_.own_ref), channel_id=1, source_target_pairs={{0,4},{1,5},{2,6},{3,7},{4,0},{5,1},{6,2},{7,3},{8,12},{9,13},{10,... | collective-permute-start | bytes 196616 | tf_op jit(solution)/shard_map/ppermute | solution.py:354
  36.6 2.4 %collective-permute-done.11.refs_4_ = bf16[128,256]{1,0:T(8,128)(2,1)S(1)} collective-permute-done((bf16[128,256]{1,0:T(8,128)(2,1)S(1)}, bf16[128,256]{1,0:T(8,128)(2,1)S(1)}, u32[]{:S(2)}, u32[]{:S(2)}) %collective-permute-start.11) | collective-permute-done | bytes 65568 | tf_op jit(solution)/shard_map/ppermute | solution.py:354
  39.0 1.9 %collective-permute-done.12.refs_5_ = bf16[128,256]{1,0:T(8,128)(2,1)S(1)} collective-permute-done((bf16[128,256]{1,0:T(8,128)(2,1)S(1)}, bf16[128,256]{1,0:T(8,128)(2,1)S(1)}, u32[]{:S(2)}, u32[]{:S(2)}) %collective-permute-start.12) | collective-permute-done | bytes 65568 | tf_op jit(solution)/shard_map/ppermute | solution.py:354
  40.9 0.0 collective-permute-done.13.refs_6_
  40.9 2.5 %collective-permute-start.15 = (bf16[384,256]{1,0:T(8,128)(2,1)S(1)}, bf16[384,256]{1,0:T(8,128)(2,1)S(1)}, u32[]{:S(2)}, u32[]{:S(2)}) collective-permute-start(bf16[384,256]{1,0:T(8,128)(2,1)S(1)} %pad_maximum_fusion.5), channel_id=1, source_target_pairs={{0,2},{1,3},{2,0},{3,1},{4,6},{5,7},{6,4},{7,5},{8,10},{9,11},{10,... | collective-permute-start | bytes 589832 | tf_op jit(solution)/shard_map/ppermute | solution.py:354
  43.4 0.1 collective-permute-start.14
  43.5 0.0 copy-done
  43.5 0.0 copy-done.1
  43.5 0.0 copy-done.6
  43.5 2.6 %filters.3.ready_ref = bf16[32,128,256]{2,1,0:T(8,128)(2,1)S(1)} custom-call(f32[64,128]{1,0:T(8,128)S(1)} %copy-done.6, bf16[2,64,512]{2,1,0:T(8,128)(2,1)S(1)} %copy-done.1, bf16[2,512,256]{2,1,0:T(8,128)(2,1)S(1)} %copy-done), custom_call_target="tpu_custom_call" | custom-call | tf_op jit(solution)/shard_map/filters/pallas_call | solution.py:234
  46.0 2.2 %collective-permute-start.9 = (bf16[128,256]{1,0:T(8,128)(2,1)S(1)}, bf16[128,256]{1,0:T(8,128)(2,1)S(1)}, u32[]{:S(2)}, u32[]{:S(2)}) collective-permute-start(bf16[128,256]{1,0:T(8,128)(2,1)S(1)} %update.2.refs_3_.own_ref), channel_id=1, source_target_pairs={{0,15},{1,2},{2,1},{3,4},{4,3},{5,6},{6,5},{7,8},{8,7},{9,10},{10,... | collective-permute-start | bytes 196616 | tf_op jit(solution)/shard_map/ppermute | solution.py:395
  48.2 0.0 collective-permute-start.10
  48.2 2.0 %collective-permute-done.14.refs_7_ = bf16[128,256]{1,0:T(8,128)(2,1)S(1)} collective-permute-done((bf16[128,256]{1,0:T(8,128)(2,1)S(1)}, bf16[128,256]{1,0:T(8,128)(2,1)S(1)}, u32[]{:S(2)}, u32[]{:S(2)}) %collective-permute-start.14) | collective-permute-done | bytes 65568 | tf_op jit(solution)/shard_map/ppermute | solution.py:354
  50.3 0.1 collective-permute-start.16
  50.4 0.0 collective-permute-done.15.refs_9_
  50.4 0.5 collective-permute-start.17
  50.9 1.6 %collective-permute-done.9 = bf16[128,256]{1,0:T(8,128)(2,1)S(1)} collective-permute-done((bf16[128,256]{1,0:T(8,128)(2,1)S(1)}, bf16[128,256]{1,0:T(8,128)(2,1)S(1)}, u32[]{:S(2)}, u32[]{:S(2)}) %collective-permute-start.9) | collective-permute-done | bytes 65568 | tf_op jit(solution)/shard_map/ppermute | solution.py:395
  52.5 0.0 collective-permute-done.10.refs_8_
  52.5 4.9 %messages.3.message_ref = bf16[128,256]{1,0:T(8,128)(2,1)S(1)} custom-call(s32[64,128]{1,0:T(8,128)S(1)} %copy-done.7, f32[64,128]{1,0:T(8,128)S(1)} %copy-done.6, s32[64,128]{1,0:T(8,128)S(1)} %copy-done.8, bf16[384,256]{1,0:T(8,128)(2,1)S(1)} %pad_maximum_fusion.4.table_ref, bf16[2,64,512]{2,1,0:T(8,128)(2,1)S(1)} %copy-done.1, ...), custom_call_target="tpu_custom_call" | custom-call | tf_op jit(solution)/shard_map/messages/pallas_call | solution.py:281
  57.5 0.0 collective-permute-done.16.refs_10_
  57.5 0.4 partial.1
  57.9 0.0 collective-permute-done.17.refs_3_
  57.9 1.1 %update.3 = bf16[128,256]{1,0:T(8,128)(2,1)} custom-call(bf16[128,256]{1,0:T(8,128)(2,1)S(1)} %update.2.refs_3_.own_ref, bf16[2,256,256]{2,1,0:T(8,128)(2,1)S(1)} %copy-done.2, bf16[2,256,256]{2,1,0:T(8,128)(2,1)S(1)} %copy-done.3, f32[128,256]{1,0:T(8,128)S(1)} %get-tuple-element.21.refs_0_, f32[128,256]{1,0:T(8,128)S(1)} %get-tuple-element.22.refs_1_, ...), custom_call_target="tpu_custom_call" | custom-call | tf_op jit(solution)/shard_map/update/pallas_call | solution.py:335
  (9 shorter events, 0.1 us)
Async XLA Ops:
  0.0 22.7 %copy-start.5 = (bf16[128,256]{1,0:T(8,128)(2,1)S(1)}, bf16[128,256]{1,0:T(8,128)(2,1)}, u32[]{:S(2)}) copy-start(bf16[128,256]{1,0:T(8,128)(2,1)} %own_ref.3) | copy-start | bytes 196612
  1.5 21.2 %copy-start.7 = (s32[64,128]{1,0:T(8,128)S(1)}, s32[64,128]{1,0:T(8,128)}, u32[]{:S(2)}) copy-start(s32[64,128]{1,0:T(8,128)} %index_ref.3) | copy-start | bytes 98308
  1.6 21.2 %copy-start.8 = (s32[64,128]{1,0:T(8,128)S(1)}, s32[64,128]{1,0:T(8,128)}, u32[]{:S(2)}) copy-start(s32[64,128]{1,0:T(8,128)} %mask_ref.3) | copy-start | bytes 98308
  1.6 7.8 %collective-permute-start.2 = (bf16[144,256]{1,0:T(8,128)(2,1)S(1)}, bf16[144,256]{1,0:T(8,128)(2,1)S(1)}, u32[]{:S(2)}, u32[]{:S(2)}) collective-permute-start(bf16[144,256]{1,0:T(8,128)(2,1)S(1)} %get-tuple-element.15.refs_0_.refs_5_), channel_id=1, source_target_pairs={{0,12},{1,13},{2,14},{3,15},{4,8},{5,9},{6,10},{7,11},{8,4},{9,5},... | collective-permute-start | bytes 221192 | tf_op jit(solution)/shard_map/ppermute | solution.py:354
  6.7 6.2 %collective-permute-start.3 = (bf16[144,256]{1,0:T(8,128)(2,1)S(1)}, bf16[144,256]{1,0:T(8,128)(2,1)S(1)}, u32[]{:S(2)}, u32[]{:S(2)}) collective-permute-start(bf16[144,256]{1,0:T(8,128)(2,1)S(1)} %get-tuple-element.15.refs_0_.refs_5_), channel_id=1, source_target_pairs={{0,8},{1,9},{2,10},{3,11},{4,12},{5,13},{6,14},{7,15},{8,0},{9,1},... | collective-permute-start | bytes 221192 | tf_op jit(solution)/shard_map/ppermute | solution.py:354
  6.7 6.2 %collective-permute-start.4 = (bf16[144,256]{1,0:T(8,128)(2,1)S(1)}, bf16[144,256]{1,0:T(8,128)(2,1)S(1)}, u32[]{:S(2)}, u32[]{:S(2)}) collective-permute-start(bf16[144,256]{1,0:T(8,128)(2,1)S(1)} %get-tuple-element.15.refs_0_.refs_5_), channel_id=1, source_target_pairs={{0,4},{1,5},{2,6},{3,7},{4,0},{5,1},{6,2},{7,3},{8,12},{9,13},{10,... | collective-permute-start | bytes 221192 | tf_op jit(solution)/shard_map/ppermute | solution.py:354
  13.0 9.2 %collective-permute-start.6 = (bf16[432,256]{1,0:T(8,128)(2,1)S(1)}, bf16[432,256]{1,0:T(8,128)(2,1)S(1)}, u32[]{:S(2)}, u32[]{:S(2)}) collective-permute-start(bf16[432,256]{1,0:T(8,128)(2,1)S(1)} %pad_maximum_fusion.2), channel_id=1, source_target_pairs={{0,2},{1,3},{2,0},{3,1},{4,6},{5,7},{6,4},{7,5},{8,10},{9,11},{10,... | collective-permute-start | bytes 663560 | tf_op jit(solution)/shard_map/ppermute | solution.py:354
  14.5 7.5 %collective-permute-start.5 = (bf16[144,256]{1,0:T(8,128)(2,1)S(1)}, bf16[144,256]{1,0:T(8,128)(2,1)S(1)}, u32[]{:S(2)}, u32[]{:S(2)}) collective-permute-start(bf16[144,256]{1,0:T(8,128)(2,1)S(1)} %get-tuple-element.15.refs_0_.refs_5_), channel_id=1, source_target_pairs={{0,2},{1,3},{2,0},{3,1},{4,6},{5,7},{6,4},{7,5},{8,10},{9,11},{10,... | collective-permute-start | bytes 221192 | tf_op jit(solution)/shard_map/ppermute | solution.py:354
  15.0 7.6 %collective-permute-start = (bf16[128,256]{1,0:T(8,128)(2,1)}, bf16[128,256]{1,0:T(8,128)(2,1)S(1)}, u32[]{:S(2)}, u32[]{:S(2)}) collective-permute-start(bf16[128,256]{1,0:T(8,128)(2,1)} %own_ref.3), channel_id=1, source_target_pairs={{0,15},{1,2},{2,1},{3,4},{4,3},{5,6},{6,5},{7,8},{8,7},{9,10},{10,... | collective-permute-start | bytes 196616 | tf_op jit(solution)/shard_map/ppermute | solution.py:395
  16.3 6.3 %collective-permute-start.1 = (bf16[144,256]{1,0:T(8,128)(2,1)S(1)}, bf16[144,256]{1,0:T(8,128)(2,1)S(1)}, u32[]{:S(2)}, u32[]{:S(2)}) collective-permute-start(bf16[144,256]{1,0:T(8,128)(2,1)S(1)} %get-tuple-element.15.refs_0_.refs_5_), channel_id=1, source_target_pairs={{0,1},{1,0},{2,3},{3,2},{4,5},{5,4},{6,7},{7,6},{8,9},{9,8},{10,11... | collective-permute-start | bytes 221192 | tf_op jit(solution)/shard_map/ppermute | solution.py:354
  22.1 6.9 %collective-permute-start.7 = (bf16[576,256]{1,0:T(8,128)(2,1)S(1)}, bf16[576,256]{1,0:T(8,128)(2,1)S(1)}, u32[]{:S(2)}, u32[]{:S(2)}) collective-permute-start(bf16[576,256]{1,0:T(8,128)(2,1)S(1)} %pad_maximum_fusion), channel_id=1, source_target_pairs={{0,1},{1,0},{2,3},{3,2},{4,5},{5,4},{6,7},{7,6},{8,9},{9,8},{10,11... | collective-permute-start | bytes 884744 | tf_op jit(solution)/shard_map/ppermute | solution.py:354
  22.2 8.1 %collective-permute-start.8 = (bf16[432,256]{1,0:T(8,128)(2,1)S(1)}, bf16[432,256]{1,0:T(8,128)(2,1)S(1)}, u32[]{:S(2)}, u32[]{:S(2)}) collective-permute-start(bf16[432,256]{1,0:T(8,128)(2,1)S(1)} %collective-permute-done.6.refs_0_.refs_11_), channel_id=1, source_target_pairs={{0,1},{1,0},{2,3},{3,2},{4,5},{5,4},{6,7},{7,6},{8,9},{9,8},{10,11... | collective-permute-start | bytes 663560 | tf_op jit(solution)/shard_map/ppermute | solution.py:354
  27.7 3.5 %copy-start.2 = (bf16[2,256,256]{2,1,0:T(8,128)(2,1)S(1)}, bf16[2,256,256]{2,1,0:T(8,128)(2,1)}, u32[]{:S(2)}) copy-start(bf16[2,256,256]{2,1,0:T(8,128)(2,1)} %mixing_ref.3) | copy-start | bytes 786436
  27.7 3.5 %copy-start.3 = (bf16[2,256,256]{2,1,0:T(8,128)(2,1)S(1)}, bf16[2,256,256]{2,1,0:T(8,128)(2,1)}, u32[]{:S(2)}) copy-start(bf16[2,256,256]{2,1,0:T(8,128)(2,1)} %long_ref.3) | copy-start | bytes 786436
  27.7 3.5 %copy-start.4 = (bf16[2,256,256]{2,1,0:T(8,128)(2,1)S(1)}, bf16[2,256,256]{2,1,0:T(8,128)(2,1)}, u32[]{:S(2)}) copy-start(bf16[2,256,256]{2,1,0:T(8,128)(2,1)} %short_ref.1) | copy-start | bytes 786436
  30.2 13.2 %copy-start = (bf16[2,512,256]{2,1,0:T(8,128)(2,1)S(1)}, bf16[2,512,256]{2,1,0:T(8,128)(2,1)}, u32[]{:S(2)}) copy-start(bf16[2,512,256]{2,1,0:T(8,128)(2,1)} %filter_ref.5) | copy-start | bytes 1572868
  30.2 13.2 %copy-start.1 = (bf16[2,64,512]{2,1,0:T(8,128)(2,1)S(1)}, bf16[2,64,512]{2,1,0:T(8,128)(2,1)}, u32[]{:S(2)}) copy-start(bf16[2,64,512]{2,1,0:T(8,128)(2,1)} %rbf_ref.5) | copy-start | bytes 393220
  30.3 13.2 %copy-start.6 = (f32[64,128]{1,0:T(8,128)S(1)}, f32[64,128]{1,0:T(8,128)}, u32[]{:S(2)}) copy-start(f32[64,128]{1,0:T(8,128)} %distance_ref.5) | copy-start | bytes 98308
  32.1 6.8 %collective-permute-start.11 = (bf16[128,256]{1,0:T(8,128)(2,1)S(1)}, bf16[128,256]{1,0:T(8,128)(2,1)S(1)}, u32[]{:S(2)}, u32[]{:S(2)}) collective-permute-start(bf16[128,256]{1,0:T(8,128)(2,1)S(1)} %update.2.refs_3_.own_ref), channel_id=1, source_target_pairs={{0,12},{1,13},{2,14},{3,15},{4,8},{5,9},{6,10},{7,11},{8,4},{9,5},... | collective-permute-start | bytes 196616 | tf_op jit(solution)/shard_map/ppermute | solution.py:354
  34.1 6.8 %collective-permute-start.12 = (bf16[128,256]{1,0:T(8,128)(2,1)S(1)}, bf16[128,256]{1,0:T(8,128)(2,1)S(1)}, u32[]{:S(2)}, u32[]{:S(2)}) collective-permute-start(bf16[128,256]{1,0:T(8,128)(2,1)S(1)} %update.2.refs_3_.own_ref), channel_id=1, source_target_pairs={{0,8},{1,9},{2,10},{3,11},{4,12},{5,13},{6,14},{7,15},{8,0},{9,1},... | collective-permute-start | bytes 196616 | tf_op jit(solution)/shard_map/ppermute | solution.py:354
  34.1 6.8 %collective-permute-start.13 = (bf16[128,256]{1,0:T(8,128)(2,1)S(1)}, bf16[128,256]{1,0:T(8,128)(2,1)S(1)}, u32[]{:S(2)}, u32[]{:S(2)}) collective-permute-start(bf16[128,256]{1,0:T(8,128)(2,1)S(1)} %update.2.refs_3_.own_ref), channel_id=1, source_target_pairs={{0,4},{1,5},{2,6},{3,7},{4,0},{5,1},{6,2},{7,3},{8,12},{9,13},{10,... | collective-permute-start | bytes 196616 | tf_op jit(solution)/shard_map/ppermute | solution.py:354
  40.9 9.5 %collective-permute-start.15 = (bf16[384,256]{1,0:T(8,128)(2,1)S(1)}, bf16[384,256]{1,0:T(8,128)(2,1)S(1)}, u32[]{:S(2)}, u32[]{:S(2)}) collective-permute-start(bf16[384,256]{1,0:T(8,128)(2,1)S(1)} %pad_maximum_fusion.5), channel_id=1, source_target_pairs={{0,2},{1,3},{2,0},{3,1},{4,6},{5,7},{6,4},{7,5},{8,10},{9,11},{10,... | collective-permute-start | bytes 589832 | tf_op jit(solution)/shard_map/ppermute | solution.py:354
  43.4 6.9 %collective-permute-start.14 = (bf16[128,256]{1,0:T(8,128)(2,1)S(1)}, bf16[128,256]{1,0:T(8,128)(2,1)S(1)}, u32[]{:S(2)}, u32[]{:S(2)}) collective-permute-start(bf16[128,256]{1,0:T(8,128)(2,1)S(1)} %update.2.refs_3_.own_ref), channel_id=1, source_target_pairs={{0,2},{1,3},{2,0},{3,1},{4,6},{5,7},{6,4},{7,5},{8,10},{9,11},{10,... | collective-permute-start | bytes 196616 | tf_op jit(solution)/shard_map/ppermute | solution.py:354
  46.0 6.5 %collective-permute-start.9 = (bf16[128,256]{1,0:T(8,128)(2,1)S(1)}, bf16[128,256]{1,0:T(8,128)(2,1)S(1)}, u32[]{:S(2)}, u32[]{:S(2)}) collective-permute-start(bf16[128,256]{1,0:T(8,128)(2,1)S(1)} %update.2.refs_3_.own_ref), channel_id=1, source_target_pairs={{0,15},{1,2},{2,1},{3,4},{4,3},{5,6},{6,5},{7,8},{8,7},{9,10},{10,... | collective-permute-start | bytes 196616 | tf_op jit(solution)/shard_map/ppermute | solution.py:395
  48.2 4.3 %collective-permute-start.10 = (bf16[128,256]{1,0:T(8,128)(2,1)S(1)}, bf16[128,256]{1,0:T(8,128)(2,1)S(1)}, u32[]{:S(2)}, u32[]{:S(2)}) collective-permute-start(bf16[128,256]{1,0:T(8,128)(2,1)S(1)} %update.2.refs_3_.own_ref), channel_id=1, source_target_pairs={{0,1},{1,0},{2,3},{3,2},{4,5},{5,4},{6,7},{7,6},{8,9},{9,8},{10,11... | collective-permute-start | bytes 196616 | tf_op jit(solution)/shard_map/ppermute | solution.py:354
  50.3 7.2 %collective-permute-start.16 = (bf16[512,256]{1,0:T(8,128)(2,1)S(1)}, bf16[512,256]{1,0:T(8,128)(2,1)S(1)}, u32[]{:S(2)}, u32[]{:S(2)}) collective-permute-start(bf16[512,256]{1,0:T(8,128)(2,1)S(1)} %pad_maximum_fusion.1), channel_id=1, source_target_pairs={{0,1},{1,0},{2,3},{3,2},{4,5},{5,4},{6,7},{7,6},{8,9},{9,8},{10,11... | collective-permute-start | bytes 786440 | tf_op jit(solution)/shard_map/ppermute | solution.py:354
  50.4 7.5 %collective-permute-start.17 = (bf16[384,256]{1,0:T(8,128)(2,1)S(1)}, bf16[384,256]{1,0:T(8,128)(2,1)S(1)}, u32[]{:S(2)}, u32[]{:S(2)}) collective-permute-start(bf16[384,256]{1,0:T(8,128)(2,1)S(1)} %collective-permute-done.15.refs_9_), channel_id=1, source_target_pairs={{0,1},{1,0},{2,3},{3,2},{4,5},{5,4},{6,7},{7,6},{8,9},{9,8},{10,11... | collective-permute-start | bytes 589832 | tf_op jit(solution)/shard_map/ppermute | solution.py:354

commit v3 on v2

--- a/solution.py
+++ b/solution.py
@@ -150,6 +150,7 @@
     packed, out_ref, right_ref, part_ref = refs[:count], refs[count], refs[count + 1], refs[count + 2]
     tile = 32
     for pair in range(0, len(places), 2):
+        turn = pair // 2 % 2
         span = min(2, len(places) - pair)
         heights = []
         for side in range(span):
@@ -158,12 +159,12 @@
             position = (block[0:3, :rows] + block[0:3, rows : 2 * rows]) + block[3:6, :rows]
             cosine, sine = plane_phases(position)
             at = slice(side * rows, (side + 1) * rows)
-            right_ref[:plane, at] = cosine.astype(BF)
-            right_ref[plane:, at] = sine.astype(BF)
+            right_ref[turn, :plane, at] = cosine.astype(BF)
+            right_ref[turn, plane:, at] = sine.astype(BF)
             heights.append(turn_trig(position[2:3]))
         wide = span * rows
         for m in range(2 * reach + 1):
-            part_ref[m, :, :wide] = dot(left_ref[m], right_ref[:, :wide])
+            part_ref[turn, m, :, :wide] = dot(left_ref[m], right_ref[turn, :, :wide])
         for side in range(span):
             zc, zs = heights[side]
             at = slice(side * rows, (side + 1) * rows)
@@ -173,12 +174,12 @@
                 c1 = oc * zc + os * zs
                 s1 = os * zc - oc * zs
                 twice = c1 + c1
-                even, odd = part_ref[reach, own, at], part_ref[2 * reach, own, at]
+                even, odd = part_ref[turn, reach, own, at], part_ref[turn, 2 * reach, own, at]
                 even_last, odd_last = 0.0, 0.0
                 for m in range(reach - 1, 0, -1):
-                    even, even_last = part_ref[m, own, at] + twice * even - even_last, even
-                    odd, odd_last = part_ref[reach + m, own, at] + twice * odd - odd_last, odd
-                total = part_ref[0, own, at] + c1 * even - even_last + s1 * odd
+                    even, even_last = part_ref[turn, m, own, at] + twice * even - even_last, even
+                    odd, odd_last = part_ref[turn, reach + m, own, at] + twice * odd - odd_last, odd
+                total = part_ref[turn, 0, own, at] + c1 * even - even_last + s1 * odd
                 out_ref[own, pair * rows + side * rows : pair * rows + (side + 1) * rows] = total.astype(BF)
 
 
@@ -188,8 +189,8 @@
         functools.partial(coupling_kernel, tuple(places), rows),
         out_shape=jax.ShapeDtypeStruct((rows, len(places) * rows), BF),
         scratch_shapes=[
-            pltpu.VMEM((2 * plane, 2 * rows), BF),
-            pltpu.VMEM((2 * reach + 1, rows, 2 * rows), F32),
+            pltpu.VMEM((2, 2 * plane, 2 * rows), BF),
+            pltpu.VMEM((2, 2 * reach + 1, rows, 2 * rows), F32),
         ],
         in_specs=[pl.BlockSpec(memory_space=pltpu.VMEM)] * (3 + len(arrays)),
         out_specs=pl.BlockSpec(memory_space=pltpu.VMEM),

time: 59.1 us -> 59.1 us (level)
  no operation moved by 1% of the time
where the time goes in v3:
time: 59.1 us; the launch traced here: 58.9 us
  Pallas kernels  22.2 us (38%)
  starting transfers between devices  19.8 us (34%)
  waiting for transfers between devices  16.4 us (28%)
    ppermute x16, starting transfers between devices, swap(): lax.ppermute(x, 'atom', [(i, i ^ (odd if i % 2 else even)) for i in range...  16.3 us
    ppermute x16, waiting for transfers between devices, swap(): lax.ppermute(x, 'atom', [(i, i ^ (odd if i % 2 else even)) for i in range...  14.8 us
    pallas_call x2, Pallas kernels, messages(): pl.pallas_call(functools.partial(message_kernel, layer), out_shape=jax.Sh...  9.83 us
    pallas_call x2, Pallas kernels, filters_of(): pl.pallas_call(functools.partial(filter_kernel, layer), out_shape=jax.Sha...  5.1 us
    ppermute x2, starting transfers between devices, neighbour_table(): lax.ppermute(own, 'atom', [(i, (i + (count - 1 if i % 2 == 0 else 1)) % c...  3.49 us
    pallas_call x3, Pallas kernels, coupling(): pl.pallas_call(functools.partial(coupling_kernel, tuple(places), rows), o...  3.31 us
    pallas_call x2, Pallas kernels, update(): pl.pallas_call(functools.partial(update_kernel, tuple(places), len(matric...  2.08 us
    ppermute x2, waiting for transfers between devices, neighbour_table(): lax.ppermute(own, 'atom', [(i, (i + (count - 1 if i % 2 == 0 else 1)) % c...  1.61 us
  transfers between devices with their start and end apart: 18, of which 7 were waited for; matrix products, arithmetic and copies ran while one was open for 0% of the time, Pallas kernels for 30%

profile of v3, /device:TPU:0, one launch (start us, length us, event | category | flops | bytes accessed | tf_op | source)
XLA Modules:
  0.0 58.9 jit_solution(863774682323896130)
XLA Ops:
  0.0 1.5 %prepare.1 = (bf16[144,256]{1,0:T(8,128)(2,1)S(1)}, bf16[13,128,256]{2,1,0:T(8,128)(2,1)S(1)}, f32[128,128]{1,0:T(8,128)S(1)}, f32[128,128]{1,0:T(8,128)S(1)}, f...) custom-call(s32[3,2048]{1,0:T(4,128)} %wave_ref.1, f32[3,128]{1,0:T(4,128)} %position_ref.1, ...), custom_call_target="tpu_custom_call" | custom-call | tf_op jit(solution)/shard_map/prepare/pallas_call | solution.py:137
  1.5 0.0 copy-start.7
  1.6 0.0 copy-start.8
  1.6 5.1 %collective-permute-start.2 = (bf16[144,256]{1,0:T(8,128)(2,1)S(1)}, bf16[144,256]{1,0:T(8,128)(2,1)S(1)}, u32[]{:S(2)}, u32[]{:S(2)}) collective-permute-start(bf16[144,256]{1,0:T(8,128)(2,1)S(1)} %get-tuple-element.15.refs_0_.refs_5_), channel_id=1, source_target_pairs={{0,12},{1,13},{2,14},{3,15},{4,8},{5,9},{6,10},{7,11},{8,4},{9,5},... | collective-permute-start | bytes 221192 | tf_op jit(solution)/shard_map/ppermute | solution.py:355
  6.7 0.0 collective-permute-start.3
  6.7 0.6 %collective-permute-start.4 = (bf16[144,256]{1,0:T(8,128)(2,1)S(1)}, bf16[144,256]{1,0:T(8,128)(2,1)S(1)}, u32[]{:S(2)}, u32[]{:S(2)}) collective-permute-start(bf16[144,256]{1,0:T(8,128)(2,1)S(1)} %get-tuple-element.15.refs_0_.refs_5_), channel_id=1, source_target_pairs={{0,4},{1,5},{2,6},{3,7},{4,0},{5,1},{6,2},{7,3},{8,12},{9,13},{10,... | collective-permute-start | bytes 221192 | tf_op jit(solution)/shard_map/ppermute | solution.py:355
  7.4 2.0 %collective-permute-done.2.refs_1_.refs_6_ = bf16[144,256]{1,0:T(8,128)(2,1)S(1)} collective-permute-done((bf16[144,256]{1,0:T(8,128)(2,1)S(1)}, bf16[144,256]{1,0:T(8,128)(2,1)S(1)}, u32[]{:S(2)}, u32[]{:S(2)}) %collective-permute-start.2) | collective-permute-done | bytes 73760 | tf_op jit(solution)/shard_map/ppermute | solution.py:355
  9.4 3.5 %collective-permute-done.3.refs_2_.refs_7_ = bf16[144,256]{1,0:T(8,128)(2,1)S(1)} collective-permute-done((bf16[144,256]{1,0:T(8,128)(2,1)S(1)}, bf16[144,256]{1,0:T(8,128)(2,1)S(1)}, u32[]{:S(2)}, u32[]{:S(2)}) %collective-permute-start.3) | collective-permute-done | bytes 73760 | tf_op jit(solution)/shard_map/ppermute | solution.py:355
  12.9 0.0 collective-permute-done.4.refs_3_.refs_8_
  13.0 1.6 %collective-permute-start.6 = (bf16[432,256]{1,0:T(8,128)(2,1)S(1)}, bf16[432,256]{1,0:T(8,128)(2,1)S(1)}, u32[]{:S(2)}, u32[]{:S(2)}) collective-permute-start(bf16[432,256]{1,0:T(8,128)(2,1)S(1)} %pad_maximum_fusion.2), channel_id=1, source_target_pairs={{0,2},{1,3},{2,0},{3,1},{4,6},{5,7},{6,4},{7,5},{8,10},{9,11},{10,... | collective-permute-start | bytes 663560 | tf_op jit(solution)/shard_map/ppermute | solution.py:355
  14.5 0.5 collective-permute-start.5
  15.0 1.3 %collective-permute-start = (bf16[128,256]{1,0:T(8,128)(2,1)}, bf16[128,256]{1,0:T(8,128)(2,1)S(1)}, u32[]{:S(2)}, u32[]{:S(2)}) collective-permute-start(bf16[128,256]{1,0:T(8,128)(2,1)} %own_ref.3), channel_id=1, source_target_pairs={{0,15},{1,2},{2,1},{3,4},{4,3},{5,6},{6,5},{7,8},{8,7},{9,10},{10,... | collective-permute-start | bytes 196616 | tf_op jit(solution)/shard_map/ppermute | solution.py:396
  16.3 0.4 collective-permute-start.1
  16.7 2.5 %filters.2.ready_ref = bf16[32,128,256]{2,1,0:T(8,128)(2,1)S(1)} custom-call(f32[64,128]{1,0:T(8,128)S(1)} %get-tuple-element.14.distance_ref, bf16[1,64,512]{2,1,0:T(8,128)(2,1)S(1)} %get-tuple-element.16.rbf_ref, bf16[1,512,256]{2,1,0:T(8,128)(2,1)S(1)} %get-tuple-element.17.filter_ref), custom_call_target="tpu_custom_call" | custom-call | tf_op jit(solution)/shard_map/filters/pallas_call | solution.py:235
  19.2 2.8 %collective-permute-done.5.refs_4_.refs_9_ = bf16[144,256]{1,0:T(8,128)(2,1)S(1)} collective-permute-done((bf16[144,256]{1,0:T(8,128)(2,1)S(1)}, bf16[144,256]{1,0:T(8,128)(2,1)S(1)}, u32[]{:S(2)}, u32[]{:S(2)}) %collective-permute-start.5) | collective-permute-done | bytes 73760 | tf_op jit(solution)/shard_map/ppermute | solution.py:355
  22.1 0.1 collective-permute-start.7
  22.2 0.0 collective-permute-done.6.refs_0_.refs_11_
  22.2 0.5 collective-permute-start.8
  22.7 0.0 collective-permute-done
  22.7 0.0 collective-permute-done.1.refs_5_.refs_10_
  22.7 0.0 copy-done.5
  22.7 0.0 copy-done.7
  22.7 0.0 copy-done.8
  22.7 4.9 %messages.2.refs_0_ = bf16[128,256]{1,0:T(8,128)(2,1)S(1)} custom-call(s32[64,128]{1,0:T(8,128)S(1)} %copy-done.7, f32[64,128]{1,0:T(8,128)S(1)} %get-tuple-element.14.distance_ref, s32[64,128]{1,0:T(8,128)S(1)} %copy-done.8, bf16[384,256]{1,0:T(8,128)(2,1)S(1)} %pad_maximum_fusion.3.table_ref, bf16[1,64,512]{2,1,0:T(8,128)(2,1)S(1)} %get-tuple-element.16.rbf_ref, ...), custom_call_target="tpu_custom_call" | custom-call | tf_op jit(solution)/shard_map/messages/pallas_call | solution.py:282
  27.7 0.0 copy-start.2
  27.7 0.0 copy-start.3
  27.7 0.0 copy-start.4
  27.7 1.2 %coupling.3.refs_2_.refs_0_ = bf16[128,768]{1,0:T(8,128)(2,1)S(1)} custom-call(bf16[13,128,256]{2,1,0:T(8,128)(2,1)S(1)} %get-tuple-element.18.left_ref, f32[128,128]{1,0:T(8,128)S(1)} %get-tuple-element.19.zc_ref, f32[128,128]{1,0:T(8,128)S(1)} %get-tuple-element.20.zs_ref, bf16[144,256]{1,0:T(8,128)(2,1)S(1)} %get-tuple-element.15.refs_0_.refs_5_, ...), custom_call_target="tpu_custom_call" | custom-call | tf_op jit(solution)/shard_map/coupling/pallas_call | solution.py:188
  28.9 0.0 collective-permute-done.7.refs_1_.refs_0_.refs_12_
  28.9 1.2 %coupling.4.refs_3_.refs_1_ = bf16[128,768]{1,0:T(8,128)(2,1)S(1)} custom-call(bf16[13,128,256]{2,1,0:T(8,128)(2,1)S(1)} %get-tuple-element.18.left_ref, f32[128,128]{1,0:T(8,128)S(1)} %get-tuple-element.19.zc_ref, f32[128,128]{1,0:T(8,128)S(1)} %get-tuple-element.20.zs_ref, bf16[432,256]{1,0:T(8,128)(2,1)S(1)} %collective-permute-done.6.refs_0_.refs_11_, ...), custom_call_target="tpu_custom_call" | custom-call | tf_op jit(solution)/shard_map/coupling/pallas_call | solution.py:188
  30.2 0.0 copy-start
  30.2 0.0 copy-start.1
  30.2 0.0 copy-start.6
  30.2 0.0 collective-permute-done.8.refs_1_.refs_13_
  30.2 0.8 %coupling.5.refs_4_.refs_2_ = bf16[128,512]{1,0:T(8,128)(2,1)S(1)} custom-call(bf16[13,128,256]{2,1,0:T(8,128)(2,1)S(1)} %get-tuple-element.18.left_ref, f32[128,128]{1,0:T(8,128)S(1)} %get-tuple-element.19.zc_ref, f32[128,128]{1,0:T(8,128)S(1)} %get-tuple-element.20.zs_ref, bf16[576,256]{1,0:T(8,128)(2,1)S(1)} %collective-permute-done.7.refs_1_.refs_0_.refs_12_, ...), custom_call_target="tpu_custom_call" | custom-call | tf_op jit(solution)/shard_map/coupling/pallas_call | solution.py:188
  31.1 0.0 copy-done.2
  31.1 0.0 copy-done.3
  31.1 0.0 copy-done.4
  31.1 1.0 %update.2.refs_3_.own_ref = bf16[128,256]{1,0:T(8,128)(2,1)S(1)} custom-call(bf16[128,256]{1,0:T(8,128)(2,1)S(1)} %copy-done.5, bf16[2,256,256]{2,1,0:T(8,128)(2,1)S(1)} %copy-done.2, bf16[2,256,256]{2,1,0:T(8,128)(2,1)S(1)} %copy-done.3, bf16[128,256]{1,0:T(8,128)(2,1)S(1)} %messages.2.refs_0_, bf16[2,256,256]{2,1,0:T(8,128)(2,1)S(1)} %copy-done.4, ...), custom_call_target="tpu_custom_call" | custom-call | tf_op jit(solution)/shard_map/update/pallas_call | solution.py:336
  32.1 1.9 %collective-permute-start.11 = (bf16[128,256]{1,0:T(8,128)(2,1)S(1)}, bf16[128,256]{1,0:T(8,128)(2,1)S(1)}, u32[]{:S(2)}, u32[]{:S(2)}) collective-permute-start(bf16[128,256]{1,0:T(8,128)(2,1)S(1)} %update.2.refs_3_.own_ref), channel_id=1, source_target_pairs={{0,12},{1,13},{2,14},{3,15},{4,8},{5,9},{6,10},{7,11},{8,4},{9,5},... | collective-permute-start | bytes 196616 | tf_op jit(solution)/shard_map/ppermute | solution.py:355
  34.0 0.0 collective-permute-start.12
  34.0 2.5 %collective-permute-start.13 = (bf16[128,256]{1,0:T(8,128)(2,1)S(1)}, bf16[128,256]{1,0:T(8,128)(2,1)S(1)}, u32[]{:S(2)}, u32[]{:S(2)}) collective-permute-start(bf16[128,256]{1,0:T(8,128)(2,1)S(1)} %update.2.refs_3_.own_ref), channel_id=1, source_target_pairs={{0,4},{1,5},{2,6},{3,7},{4,0},{5,1},{6,2},{7,3},{8,12},{9,13},{10,... | collective-permute-start | bytes 196616 | tf_op jit(solution)/shard_map/ppermute | solution.py:355
  36.5 2.4 %collective-permute-done.11.refs_4_ = bf16[128,256]{1,0:T(8,128)(2,1)S(1)} collective-permute-done((bf16[128,256]{1,0:T(8,128)(2,1)S(1)}, bf16[128,256]{1,0:T(8,128)(2,1)S(1)}, u32[]{:S(2)}, u32[]{:S(2)}) %collective-permute-start.11) | collective-permute-done | bytes 65568 | tf_op jit(solution)/shard_map/ppermute | solution.py:355
  38.9 2.0 %collective-permute-done.12.refs_5_ = bf16[128,256]{1,0:T(8,128)(2,1)S(1)} collective-permute-done((bf16[128,256]{1,0:T(8,128)(2,1)S(1)}, bf16[128,256]{1,0:T(8,128)(2,1)S(1)}, u32[]{:S(2)}, u32[]{:S(2)}) %collective-permute-start.12) | collective-permute-done | bytes 65568 | tf_op jit(solution)/shard_map/ppermute | solution.py:355
  40.9 0.0 collective-permute-done.13.refs_6_
  40.9 2.5 %collective-permute-start.15 = (bf16[384,256]{1,0:T(8,128)(2,1)S(1)}, bf16[384,256]{1,0:T(8,128)(2,1)S(1)}, u32[]{:S(2)}, u32[]{:S(2)}) collective-permute-start(bf16[384,256]{1,0:T(8,128)(2,1)S(1)} %pad_maximum_fusion.5), channel_id=1, source_target_pairs={{0,2},{1,3},{2,0},{3,1},{4,6},{5,7},{6,4},{7,5},{8,10},{9,11},{10,... | collective-permute-start | bytes 589832 | tf_op jit(solution)/shard_map/ppermute | solution.py:355
  43.3 0.1 collective-permute-start.14
  43.4 0.0 copy-done
  43.4 0.0 copy-done.1
  43.4 0.0 copy-done.6
  43.4 2.5 %filters.3.ready_ref = bf16[32,128,256]{2,1,0:T(8,128)(2,1)S(1)} custom-call(f32[64,128]{1,0:T(8,128)S(1)} %copy-done.6, bf16[2,64,512]{2,1,0:T(8,128)(2,1)S(1)} %copy-done.1, bf16[2,512,256]{2,1,0:T(8,128)(2,1)S(1)} %copy-done), custom_call_target="tpu_custom_call" | custom-call | tf_op jit(solution)/shard_map/filters/pallas_call | solution.py:235
  46.0 2.2 %collective-permute-start.9 = (bf16[128,256]{1,0:T(8,128)(2,1)S(1)}, bf16[128,256]{1,0:T(8,128)(2,1)S(1)}, u32[]{:S(2)}, u32[]{:S(2)}) collective-permute-start(bf16[128,256]{1,0:T(8,128)(2,1)S(1)} %update.2.refs_3_.own_ref), channel_id=1, source_target_pairs={{0,15},{1,2},{2,1},{3,4},{4,3},{5,6},{6,5},{7,8},{8,7},{9,10},{10,... | collective-permute-start | bytes 196616 | tf_op jit(solution)/shard_map/ppermute | solution.py:396
  48.2 0.0 collective-permute-start.10
  48.2 2.0 %collective-permute-done.14.refs_7_ = bf16[128,256]{1,0:T(8,128)(2,1)S(1)} collective-permute-done((bf16[128,256]{1,0:T(8,128)(2,1)S(1)}, bf16[128,256]{1,0:T(8,128)(2,1)S(1)}, u32[]{:S(2)}, u32[]{:S(2)}) %collective-permute-start.14) | collective-permute-done | bytes 65568 | tf_op jit(solution)/shard_map/ppermute | solution.py:355
  50.2 0.1 collective-permute-start.16
  50.3 0.0 collective-permute-done.15.refs_9_
  50.3 0.5 collective-permute-start.17
  50.8 1.6 %collective-permute-done.9 = bf16[128,256]{1,0:T(8,128)(2,1)S(1)} collective-permute-done((bf16[128,256]{1,0:T(8,128)(2,1)S(1)}, bf16[128,256]{1,0:T(8,128)(2,1)S(1)}, u32[]{:S(2)}, u32[]{:S(2)}) %collective-permute-start.9) | collective-permute-done | bytes 65568 | tf_op jit(solution)/shard_map/ppermute | solution.py:396
  52.4 0.0 collective-permute-done.10.refs_8_
  52.5 4.9 %messages.3.message_ref = bf16[128,256]{1,0:T(8,128)(2,1)S(1)} custom-call(s32[64,128]{1,0:T(8,128)S(1)} %copy-done.7, f32[64,128]{1,0:T(8,128)S(1)} %copy-done.6, s32[64,128]{1,0:T(8,128)S(1)} %copy-done.8, bf16[384,256]{1,0:T(8,128)(2,1)S(1)} %pad_maximum_fusion.4.table_ref, bf16[2,64,512]{2,1,0:T(8,128)(2,1)S(1)} %copy-done.1, ...), custom_call_target="tpu_custom_call" | custom-call | tf_op jit(solution)/shard_map/messages/pallas_call | solution.py:282
  57.4 0.0 collective-permute-done.16.refs_10_
  57.4 0.4 partial.1
  57.8 0.0 collective-permute-done.17.refs_3_
  57.8 1.1 %update.3 = bf16[128,256]{1,0:T(8,128)(2,1)} custom-call(bf16[128,256]{1,0:T(8,128)(2,1)S(1)} %update.2.refs_3_.own_ref, bf16[2,256,256]{2,1,0:T(8,128)(2,1)S(1)} %copy-done.2, bf16[2,256,256]{2,1,0:T(8,128)(2,1)S(1)} %copy-done.3, f32[128,256]{1,0:T(8,128)S(1)} %get-tuple-element.21.refs_0_, f32[128,256]{1,0:T(8,128)S(1)} %get-tuple-element.22.refs_1_, ...), custom_call_target="tpu_custom_call" | custom-call | tf_op jit(solution)/shard_map/update/pallas_call | solution.py:336
  (9 shorter events, 0.1 us)
Async XLA Ops:
  0.0 22.7 %copy-start.5 = (bf16[128,256]{1,0:T(8,128)(2,1)S(1)}, bf16[128,256]{1,0:T(8,128)(2,1)}, u32[]{:S(2)}) copy-start(bf16[128,256]{1,0:T(8,128)(2,1)} %own_ref.3) | copy-start | bytes 196612
  1.5 21.2 %copy-start.7 = (s32[64,128]{1,0:T(8,128)S(1)}, s32[64,128]{1,0:T(8,128)}, u32[]{:S(2)}) copy-start(s32[64,128]{1,0:T(8,128)} %index_ref.3) | copy-start | bytes 98308
  1.6 21.2 %copy-start.8 = (s32[64,128]{1,0:T(8,128)S(1)}, s32[64,128]{1,0:T(8,128)}, u32[]{:S(2)}) copy-start(s32[64,128]{1,0:T(8,128)} %mask_ref.3) | copy-start | bytes 98308
  1.6 7.8 %collective-permute-start.2 = (bf16[144,256]{1,0:T(8,128)(2,1)S(1)}, bf16[144,256]{1,0:T(8,128)(2,1)S(1)}, u32[]{:S(2)}, u32[]{:S(2)}) collective-permute-start(bf16[144,256]{1,0:T(8,128)(2,1)S(1)} %get-tuple-element.15.refs_0_.refs_5_), channel_id=1, source_target_pairs={{0,12},{1,13},{2,14},{3,15},{4,8},{5,9},{6,10},{7,11},{8,4},{9,5},... | collective-permute-start | bytes 221192 | tf_op jit(solution)/shard_map/ppermute | solution.py:355
  6.7 6.2 %collective-permute-start.3 = (bf16[144,256]{1,0:T(8,128)(2,1)S(1)}, bf16[144,256]{1,0:T(8,128)(2,1)S(1)}, u32[]{:S(2)}, u32[]{:S(2)}) collective-permute-start(bf16[144,256]{1,0:T(8,128)(2,1)S(1)} %get-tuple-element.15.refs_0_.refs_5_), channel_id=1, source_target_pairs={{0,8},{1,9},{2,10},{3,11},{4,12},{5,13},{6,14},{7,15},{8,0},{9,1},... | collective-permute-start | bytes 221192 | tf_op jit(solution)/shard_map/ppermute | solution.py:355
  6.7 6.2 %collective-permute-start.4 = (bf16[144,256]{1,0:T(8,128)(2,1)S(1)}, bf16[144,256]{1,0:T(8,128)(2,1)S(1)}, u32[]{:S(2)}, u32[]{:S(2)}) collective-permute-start(bf16[144,256]{1,0:T(8,128)(2,1)S(1)} %get-tuple-element.15.refs_0_.refs_5_), channel_id=1, source_target_pairs={{0,4},{1,5},{2,6},{3,7},{4,0},{5,1},{6,2},{7,3},{8,12},{9,13},{10,... | collective-permute-start | bytes 221192 | tf_op jit(solution)/shard_map/ppermute | solution.py:355
  13.0 9.2 %collective-permute-start.6 = (bf16[432,256]{1,0:T(8,128)(2,1)S(1)}, bf16[432,256]{1,0:T(8,128)(2,1)S(1)}, u32[]{:S(2)}, u32[]{:S(2)}) collective-permute-start(bf16[432,256]{1,0:T(8,128)(2,1)S(1)} %pad_maximum_fusion.2), channel_id=1, source_target_pairs={{0,2},{1,3},{2,0},{3,1},{4,6},{5,7},{6,4},{7,5},{8,10},{9,11},{10,... | collective-permute-start | bytes 663560 | tf_op jit(solution)/shard_map/ppermute | solution.py:355
  14.5 7.5 %collective-permute-start.5 = (bf16[144,256]{1,0:T(8,128)(2,1)S(1)}, bf16[144,256]{1,0:T(8,128)(2,1)S(1)}, u32[]{:S(2)}, u32[]{:S(2)}) collective-permute-start(bf16[144,256]{1,0:T(8,128)(2,1)S(1)} %get-tuple-element.15.refs_0_.refs_5_), channel_id=1, source_target_pairs={{0,2},{1,3},{2,0},{3,1},{4,6},{5,7},{6,4},{7,5},{8,10},{9,11},{10,... | collective-permute-start | bytes 221192 | tf_op jit(solution)/shard_map/ppermute | solution.py:355
  15.0 7.6 %collective-permute-start = (bf16[128,256]{1,0:T(8,128)(2,1)}, bf16[128,256]{1,0:T(8,128)(2,1)S(1)}, u32[]{:S(2)}, u32[]{:S(2)}) collective-permute-start(bf16[128,256]{1,0:T(8,128)(2,1)} %own_ref.3), channel_id=1, source_target_pairs={{0,15},{1,2},{2,1},{3,4},{4,3},{5,6},{6,5},{7,8},{8,7},{9,10},{10,... | collective-permute-start | bytes 196616 | tf_op jit(solution)/shard_map/ppermute | solution.py:396
  16.3 6.3 %collective-permute-start.1 = (bf16[144,256]{1,0:T(8,128)(2,1)S(1)}, bf16[144,256]{1,0:T(8,128)(2,1)S(1)}, u32[]{:S(2)}, u32[]{:S(2)}) collective-permute-start(bf16[144,256]{1,0:T(8,128)(2,1)S(1)} %get-tuple-element.15.refs_0_.refs_5_), channel_id=1, source_target_pairs={{0,1},{1,0},{2,3},{3,2},{4,5},{5,4},{6,7},{7,6},{8,9},{9,8},{10,11... | collective-permute-start | bytes 221192 | tf_op jit(solution)/shard_map/ppermute | solution.py:355
  22.1 6.9 %collective-permute-start.7 = (bf16[576,256]{1,0:T(8,128)(2,1)S(1)}, bf16[576,256]{1,0:T(8,128)(2,1)S(1)}, u32[]{:S(2)}, u32[]{:S(2)}) collective-permute-start(bf16[576,256]{1,0:T(8,128)(2,1)S(1)} %pad_maximum_fusion), channel_id=1, source_target_pairs={{0,1},{1,0},{2,3},{3,2},{4,5},{5,4},{6,7},{7,6},{8,9},{9,8},{10,11... | collective-permute-start | bytes 884744 | tf_op jit(solution)/shard_map/ppermute | solution.py:355
  22.2 8.1 %collective-permute-start.8 = (bf16[432,256]{1,0:T(8,128)(2,1)S(1)}, bf16[432,256]{1,0:T(8,128)(2,1)S(1)}, u32[]{:S(2)}, u32[]{:S(2)}) collective-permute-start(bf16[432,256]{1,0:T(8,128)(2,1)S(1)} %collective-permute-done.6.refs_0_.refs_11_), channel_id=1, source_target_pairs={{0,1},{1,0},{2,3},{3,2},{4,5},{5,4},{6,7},{7,6},{8,9},{9,8},{10,11... | collective-permute-start | bytes 663560 | tf_op jit(solution)/shard_map/ppermute | solution.py:355
  27.7 3.4 %copy-start.2 = (bf16[2,256,256]{2,1,0:T(8,128)(2,1)S(1)}, bf16[2,256,256]{2,1,0:T(8,128)(2,1)}, u32[]{:S(2)}) copy-start(bf16[2,256,256]{2,1,0:T(8,128)(2,1)} %mixing_ref.3) | copy-start | bytes 786436
  27.7 3.4 %copy-start.3 = (bf16[2,256,256]{2,1,0:T(8,128)(2,1)S(1)}, bf16[2,256,256]{2,1,0:T(8,128)(2,1)}, u32[]{:S(2)}) copy-start(bf16[2,256,256]{2,1,0:T(8,128)(2,1)} %long_ref.3) | copy-start | bytes 786436
  27.7 3.4 %copy-start.4 = (bf16[2,256,256]{2,1,0:T(8,128)(2,1)S(1)}, bf16[2,256,256]{2,1,0:T(8,128)(2,1)}, u32[]{:S(2)}) copy-start(bf16[2,256,256]{2,1,0:T(8,128)(2,1)} %short_ref.1) | copy-start | bytes 786436
  30.2 13.2 %copy-start = (bf16[2,512,256]{2,1,0:T(8,128)(2,1)S(1)}, bf16[2,512,256]{2,1,0:T(8,128)(2,1)}, u32[]{:S(2)}) copy-start(bf16[2,512,256]{2,1,0:T(8,128)(2,1)} %filter_ref.5) | copy-start | bytes 1572868
  30.2 13.2 %copy-start.1 = (bf16[2,64,512]{2,1,0:T(8,128)(2,1)S(1)}, bf16[2,64,512]{2,1,0:T(8,128)(2,1)}, u32[]{:S(2)}) copy-start(bf16[2,64,512]{2,1,0:T(8,128)(2,1)} %rbf_ref.5) | copy-start | bytes 393220
  30.2 13.2 %copy-start.6 = (f32[64,128]{1,0:T(8,128)S(1)}, f32[64,128]{1,0:T(8,128)}, u32[]{:S(2)}) copy-start(f32[64,128]{1,0:T(8,128)} %distance_ref.5) | copy-start | bytes 98308
  32.1 6.8 %collective-permute-start.11 = (bf16[128,256]{1,0:T(8,128)(2,1)S(1)}, bf16[128,256]{1,0:T(8,128)(2,1)S(1)}, u32[]{:S(2)}, u32[]{:S(2)}) collective-permute-start(bf16[128,256]{1,0:T(8,128)(2,1)S(1)} %update.2.refs_3_.own_ref), channel_id=1, source_target_pairs={{0,12},{1,13},{2,14},{3,15},{4,8},{5,9},{6,10},{7,11},{8,4},{9,5},... | collective-permute-start | bytes 196616 | tf_op jit(solution)/shard_map/ppermute | solution.py:355
  34.0 6.8 %collective-permute-start.12 = (bf16[128,256]{1,0:T(8,128)(2,1)S(1)}, bf16[128,256]{1,0:T(8,128)(2,1)S(1)}, u32[]{:S(2)}, u32[]{:S(2)}) collective-permute-start(bf16[128,256]{1,0:T(8,128)(2,1)S(1)} %update.2.refs_3_.own_ref), channel_id=1, source_target_pairs={{0,8},{1,9},{2,10},{3,11},{4,12},{5,13},{6,14},{7,15},{8,0},{9,1},... | collective-permute-start | bytes 196616 | tf_op jit(solution)/shard_map/ppermute | solution.py:355
  34.0 6.8 %collective-permute-start.13 = (bf16[128,256]{1,0:T(8,128)(2,1)S(1)}, bf16[128,256]{1,0:T(8,128)(2,1)S(1)}, u32[]{:S(2)}, u32[]{:S(2)}) collective-permute-start(bf16[128,256]{1,0:T(8,128)(2,1)S(1)} %update.2.refs_3_.own_ref), channel_id=1, source_target_pairs={{0,4},{1,5},{2,6},{3,7},{4,0},{5,1},{6,2},{7,3},{8,12},{9,13},{10,... | collective-permute-start | bytes 196616 | tf_op jit(solution)/shard_map/ppermute | solution.py:355
  40.9 9.4 %collective-permute-start.15 = (bf16[384,256]{1,0:T(8,128)(2,1)S(1)}, bf16[384,256]{1,0:T(8,128)(2,1)S(1)}, u32[]{:S(2)}, u32[]{:S(2)}) collective-permute-start(bf16[384,256]{1,0:T(8,128)(2,1)S(1)} %pad_maximum_fusion.5), channel_id=1, source_target_pairs={{0,2},{1,3},{2,0},{3,1},{4,6},{5,7},{6,4},{7,5},{8,10},{9,11},{10,... | collective-permute-start | bytes 589832 | tf_op jit(solution)/shard_map/ppermute | solution.py:355
  43.3 6.9 %collective-permute-start.14 = (bf16[128,256]{1,0:T(8,128)(2,1)S(1)}, bf16[128,256]{1,0:T(8,128)(2,1)S(1)}, u32[]{:S(2)}, u32[]{:S(2)}) collective-permute-start(bf16[128,256]{1,0:T(8,128)(2,1)S(1)} %update.2.refs_3_.own_ref), channel_id=1, source_target_pairs={{0,2},{1,3},{2,0},{3,1},{4,6},{5,7},{6,4},{7,5},{8,10},{9,11},{10,... | collective-permute-start | bytes 196616 | tf_op jit(solution)/shard_map/ppermute | solution.py:355
  46.0 6.5 %collective-permute-start.9 = (bf16[128,256]{1,0:T(8,128)(2,1)S(1)}, bf16[128,256]{1,0:T(8,128)(2,1)S(1)}, u32[]{:S(2)}, u32[]{:S(2)}) collective-permute-start(bf16[128,256]{1,0:T(8,128)(2,1)S(1)} %update.2.refs_3_.own_ref), channel_id=1, source_target_pairs={{0,15},{1,2},{2,1},{3,4},{4,3},{5,6},{6,5},{7,8},{8,7},{9,10},{10,... | collective-permute-start | bytes 196616 | tf_op jit(solution)/shard_map/ppermute | solution.py:396
  48.2 4.3 %collective-permute-start.10 = (bf16[128,256]{1,0:T(8,128)(2,1)S(1)}, bf16[128,256]{1,0:T(8,128)(2,1)S(1)}, u32[]{:S(2)}, u32[]{:S(2)}) collective-permute-start(bf16[128,256]{1,0:T(8,128)(2,1)S(1)} %update.2.refs_3_.own_ref), channel_id=1, source_target_pairs={{0,1},{1,0},{2,3},{3,2},{4,5},{5,4},{6,7},{7,6},{8,9},{9,8},{10,11... | collective-permute-start | bytes 196616 | tf_op jit(solution)/shard_map/ppermute | solution.py:355
  50.2 7.2 %collective-permute-start.16 = (bf16[512,256]{1,0:T(8,128)(2,1)S(1)}, bf16[512,256]{1,0:T(8,128)(2,1)S(1)}, u32[]{:S(2)}, u32[]{:S(2)}) collective-permute-start(bf16[512,256]{1,0:T(8,128)(2,1)S(1)} %pad_maximum_fusion.1), channel_id=1, source_target_pairs={{0,1},{1,0},{2,3},{3,2},{4,5},{5,4},{6,7},{7,6},{8,9},{9,8},{10,11... | collective-permute-start | bytes 786440 | tf_op jit(solution)/shard_map/ppermute | solution.py:355
  50.3 7.5 %collective-permute-start.17 = (bf16[384,256]{1,0:T(8,128)(2,1)S(1)}, bf16[384,256]{1,0:T(8,128)(2,1)S(1)}, u32[]{:S(2)}, u32[]{:S(2)}) collective-permute-start(bf16[384,256]{1,0:T(8,128)(2,1)S(1)} %collective-permute-done.15.refs_9_), channel_id=1, source_target_pairs={{0,1},{1,0},{2,3},{3,2},{4,5},{5,4},{6,7},{7,6},{8,9},{9,8},{10,11... | collective-permute-start | bytes 589832 | tf_op jit(solution)/shard_map/ppermute | solution.py:355

commit v4 on v3

--- a/solution.py
+++ b/solution.py
@@ -148,7 +148,7 @@
 def coupling_kernel(places, rows, left_ref, zc_ref, zs_ref, *refs):
     count = max(p[0] for p in places) + 1
     packed, out_ref, right_ref, part_ref = refs[:count], refs[count], refs[count + 1], refs[count + 2]
-    tile = 32
+    tile = 64
     for pair in range(0, len(places), 2):
         turn = pair // 2 % 2
         span = min(2, len(places) - pair)
@@ -299,48 +299,42 @@
     return total
 
 
-def partial_kernel(places, pairs, layer, message_ref, short_ref, *refs):
-    matrices, states, total_ref, close_ref = refs[:pairs], refs[pairs:-2], refs[-2], refs[-1]
+def partial_kernel(places, pairs, layer, message_ref, short_ref, mixing_ref, long_ref, *refs):
+    matrices, states = refs[:pairs], refs[pairs:-3]
+    total_ref, close_ref, joint_ref = refs[-3:]
     total_ref[...] = gathered_field(places, message_ref.shape[0], matrices, states)
     close_ref[...] = dot(message_ref[...], short_ref[layer])
-
-
-def partial_update(message, w_short, layer, matrices, arrays, places):
+    joint_ref[...] = dot(mixing_ref[layer], long_ref[layer]).astype(BF)
+
+
+def partial_update(message, w_short, w_mixing, w_long, layer, matrices, arrays, places):
     shape = jax.ShapeDtypeStruct(message.shape, F32)
     return pl.pallas_call(
         functools.partial(partial_kernel, tuple(places), len(matrices), layer),
-        out_shape=(shape, shape),
-        in_specs=[VM] * (2 + len(matrices) + len(arrays)),
-        out_specs=(VM, VM),
+        out_shape=(shape, shape, jax.ShapeDtypeStruct(w_mixing.shape[1:], BF)),
+        in_specs=[VM] * (4 + len(matrices) + len(arrays)),
+        out_specs=(VM,) * 3,
         compiler_params=limit,
         name="partial",
-    )(message, w_short, *matrices, *arrays)
-
-
-def update_kernel(places, pairs, begun, layer, before, after, own_ref, mixing_ref, long_ref, *refs):
-    rows, _ = own_ref.shape
-    head, matrices, states, out_ref = refs[:2], refs[2 : 2 + pairs], refs[2 + pairs : -1], refs[-1]
-    total = gathered_field(places, rows, matrices, states)
-    if begun:
-        total = total + head[0][...]
-        close = head[1][...]
-    else:
-        close = dot(head[0][...], head[1][layer])
-    potential = dot((total * before).astype(BF), mixing_ref[layer]).astype(BF)
-    field = (potential.astype(F32) * after).astype(BF)
-    half = 0.5 * (close + dot(field, long_ref[layer]))
+    )(message, w_short, w_mixing, w_long, *matrices, *arrays)
+
+
+def update_kernel(places, pairs, scale, own_ref, total_ref, close_ref, joint_ref, *refs):
+    matrices, states, out_ref = refs[:pairs], refs[pairs:-1], refs[-1]
+    total = total_ref[...] + gathered_field(places, own_ref.shape[0], matrices, states)
+    half = 0.5 * (close_ref[...] + dot((total * scale).astype(BF), joint_ref[...]))
     out_ref[...] = (own_ref[...].astype(F32) + (half + half * jnp.tanh(half))).astype(BF)
 
 
-def update(own, head, begun, mixing, long, layer, matrices, arrays, places, before, after):
-    return pl.pallas_call(
-        functools.partial(update_kernel, tuple(places), len(matrices), begun, layer, before, after),
+def update(own, head, matrices, arrays, places, scale):
+    return pl.pallas_call(
+        functools.partial(update_kernel, tuple(places), len(matrices), scale),
         out_shape=jax.ShapeDtypeStruct(own.shape, BF),
-        in_specs=[VM] * (5 + len(matrices) + len(arrays)),
+        in_specs=[VM] * (4 + len(matrices) + len(arrays)),
         out_specs=VM,
         compiler_params=limit,
         name="update",
-    )(own, mixing, long, *head, *matrices, *arrays)
+    )(own, *head, *matrices, *arrays)
 
 
 def picked(spots, matrices, arrays):
@@ -451,18 +445,15 @@
                 couple(arrays, places)
             early = list(places)
             arrays, places = exchange(arrays, places, stage, size)
+        early = [q for q in early if layer or q in where]
+        spot = {q: places[q] + where[q] for q in early}
+        used, held, spots = picked([spot[q] for q in early], matrices, arrays)
+        head = partial_update(message, w_short, w_mixing, w_long, layer, used, held, spots)
         if layer == 0:
             couple(arrays, places)
-            early = []
-        spot = {q: places[q] + where[q] for q in places}
-        head, late = (message, w_short), [q for q in places if q not in early]
-        if early:
-            used, held, spots = picked([spot[q] for q in early], matrices, arrays)
-            head = partial_update(message, w_short, layer, used, held, spots)
-        used, held, spots = picked([spot[q] for q in late], matrices, arrays)
-        state = update(
-            state, head, bool(early), w_mixing, w_long, layer, used, held, spots, before, after
-        )
+        spot = {q: places[q] + where[q] for q in places if q not in early}
+        used, held, spots = picked(list(spot.values()), matrices, arrays)
+        state = update(state, head, used, held, spots, before * after)
     return state
 
 

time: 59.1 us -> 59 us (level)
    pallas_call x2, Pallas kernels: 2.08 us -> 1.37 us  [update(): pl.pallas_call(functools.partial(update_kernel, tuple(places), len(matric...]
  transfers between devices with their start and end apart: 18 -> 18, of which waited for: 7 -> 7; matrix products, arithmetic and copies ran while one was open for 0% -> 0% of each run, Pallas kernels for 30% -> 31%
where the time goes in v4:
time: 59 us; the launch traced here: 58.9 us
  Pallas kernels  22.2 us (38%)
  starting transfers between devices  19.8 us (34%)
  waiting for transfers between devices  16.4 us (28%)
    ppermute x16, starting transfers between devices, swap(): lax.ppermute(x, 'atom', [(i, i ^ (odd if i % 2 else even)) for i in range...  16.4 us
    ppermute x16, waiting for transfers between devices, swap(): lax.ppermute(x, 'atom', [(i, i ^ (odd if i % 2 else even)) for i in range...  14.8 us
    pallas_call x2, Pallas kernels, messages(): pl.pallas_call(functools.partial(message_kernel, layer), out_shape=jax.Sh...  9.83 us
    pallas_call x2, Pallas kernels, filters_of(): pl.pallas_call(functools.partial(filter_kernel, layer), out_shape=jax.Sha...  5.1 us
    pallas_call x3, Pallas kernels, coupling(): pl.pallas_call(functools.partial(coupling_kernel, tuple(places), rows), o...  3.48 us
    ppermute x2, starting transfers between devices, neighbour_table(): lax.ppermute(own, 'atom', [(i, (i + (count - 1 if i % 2 == 0 else 1)) % c...  3.46 us
    ppermute x2, waiting for transfers between devices, neighbour_table(): lax.ppermute(own, 'atom', [(i, (i + (count - 1 if i % 2 == 0 else 1)) % c...  1.61 us
    pallas_call x1, Pallas kernels, prepare(): pl.pallas_call(prepare_kernel, out_shape=shapes, grid=(1,), in_specs=[who...  1.54 us
  transfers between devices with their start and end apart: 18, of which 7 were waited for; matrix products, arithmetic and copies ran while one was open for 0% of the time, Pallas kernels for 31%

profile of v4, /device:TPU:0, one launch (start us, length us, event | category | flops | bytes accessed | tf_op | source)
XLA Modules:
  0.0 58.9 jit_solution(16879400404313689450)
XLA Ops:
  0.0 1.5 %prepare.1 = (bf16[144,256]{1,0:T(8,128)(2,1)S(1)}, bf16[13,128,256]{2,1,0:T(8,128)(2,1)S(1)}, f32[128,128]{1,0:T(8,128)S(1)}, f32[128,128]{1,0:T(8,128)S(1)}, f...) custom-call(s32[3,2048]{1,0:T(4,128)} %wave_ref.1, f32[3,128]{1,0:T(4,128)} %position_ref.1, ...), custom_call_target="tpu_custom_call" | custom-call | tf_op jit(solution)/shard_map/prepare/pallas_call | solution.py:137
  1.5 0.0 copy-start.7
  1.6 0.0 copy-start.8
  1.6 5.1 %collective-permute-start.2 = (bf16[144,256]{1,0:T(8,128)(2,1)S(1)}, bf16[144,256]{1,0:T(8,128)(2,1)S(1)}, u32[]{:S(2)}, u32[]{:S(2)}) collective-permute-start(bf16[144,256]{1,0:T(8,128)(2,1)S(1)} %get-tuple-element.19.refs_0_.refs_2_), channel_id=1, source_target_pairs={{0,12},{1,13},{2,14},{3,15},{4,8},{5,9},{6,10},{7,11},{8,4},{9,5},... | collective-permute-start | bytes 221192 | tf_op jit(solution)/shard_map/ppermute | solution.py:349
  6.7 0.0 collective-permute-start.3
  6.7 0.6 %collective-permute-start.4 = (bf16[144,256]{1,0:T(8,128)(2,1)S(1)}, bf16[144,256]{1,0:T(8,128)(2,1)S(1)}, u32[]{:S(2)}, u32[]{:S(2)}) collective-permute-start(bf16[144,256]{1,0:T(8,128)(2,1)S(1)} %get-tuple-element.19.refs_0_.refs_2_), channel_id=1, source_target_pairs={{0,4},{1,5},{2,6},{3,7},{4,0},{5,1},{6,2},{7,3},{8,12},{9,13},{10,... | collective-permute-start | bytes 221192 | tf_op jit(solution)/shard_map/ppermute | solution.py:349
  7.4 2.0 %collective-permute-done.2.refs_1_.refs_3_ = bf16[144,256]{1,0:T(8,128)(2,1)S(1)} collective-permute-done((bf16[144,256]{1,0:T(8,128)(2,1)S(1)}, bf16[144,256]{1,0:T(8,128)(2,1)S(1)}, u32[]{:S(2)}, u32[]{:S(2)}) %collective-permute-start.2) | collective-permute-done | bytes 73760 | tf_op jit(solution)/shard_map/ppermute | solution.py:349
  9.4 3.5 %collective-permute-done.3.refs_2_.refs_4_ = bf16[144,256]{1,0:T(8,128)(2,1)S(1)} collective-permute-done((bf16[144,256]{1,0:T(8,128)(2,1)S(1)}, bf16[144,256]{1,0:T(8,128)(2,1)S(1)}, u32[]{:S(2)}, u32[]{:S(2)}) %collective-permute-start.3) | collective-permute-done | bytes 73760 | tf_op jit(solution)/shard_map/ppermute | solution.py:349
  12.9 0.0 collective-permute-done.4.refs_3_.refs_5_
  13.0 1.6 %collective-permute-start.6 = (bf16[432,256]{1,0:T(8,128)(2,1)S(1)}, bf16[432,256]{1,0:T(8,128)(2,1)S(1)}, u32[]{:S(2)}, u32[]{:S(2)}) collective-permute-start(bf16[432,256]{1,0:T(8,128)(2,1)S(1)} %pad_maximum_fusion.2), channel_id=1, source_target_pairs={{0,2},{1,3},{2,0},{3,1},{4,6},{5,7},{6,4},{7,5},{8,10},{9,11},{10,... | collective-permute-start | bytes 663560 | tf_op jit(solution)/shard_map/ppermute | solution.py:349
  14.5 0.5 collective-permute-start.5
  15.0 1.3 %collective-permute-start = (bf16[128,256]{1,0:T(8,128)(2,1)}, bf16[128,256]{1,0:T(8,128)(2,1)S(1)}, u32[]{:S(2)}, u32[]{:S(2)}) collective-permute-start(bf16[128,256]{1,0:T(8,128)(2,1)} %own_ref.3), channel_id=1, source_target_pairs={{0,15},{1,2},{2,1},{3,4},{4,3},{5,6},{6,5},{7,8},{8,7},{9,10},{10,... | collective-permute-start | bytes 196616 | tf_op jit(solution)/shard_map/ppermute | solution.py:390
  16.3 0.4 collective-permute-start.1
  16.7 2.5 %filters.2.ready_ref = bf16[32,128,256]{2,1,0:T(8,128)(2,1)S(1)} custom-call(f32[64,128]{1,0:T(8,128)S(1)} %get-tuple-element.18.distance_ref, bf16[1,64,512]{2,1,0:T(8,128)(2,1)S(1)} %get-tuple-element.20.rbf_ref, bf16[1,512,256]{2,1,0:T(8,128)(2,1)S(1)} %get-tuple-element.21.filter_ref), custom_call_target="tpu_custom_call" | custom-call | tf_op jit(solution)/shard_map/filters/pallas_call | solution.py:235
  19.2 2.8 %collective-permute-done.5.refs_4_.refs_6_ = bf16[144,256]{1,0:T(8,128)(2,1)S(1)} collective-permute-done((bf16[144,256]{1,0:T(8,128)(2,1)S(1)}, bf16[144,256]{1,0:T(8,128)(2,1)S(1)}, u32[]{:S(2)}, u32[]{:S(2)}) %collective-permute-start.5) | collective-permute-done | bytes 73760 | tf_op jit(solution)/shard_map/ppermute | solution.py:349
  22.1 0.1 collective-permute-start.7
  22.2 0.0 collective-permute-done.6.refs_0_.refs_8_
  22.2 0.5 collective-permute-start.8
  22.7 0.0 collective-permute-done
  22.7 0.0 collective-permute-done.1.refs_5_.refs_7_
  22.7 0.0 copy-done.5
  22.7 0.0 copy-done.7
  22.7 0.0 copy-done.8
  22.7 4.9 %messages.2.message_ref = bf16[128,256]{1,0:T(8,128)(2,1)S(1)} custom-call(s32[64,128]{1,0:T(8,128)S(1)} %copy-done.7, f32[64,128]{1,0:T(8,128)S(1)} %get-tuple-element.18.distance_ref, s32[64,128]{1,0:T(8,128)S(1)} %copy-done.8, bf16[384,256]{1,0:T(8,128)(2,1)S(1)} %pad_maximum_fusion.3.table_ref, bf16[1,64,512]{2,1,0:T(8,128)(2,1)S(1)} %get-tuple-element.20.rbf_ref, ...), custom_call_target="tpu_custom_call" | custom-call | tf_op jit(solution)/shard_map/messages/pallas_call | solution.py:282
  27.7 0.0 copy-start.2
  27.7 0.0 copy-start.3
  27.7 0.0 copy-start.4
  27.7 1.2 %coupling.3.refs_0_ = bf16[128,768]{1,0:T(8,128)(2,1)S(1)} custom-call(bf16[13,128,256]{2,1,0:T(8,128)(2,1)S(1)} %get-tuple-element.22.left_ref, f32[128,128]{1,0:T(8,128)S(1)} %get-tuple-element.23.zc_ref, f32[128,128]{1,0:T(8,128)S(1)} %get-tuple-element.24.zs_ref, bf16[144,256]{1,0:T(8,128)(2,1)S(1)} %get-tuple-element.19.refs_0_.refs_2_, ...), custom_call_target="tpu_custom_call" | custom-call | tf_op jit(solution)/shard_map/coupling/pallas_call | solution.py:188
  28.9 0.0 collective-permute-done.7.refs_1_.refs_9_.refs_0_
  28.9 1.2 %coupling.4.refs_1_ = bf16[128,768]{1,0:T(8,128)(2,1)S(1)} custom-call(bf16[13,128,256]{2,1,0:T(8,128)(2,1)S(1)} %get-tuple-element.22.left_ref, f32[128,128]{1,0:T(8,128)S(1)} %get-tuple-element.23.zc_ref, f32[128,128]{1,0:T(8,128)S(1)} %get-tuple-element.24.zs_ref, bf16[432,256]{1,0:T(8,128)(2,1)S(1)} %collective-permute-done.6.refs_0_.refs_8_, ...), custom_call_target="tpu_custom_call" | custom-call | tf_op jit(solution)/shard_map/coupling/pallas_call | solution.py:188
  30.2 0.0 copy-done.2
  30.2 0.0 copy-done.3
  30.2 0.0 copy-done.4
  30.2 0.4 partial.2
  30.7 0.0 copy-start
  30.7 0.0 copy-start.1
  30.7 0.0 copy-start.6
  30.7 0.0 collective-permute-done.8.refs_1_.refs_2_
  30.7 1.0 %coupling.5.refs_0_.refs_2_ = bf16[128,512]{1,0:T(8,128)(2,1)S(1)} custom-call(bf16[13,128,256]{2,1,0:T(8,128)(2,1)S(1)} %get-tuple-element.22.left_ref, f32[128,128]{1,0:T(8,128)S(1)} %get-tuple-element.23.zc_ref, f32[128,128]{1,0:T(8,128)S(1)} %get-tuple-element.24.zs_ref, bf16[576,256]{1,0:T(8,128)(2,1)S(1)} %collective-permute-done.7.refs_1_.refs_9_.refs_0_, ...), custom_call_target="tpu_custom_call" | custom-call | tf_op jit(solution)/shard_map/coupling/pallas_call | solution.py:188
  31.7 0.4 update.2.refs_3_.own_ref
  32.1 1.9 %collective-permute-start.11 = (bf16[128,256]{1,0:T(8,128)(2,1)S(1)}, bf16[128,256]{1,0:T(8,128)(2,1)S(1)}, u32[]{:S(2)}, u32[]{:S(2)}) collective-permute-start(bf16[128,256]{1,0:T(8,128)(2,1)S(1)} %update.2.refs_3_.own_ref), channel_id=1, source_target_pairs={{0,12},{1,13},{2,14},{3,15},{4,8},{5,9},{6,10},{7,11},{8,4},{9,5},... | collective-permute-start | bytes 196616 | tf_op jit(solution)/shard_map/ppermute | solution.py:349
  34.1 0.0 collective-permute-start.12
  34.1 2.5 %collective-permute-start.13 = (bf16[128,256]{1,0:T(8,128)(2,1)S(1)}, bf16[128,256]{1,0:T(8,128)(2,1)S(1)}, u32[]{:S(2)}, u32[]{:S(2)}) collective-permute-start(bf16[128,256]{1,0:T(8,128)(2,1)S(1)} %update.2.refs_3_.own_ref), channel_id=1, source_target_pairs={{0,4},{1,5},{2,6},{3,7},{4,0},{5,1},{6,2},{7,3},{8,12},{9,13},{10,... | collective-permute-start | bytes 196616 | tf_op jit(solution)/shard_map/ppermute | solution.py:349
  36.6 2.4 %collective-permute-done.11.refs_4_ = bf16[128,256]{1,0:T(8,128)(2,1)S(1)} collective-permute-done((bf16[128,256]{1,0:T(8,128)(2,1)S(1)}, bf16[128,256]{1,0:T(8,128)(2,1)S(1)}, u32[]{:S(2)}, u32[]{:S(2)}) %collective-permute-start.11) | collective-permute-done | bytes 65568 | tf_op jit(solution)/shard_map/ppermute | solution.py:349
  39.0 1.9 %collective-permute-done.12.refs_5_ = bf16[128,256]{1,0:T(8,128)(2,1)S(1)} collective-permute-done((bf16[128,256]{1,0:T(8,128)(2,1)S(1)}, bf16[128,256]{1,0:T(8,128)(2,1)S(1)}, u32[]{:S(2)}, u32[]{:S(2)}) %collective-permute-start.12) | collective-permute-done | bytes 65568 | tf_op jit(solution)/shard_map/ppermute | solution.py:349
  40.9 0.0 collective-permute-done.13.refs_6_
  40.9 2.5 %collective-permute-start.15 = (bf16[384,256]{1,0:T(8,128)(2,1)S(1)}, bf16[384,256]{1,0:T(8,128)(2,1)S(1)}, u32[]{:S(2)}, u32[]{:S(2)}) collective-permute-start(bf16[384,256]{1,0:T(8,128)(2,1)S(1)} %pad_maximum_fusion.5), channel_id=1, source_target_pairs={{0,2},{1,3},{2,0},{3,1},{4,6},{5,7},{6,4},{7,5},{8,10},{9,11},{10,... | collective-permute-start | bytes 589832 | tf_op jit(solution)/shard_map/ppermute | solution.py:349
  43.4 0.1 collective-permute-start.14
  43.5 0.0 copy-done
  43.5 0.0 copy-done.1
  43.5 2.6 %filters.3.ready_ref = bf16[32,128,256]{2,1,0:T(8,128)(2,1)S(1)} custom-call(f32[64,128]{1,0:T(8,128)S(1)} %copy-done.6, bf16[2,64,512]{2,1,0:T(8,128)(2,1)S(1)} %copy-done.1, bf16[2,512,256]{2,1,0:T(8,128)(2,1)S(1)} %copy-done), custom_call_target="tpu_custom_call" | custom-call | tf_op jit(solution)/shard_map/filters/pallas_call | solution.py:235
  46.0 2.2 %collective-permute-start.9 = (bf16[128,256]{1,0:T(8,128)(2,1)S(1)}, bf16[128,256]{1,0:T(8,128)(2,1)S(1)}, u32[]{:S(2)}, u32[]{:S(2)}) collective-permute-start(bf16[128,256]{1,0:T(8,128)(2,1)S(1)} %update.2.refs_3_.own_ref), channel_id=1, source_target_pairs={{0,15},{1,2},{2,1},{3,4},{4,3},{5,6},{6,5},{7,8},{8,7},{9,10},{10,... | collective-permute-start | bytes 196616 | tf_op jit(solution)/shard_map/ppermute | solution.py:390
  48.2 0.0 collective-permute-start.10
  48.2 2.1 %collective-permute-done.14.refs_7_ = bf16[128,256]{1,0:T(8,128)(2,1)S(1)} collective-permute-done((bf16[128,256]{1,0:T(8,128)(2,1)S(1)}, bf16[128,256]{1,0:T(8,128)(2,1)S(1)}, u32[]{:S(2)}, u32[]{:S(2)}) %collective-permute-start.14) | collective-permute-done | bytes 65568 | tf_op jit(solution)/shard_map/ppermute | solution.py:349
  50.3 0.1 collective-permute-start.16
  50.4 0.0 collective-permute-done.15.refs_9_
  50.4 0.5 collective-permute-start.17
  50.9 1.6 %collective-permute-done.9 = bf16[128,256]{1,0:T(8,128)(2,1)S(1)} collective-permute-done((bf16[128,256]{1,0:T(8,128)(2,1)S(1)}, bf16[128,256]{1,0:T(8,128)(2,1)S(1)}, u32[]{:S(2)}, u32[]{:S(2)}) %collective-permute-start.9) | collective-permute-done | bytes 65568 | tf_op jit(solution)/shard_map/ppermute | solution.py:390
  52.5 0.0 collective-permute-done.10.refs_8_
  52.5 4.9 %messages.3.message_ref = bf16[128,256]{1,0:T(8,128)(2,1)S(1)} custom-call(s32[64,128]{1,0:T(8,128)S(1)} %copy-done.7, f32[64,128]{1,0:T(8,128)S(1)} %copy-done.6, s32[64,128]{1,0:T(8,128)S(1)} %copy-done.8, bf16[384,256]{1,0:T(8,128)(2,1)S(1)} %pad_maximum_fusion.4.table_ref, bf16[2,64,512]{2,1,0:T(8,128)(2,1)S(1)} %copy-done.1, ...), custom_call_target="tpu_custom_call" | custom-call | tf_op jit(solution)/shard_map/messages/pallas_call | solution.py:282
  57.4 0.0 collective-permute-done.16.refs_10_
  57.5 0.4 partial.3
  57.9 0.0 collective-permute-done.17.refs_1_
  57.9 1.0 %update.3 = bf16[128,256]{1,0:T(8,128)(2,1)} custom-call(bf16[128,256]{1,0:T(8,128)(2,1)S(1)} %update.2.refs_3_.own_ref, f32[128,256]{1,0:T(8,128)S(1)} %get-tuple-element.28.total_ref, f32[128,256]{1,0:T(8,128)S(1)} %get-tuple-element.29.close_ref, bf16[256,256]{1,0:T(8,128)(2,1)S(1)} %get-tuple-element.30.joint_ref, ...), custom_call_target="tpu_custom_call" | custom-call | tf_op jit(solution)/shard_map/update/pallas_call | solution.py:330
  (10 shorter events, 0.1 us)
Async XLA Ops:
  0.0 22.7 %copy-start.5 = (bf16[128,256]{1,0:T(8,128)(2,1)S(1)}, bf16[128,256]{1,0:T(8,128)(2,1)}, u32[]{:S(2)}) copy-start(bf16[128,256]{1,0:T(8,128)(2,1)} %own_ref.3) | copy-start | bytes 196612
  1.5 21.2 %copy-start.7 = (s32[64,128]{1,0:T(8,128)S(1)}, s32[64,128]{1,0:T(8,128)}, u32[]{:S(2)}) copy-start(s32[64,128]{1,0:T(8,128)} %index_ref.3) | copy-start | bytes 98308
  1.6 21.2 %copy-start.8 = (s32[64,128]{1,0:T(8,128)S(1)}, s32[64,128]{1,0:T(8,128)}, u32[]{:S(2)}) copy-start(s32[64,128]{1,0:T(8,128)} %mask_ref.3) | copy-start | bytes 98308
  1.6 7.8 %collective-permute-start.2 = (bf16[144,256]{1,0:T(8,128)(2,1)S(1)}, bf16[144,256]{1,0:T(8,128)(2,1)S(1)}, u32[]{:S(2)}, u32[]{:S(2)}) collective-permute-start(bf16[144,256]{1,0:T(8,128)(2,1)S(1)} %get-tuple-element.19.refs_0_.refs_2_), channel_id=1, source_target_pairs={{0,12},{1,13},{2,14},{3,15},{4,8},{5,9},{6,10},{7,11},{8,4},{9,5},... | collective-permute-start | bytes 221192 | tf_op jit(solution)/shard_map/ppermute | solution.py:349
  6.7 6.2 %collective-permute-start.3 = (bf16[144,256]{1,0:T(8,128)(2,1)S(1)}, bf16[144,256]{1,0:T(8,128)(2,1)S(1)}, u32[]{:S(2)}, u32[]{:S(2)}) collective-permute-start(bf16[144,256]{1,0:T(8,128)(2,1)S(1)} %get-tuple-element.19.refs_0_.refs_2_), channel_id=1, source_target_pairs={{0,8},{1,9},{2,10},{3,11},{4,12},{5,13},{6,14},{7,15},{8,0},{9,1},... | collective-permute-start | bytes 221192 | tf_op jit(solution)/shard_map/ppermute | solution.py:349
  6.7 6.2 %collective-permute-start.4 = (bf16[144,256]{1,0:T(8,128)(2,1)S(1)}, bf16[144,256]{1,0:T(8,128)(2,1)S(1)}, u32[]{:S(2)}, u32[]{:S(2)}) collective-permute-start(bf16[144,256]{1,0:T(8,128)(2,1)S(1)} %get-tuple-element.19.refs_0_.refs_2_), channel_id=1, source_target_pairs={{0,4},{1,5},{2,6},{3,7},{4,0},{5,1},{6,2},{7,3},{8,12},{9,13},{10,... | collective-permute-start | bytes 221192 | tf_op jit(solution)/shard_map/ppermute | solution.py:349
  13.0 9.2 %collective-permute-start.6 = (bf16[432,256]{1,0:T(8,128)(2,1)S(1)}, bf16[432,256]{1,0:T(8,128)(2,1)S(1)}, u32[]{:S(2)}, u32[]{:S(2)}) collective-permute-start(bf16[432,256]{1,0:T(8,128)(2,1)S(1)} %pad_maximum_fusion.2), channel_id=1, source_target_pairs={{0,2},{1,3},{2,0},{3,1},{4,6},{5,7},{6,4},{7,5},{8,10},{9,11},{10,... | collective-permute-start | bytes 663560 | tf_op jit(solution)/shard_map/ppermute | solution.py:349
  14.5 7.5 %collective-permute-start.5 = (bf16[144,256]{1,0:T(8,128)(2,1)S(1)}, bf16[144,256]{1,0:T(8,128)(2,1)S(1)}, u32[]{:S(2)}, u32[]{:S(2)}) collective-permute-start(bf16[144,256]{1,0:T(8,128)(2,1)S(1)} %get-tuple-element.19.refs_0_.refs_2_), channel_id=1, source_target_pairs={{0,2},{1,3},{2,0},{3,1},{4,6},{5,7},{6,4},{7,5},{8,10},{9,11},{10,... | collective-permute-start | bytes 221192 | tf_op jit(solution)/shard_map/ppermute | solution.py:349
  15.0 7.6 %collective-permute-start = (bf16[128,256]{1,0:T(8,128)(2,1)}, bf16[128,256]{1,0:T(8,128)(2,1)S(1)}, u32[]{:S(2)}, u32[]{:S(2)}) collective-permute-start(bf16[128,256]{1,0:T(8,128)(2,1)} %own_ref.3), channel_id=1, source_target_pairs={{0,15},{1,2},{2,1},{3,4},{4,3},{5,6},{6,5},{7,8},{8,7},{9,10},{10,... | collective-permute-start | bytes 196616 | tf_op jit(solution)/shard_map/ppermute | solution.py:390
  16.3 6.3 %collective-permute-start.1 = (bf16[144,256]{1,0:T(8,128)(2,1)S(1)}, bf16[144,256]{1,0:T(8,128)(2,1)S(1)}, u32[]{:S(2)}, u32[]{:S(2)}) collective-permute-start(bf16[144,256]{1,0:T(8,128)(2,1)S(1)} %get-tuple-element.19.refs_0_.refs_2_), channel_id=1, source_target_pairs={{0,1},{1,0},{2,3},{3,2},{4,5},{5,4},{6,7},{7,6},{8,9},{9,8},{10,11... | collective-permute-start | bytes 221192 | tf_op jit(solution)/shard_map/ppermute | solution.py:349
  22.1 6.9 %collective-permute-start.7 = (bf16[576,256]{1,0:T(8,128)(2,1)S(1)}, bf16[576,256]{1,0:T(8,128)(2,1)S(1)}, u32[]{:S(2)}, u32[]{:S(2)}) collective-permute-start(bf16[576,256]{1,0:T(8,128)(2,1)S(1)} %pad_maximum_fusion), channel_id=1, source_target_pairs={{0,1},{1,0},{2,3},{3,2},{4,5},{5,4},{6,7},{7,6},{8,9},{9,8},{10,11... | collective-permute-start | bytes 884744 | tf_op jit(solution)/shard_map/ppermute | solution.py:349
  22.2 8.5 %collective-permute-start.8 = (bf16[432,256]{1,0:T(8,128)(2,1)S(1)}, bf16[432,256]{1,0:T(8,128)(2,1)S(1)}, u32[]{:S(2)}, u32[]{:S(2)}) collective-permute-start(bf16[432,256]{1,0:T(8,128)(2,1)S(1)} %collective-permute-done.6.refs_0_.refs_8_), channel_id=1, source_target_pairs={{0,1},{1,0},{2,3},{3,2},{4,5},{5,4},{6,7},{7,6},{8,9},{9,8},{10,11... | collective-permute-start | bytes 663560 | tf_op jit(solution)/shard_map/ppermute | solution.py:349
  27.7 2.5 %copy-start.2 = (bf16[2,256,256]{2,1,0:T(8,128)(2,1)S(1)}, bf16[2,256,256]{2,1,0:T(8,128)(2,1)}, u32[]{:S(2)}) copy-start(bf16[2,256,256]{2,1,0:T(8,128)(2,1)} %short_ref.3) | copy-start | bytes 786436
  27.7 2.5 %copy-start.3 = (bf16[2,256,256]{2,1,0:T(8,128)(2,1)S(1)}, bf16[2,256,256]{2,1,0:T(8,128)(2,1)}, u32[]{:S(2)}) copy-start(bf16[2,256,256]{2,1,0:T(8,128)(2,1)} %mixing_ref.3) | copy-start | bytes 786436
  27.7 2.5 %copy-start.4 = (bf16[2,256,256]{2,1,0:T(8,128)(2,1)S(1)}, bf16[2,256,256]{2,1,0:T(8,128)(2,1)}, u32[]{:S(2)}) copy-start(bf16[2,256,256]{2,1,0:T(8,128)(2,1)} %long_ref.3) | copy-start | bytes 786436
  30.7 12.8 %copy-start = (bf16[2,512,256]{2,1,0:T(8,128)(2,1)S(1)}, bf16[2,512,256]{2,1,0:T(8,128)(2,1)}, u32[]{:S(2)}) copy-start(bf16[2,512,256]{2,1,0:T(8,128)(2,1)} %filter_ref.5) | copy-start | bytes 1572868
  30.7 12.8 %copy-start.1 = (bf16[2,64,512]{2,1,0:T(8,128)(2,1)S(1)}, bf16[2,64,512]{2,1,0:T(8,128)(2,1)}, u32[]{:S(2)}) copy-start(bf16[2,64,512]{2,1,0:T(8,128)(2,1)} %rbf_ref.5) | copy-start | bytes 393220
  30.7 12.8 %copy-start.6 = (f32[64,128]{1,0:T(8,128)S(1)}, f32[64,128]{1,0:T(8,128)}, u32[]{:S(2)}) copy-start(f32[64,128]{1,0:T(8,128)} %distance_ref.5) | copy-start | bytes 98308
  32.1 6.8 %collective-permute-start.11 = (bf16[128,256]{1,0:T(8,128)(2,1)S(1)}, bf16[128,256]{1,0:T(8,128)(2,1)S(1)}, u32[]{:S(2)}, u32[]{:S(2)}) collective-permute-start(bf16[128,256]{1,0:T(8,128)(2,1)S(1)} %update.2.refs_3_.own_ref), channel_id=1, source_target_pairs={{0,12},{1,13},{2,14},{3,15},{4,8},{5,9},{6,10},{7,11},{8,4},{9,5},... | collective-permute-start | bytes 196616 | tf_op jit(solution)/shard_map/ppermute | solution.py:349
  34.1 6.8 %collective-permute-start.12 = (bf16[128,256]{1,0:T(8,128)(2,1)S(1)}, bf16[128,256]{1,0:T(8,128)(2,1)S(1)}, u32[]{:S(2)}, u32[]{:S(2)}) collective-permute-start(bf16[128,256]{1,0:T(8,128)(2,1)S(1)} %update.2.refs_3_.own_ref), channel_id=1, source_target_pairs={{0,8},{1,9},{2,10},{3,11},{4,12},{5,13},{6,14},{7,15},{8,0},{9,1},... | collective-permute-start | bytes 196616 | tf_op jit(solution)/shard_map/ppermute | solution.py:349
  34.1 6.8 %collective-permute-start.13 = (bf16[128,256]{1,0:T(8,128)(2,1)S(1)}, bf16[128,256]{1,0:T(8,128)(2,1)S(1)}, u32[]{:S(2)}, u32[]{:S(2)}) collective-permute-start(bf16[128,256]{1,0:T(8,128)(2,1)S(1)} %update.2.refs_3_.own_ref), channel_id=1, source_target_pairs={{0,4},{1,5},{2,6},{3,7},{4,0},{5,1},{6,2},{7,3},{8,12},{9,13},{10,... | collective-permute-start | bytes 196616 | tf_op jit(solution)/shard_map/ppermute | solution.py:349
  40.9 9.5 %collective-permute-start.15 = (bf16[384,256]{1,0:T(8,128)(2,1)S(1)}, bf16[384,256]{1,0:T(8,128)(2,1)S(1)}, u32[]{:S(2)}, u32[]{:S(2)}) collective-permute-start(bf16[384,256]{1,0:T(8,128)(2,1)S(1)} %pad_maximum_fusion.5), channel_id=1, source_target_pairs={{0,2},{1,3},{2,0},{3,1},{4,6},{5,7},{6,4},{7,5},{8,10},{9,11},{10,... | collective-permute-start | bytes 589832 | tf_op jit(solution)/shard_map/ppermute | solution.py:349
  43.4 6.9 %collective-permute-start.14 = (bf16[128,256]{1,0:T(8,128)(2,1)S(1)}, bf16[128,256]{1,0:T(8,128)(2,1)S(1)}, u32[]{:S(2)}, u32[]{:S(2)}) collective-permute-start(bf16[128,256]{1,0:T(8,128)(2,1)S(1)} %update.2.refs_3_.own_ref), channel_id=1, source_target_pairs={{0,2},{1,3},{2,0},{3,1},{4,6},{5,7},{6,4},{7,5},{8,10},{9,11},{10,... | collective-permute-start | bytes 196616 | tf_op jit(solution)/shard_map/ppermute | solution.py:349
  46.0 6.5 %collective-permute-start.9 = (bf16[128,256]{1,0:T(8,128)(2,1)S(1)}, bf16[128,256]{1,0:T(8,128)(2,1)S(1)}, u32[]{:S(2)}, u32[]{:S(2)}) collective-permute-start(bf16[128,256]{1,0:T(8,128)(2,1)S(1)} %update.2.refs_3_.own_ref), channel_id=1, source_target_pairs={{0,15},{1,2},{2,1},{3,4},{4,3},{5,6},{6,5},{7,8},{8,7},{9,10},{10,... | collective-permute-start | bytes 196616 | tf_op jit(solution)/shard_map/ppermute | solution.py:390
  48.2 4.3 %collective-permute-start.10 = (bf16[128,256]{1,0:T(8,128)(2,1)S(1)}, bf16[128,256]{1,0:T(8,128)(2,1)S(1)}, u32[]{:S(2)}, u32[]{:S(2)}) collective-permute-start(bf16[128,256]{1,0:T(8,128)(2,1)S(1)} %update.2.refs_3_.own_ref), channel_id=1, source_target_pairs={{0,1},{1,0},{2,3},{3,2},{4,5},{5,4},{6,7},{7,6},{8,9},{9,8},{10,11... | collective-permute-start | bytes 196616 | tf_op jit(solution)/shard_map/ppermute | solution.py:349
  50.3 7.2 %collective-permute-start.16 = (bf16[512,256]{1,0:T(8,128)(2,1)S(1)}, bf16[512,256]{1,0:T(8,128)(2,1)S(1)}, u32[]{:S(2)}, u32[]{:S(2)}) collective-permute-start(bf16[512,256]{1,0:T(8,128)(2,1)S(1)} %pad_maximum_fusion.1), channel_id=1, source_target_pairs={{0,1},{1,0},{2,3},{3,2},{4,5},{5,4},{6,7},{7,6},{8,9},{9,8},{10,11... | collective-permute-start | bytes 786440 | tf_op jit(solution)/shard_map/ppermute | solution.py:349
  50.4 7.5 %collective-permute-start.17 = (bf16[384,256]{1,0:T(8,128)(2,1)S(1)}, bf16[384,256]{1,0:T(8,128)(2,1)S(1)}, u32[]{:S(2)}, u32[]{:S(2)}) collective-permute-start(bf16[384,256]{1,0:T(8,128)(2,1)S(1)} %collective-permute-done.15.refs_9_), channel_id=1, source_target_pairs={{0,1},{1,0},{2,3},{3,2},{4,5},{5,4},{6,7},{7,6},{8,9},{9,8},{10,11... | collective-permute-start | bytes 589832 | tf_op jit(solution)/shard_map/ppermute | solution.py:349

commit v5 on v4

--- a/solution.py
+++ b/solution.py
@@ -47,14 +47,15 @@
     x, y = position[0:1], position[1:2]
     first = lax.broadcasted_iota(jnp.int32, (8, rows), 0).astype(F32)
     second = lax.broadcasted_iota(jnp.int32, (columns, rows), 0).astype(F32) - reach
-    xc, xs = turn_trig(first * x)
+    xc, xs = turn_trig(jnp.where(first > reach, position[2:3], first * x))
     yc, ys = turn_trig(second * y)
     cosines, sines = [], []
     for a in range(plane // columns):
         pc, ps = xc[a : a + 1], xs[a : a + 1]
         cosines.append(pc * yc - ps * ys)
         sines.append(pc * ys + ps * yc)
-    return jnp.concatenate(cosines, axis=0), jnp.concatenate(sines, axis=0)
+    height = xc[orders : orders + 1], xs[orders : orders + 1]
+    return jnp.concatenate(cosines, axis=0), jnp.concatenate(sines, axis=0), height
 
 
 def in_hbm(x):
@@ -107,7 +108,7 @@
     k2 = (lax.broadcasted_iota(jnp.int32, (16, plane), 0) % 8).astype(F32)
     strength = count / (1.0 + (k0 * k0 + k1 * k1 + k2 * k2) / 16.0)
 
-    cosine, sine = plane_phases(position)
+    cosine, sine, (zc, zs) = plane_phases(position)
     cosine, sine = cosine.T, sine.T
     for m in range(orders):
         even = strength[m : m + 1]
@@ -117,7 +118,6 @@
             odd = strength[8 + m : 9 + m]
             left_ref[reach + m, :, :plane] = (sine * -odd).astype(BF)
             left_ref[reach + m, :, plane:] = (cosine * odd).astype(BF)
-    zc, zs = turn_trig(position[2:3])
     zc_ref[...] = jnp.broadcast_to(zc, (rows, rows)).T
     zs_ref[...] = jnp.broadcast_to(zs, (rows, rows)).T
 
@@ -157,11 +157,11 @@
             which, start = places[pair + side]
             block = packed[which][start + rows : start + rows + extra_rows, :].astype(F32)
             position = (block[0:3, :rows] + block[0:3, rows : 2 * rows]) + block[3:6, :rows]
-            cosine, sine = plane_phases(position)
+            cosine, sine, height = plane_phases(position)
             at = slice(side * rows, (side + 1) * rows)
             right_ref[turn, :plane, at] = cosine.astype(BF)
             right_ref[turn, plane:, at] = sine.astype(BF)
-            heights.append(turn_trig(position[2:3]))
+            heights.append(height)
         wide = span * rows
         for m in range(2 * reach + 1):
             part_ref[turn, m, :, :wide] = dot(left_ref[m], right_ref[turn, :, :wide])

time: 59 us -> 59 us (level)
  no operation moved by 1% of the time
where the time goes in v5:
time: 59 us; the launch traced here: 58.8 us
  Pallas kernels  22.1 us (37%)
  starting transfers between devices  19.8 us (34%)
  waiting for transfers between devices  16.4 us (28%)
    ppermute x16, starting transfers between devices, swap(): lax.ppermute(x, 'atom', [(i, i ^ (odd if i % 2 else even)) for i in range...  16.4 us
    ppermute x16, waiting for transfers between devices, swap(): lax.ppermute(x, 'atom', [(i, i ^ (odd if i % 2 else even)) for i in range...  14.8 us
    pallas_call x2, Pallas kernels, messages(): pl.pallas_call(functools.partial(message_kernel, layer), out_shape=jax.Sh...  9.83 us
    pallas_call x2, Pallas kernels, filters_of(): pl.pallas_call(functools.partial(filter_kernel, layer), out_shape=jax.Sha...  5.1 us
    pallas_call x3, Pallas kernels, coupling(): pl.pallas_call(functools.partial(coupling_kernel, tuple(places), rows), o...  3.46 us
    ppermute x2, starting transfers between devices, neighbour_table(): lax.ppermute(own, 'atom', [(i, (i + (count - 1 if i % 2 == 0 else 1)) % c...  3.45 us
    ppermute x2, waiting for transfers between devices, neighbour_table(): lax.ppermute(own, 'atom', [(i, (i + (count - 1 if i % 2 == 0 else 1)) % c...  1.61 us
    pallas_call x1, Pallas kernels, prepare(): pl.pallas_call(prepare_kernel, out_shape=shapes, grid=(1,), in_specs=[who...  1.53 us
  transfers between devices with their start and end apart: 18, of which 7 were waited for; matrix products, arithmetic and copies ran while one was open for 0% of the time, Pallas kernels for 31%

profile of v5, /device:TPU:0, one launch (start us, length us, event | category | flops | bytes accessed | tf_op | source)
XLA Modules:
  0.0 58.8 jit_solution(3357383387871915783)
XLA Ops:
  0.0 1.5 %prepare.1 = (bf16[144,256]{1,0:T(8,128)(2,1)S(1)}, bf16[13,128,256]{2,1,0:T(8,128)(2,1)S(1)}, f32[128,128]{1,0:T(8,128)S(1)}, f32[128,128]{1,0:T(8,128)S(1)}, f...) custom-call(s32[3,2048]{1,0:T(4,128)} %wave_ref.1, f32[3,128]{1,0:T(4,128)} %position_ref.1, ...), custom_call_target="tpu_custom_call" | custom-call | tf_op jit(solution)/shard_map/prepare/pallas_call | solution.py:137
  1.5 0.0 copy-start.7
  1.6 0.0 copy-start.8
  1.6 5.1 %collective-permute-start.2 = (bf16[144,256]{1,0:T(8,128)(2,1)S(1)}, bf16[144,256]{1,0:T(8,128)(2,1)S(1)}, u32[]{:S(2)}, u32[]{:S(2)}) collective-permute-start(bf16[144,256]{1,0:T(8,128)(2,1)S(1)} %get-tuple-element.19.refs_0_.refs_2_), channel_id=1, source_target_pairs={{0,12},{1,13},{2,14},{3,15},{4,8},{5,9},{6,10},{7,11},{8,4},{9,5},... | collective-permute-start | bytes 221192 | tf_op jit(solution)/shard_map/ppermute | solution.py:349
  6.7 0.0 collective-permute-start.3
  6.7 0.6 %collective-permute-start.4 = (bf16[144,256]{1,0:T(8,128)(2,1)S(1)}, bf16[144,256]{1,0:T(8,128)(2,1)S(1)}, u32[]{:S(2)}, u32[]{:S(2)}) collective-permute-start(bf16[144,256]{1,0:T(8,128)(2,1)S(1)} %get-tuple-element.19.refs_0_.refs_2_), channel_id=1, source_target_pairs={{0,4},{1,5},{2,6},{3,7},{4,0},{5,1},{6,2},{7,3},{8,12},{9,13},{10,... | collective-permute-start | bytes 221192 | tf_op jit(solution)/shard_map/ppermute | solution.py:349
  7.3 2.0 %collective-permute-done.2.refs_1_.refs_3_ = bf16[144,256]{1,0:T(8,128)(2,1)S(1)} collective-permute-done((bf16[144,256]{1,0:T(8,128)(2,1)S(1)}, bf16[144,256]{1,0:T(8,128)(2,1)S(1)}, u32[]{:S(2)}, u32[]{:S(2)}) %collective-permute-start.2) | collective-permute-done | bytes 73760 | tf_op jit(solution)/shard_map/ppermute | solution.py:349
  9.4 3.5 %collective-permute-done.3.refs_2_.refs_4_ = bf16[144,256]{1,0:T(8,128)(2,1)S(1)} collective-permute-done((bf16[144,256]{1,0:T(8,128)(2,1)S(1)}, bf16[144,256]{1,0:T(8,128)(2,1)S(1)}, u32[]{:S(2)}, u32[]{:S(2)}) %collective-permute-start.3) | collective-permute-done | bytes 73760 | tf_op jit(solution)/shard_map/ppermute | solution.py:349
  12.9 0.0 collective-permute-done.4.refs_3_.refs_5_
  12.9 1.6 %collective-permute-start.6 = (bf16[432,256]{1,0:T(8,128)(2,1)S(1)}, bf16[432,256]{1,0:T(8,128)(2,1)S(1)}, u32[]{:S(2)}, u32[]{:S(2)}) collective-permute-start(bf16[432,256]{1,0:T(8,128)(2,1)S(1)} %pad_maximum_fusion.2), channel_id=1, source_target_pairs={{0,2},{1,3},{2,0},{3,1},{4,6},{5,7},{6,4},{7,5},{8,10},{9,11},{10,... | collective-permute-start | bytes 663560 | tf_op jit(solution)/shard_map/ppermute | solution.py:349
  14.5 0.5 collective-permute-start.5
  15.0 1.3 %collective-permute-start = (bf16[128,256]{1,0:T(8,128)(2,1)}, bf16[128,256]{1,0:T(8,128)(2,1)S(1)}, u32[]{:S(2)}, u32[]{:S(2)}) collective-permute-start(bf16[128,256]{1,0:T(8,128)(2,1)} %own_ref.3), channel_id=1, source_target_pairs={{0,15},{1,2},{2,1},{3,4},{4,3},{5,6},{6,5},{7,8},{8,7},{9,10},{10,... | collective-permute-start | bytes 196616 | tf_op jit(solution)/shard_map/ppermute | solution.py:390
  16.3 0.4 collective-permute-start.1
  16.7 2.5 %filters.2.ready_ref = bf16[32,128,256]{2,1,0:T(8,128)(2,1)S(1)} custom-call(f32[64,128]{1,0:T(8,128)S(1)} %get-tuple-element.18.distance_ref, bf16[1,64,512]{2,1,0:T(8,128)(2,1)S(1)} %get-tuple-element.20.rbf_ref, bf16[1,512,256]{2,1,0:T(8,128)(2,1)S(1)} %get-tuple-element.21.filter_ref), custom_call_target="tpu_custom_call" | custom-call | tf_op jit(solution)/shard_map/filters/pallas_call | solution.py:235
  19.2 2.8 %collective-permute-done.5.refs_4_.refs_6_ = bf16[144,256]{1,0:T(8,128)(2,1)S(1)} collective-permute-done((bf16[144,256]{1,0:T(8,128)(2,1)S(1)}, bf16[144,256]{1,0:T(8,128)(2,1)S(1)}, u32[]{:S(2)}, u32[]{:S(2)}) %collective-permute-start.5) | collective-permute-done | bytes 73760 | tf_op jit(solution)/shard_map/ppermute | solution.py:349
  22.1 0.1 collective-permute-start.7
  22.2 0.0 collective-permute-done.6.refs_0_.refs_8_
  22.2 0.5 collective-permute-start.8
  22.7 0.0 collective-permute-done
  22.7 0.0 collective-permute-done.1.refs_5_.refs_7_
  22.7 0.0 copy-done.5
  22.7 0.0 copy-done.7
  22.7 0.0 copy-done.8
  22.7 4.9 %messages.2.message_ref = bf16[128,256]{1,0:T(8,128)(2,1)S(1)} custom-call(s32[64,128]{1,0:T(8,128)S(1)} %copy-done.7, f32[64,128]{1,0:T(8,128)S(1)} %get-tuple-element.18.distance_ref, s32[64,128]{1,0:T(8,128)S(1)} %copy-done.8, bf16[384,256]{1,0:T(8,128)(2,1)S(1)} %pad_maximum_fusion.3.table_ref, bf16[1,64,512]{2,1,0:T(8,128)(2,1)S(1)} %get-tuple-element.20.rbf_ref, ...), custom_call_target="tpu_custom_call" | custom-call | tf_op jit(solution)/shard_map/messages/pallas_call | solution.py:282
  27.7 0.0 copy-start.2
  27.7 0.0 copy-start.3
  27.7 0.0 copy-start.4
  27.7 1.2 %coupling.3.refs_0_ = bf16[128,768]{1,0:T(8,128)(2,1)S(1)} custom-call(bf16[13,128,256]{2,1,0:T(8,128)(2,1)S(1)} %get-tuple-element.22.left_ref, f32[128,128]{1,0:T(8,128)S(1)} %get-tuple-element.23.zc_ref, f32[128,128]{1,0:T(8,128)S(1)} %get-tuple-element.24.zs_ref, bf16[144,256]{1,0:T(8,128)(2,1)S(1)} %get-tuple-element.19.refs_0_.refs_2_, ...), custom_call_target="tpu_custom_call" | custom-call | tf_op jit(solution)/shard_map/coupling/pallas_call | solution.py:188
  28.9 0.0 collective-permute-done.7.refs_1_.refs_9_.refs_0_
  28.9 1.2 %coupling.4.refs_1_ = bf16[128,768]{1,0:T(8,128)(2,1)S(1)} custom-call(bf16[13,128,256]{2,1,0:T(8,128)(2,1)S(1)} %get-tuple-element.22.left_ref, f32[128,128]{1,0:T(8,128)S(1)} %get-tuple-element.23.zc_ref, f32[128,128]{1,0:T(8,128)S(1)} %get-tuple-element.24.zs_ref, bf16[432,256]{1,0:T(8,128)(2,1)S(1)} %collective-permute-done.6.refs_0_.refs_8_, ...), custom_call_target="tpu_custom_call" | custom-call | tf_op jit(solution)/shard_map/coupling/pallas_call | solution.py:188
  30.2 0.0 copy-done.2
  30.2 0.0 copy-done.3
  30.2 0.0 copy-done.4
  30.2 0.4 partial.2
  30.6 0.0 copy-start
  30.6 0.0 copy-start.1
  30.7 0.0 copy-start.6
  30.7 0.0 collective-permute-done.8.refs_1_.refs_2_
  30.7 1.0 %coupling.5.refs_0_.refs_2_ = bf16[128,512]{1,0:T(8,128)(2,1)S(1)} custom-call(bf16[13,128,256]{2,1,0:T(8,128)(2,1)S(1)} %get-tuple-element.22.left_ref, f32[128,128]{1,0:T(8,128)S(1)} %get-tuple-element.23.zc_ref, f32[128,128]{1,0:T(8,128)S(1)} %get-tuple-element.24.zs_ref, bf16[576,256]{1,0:T(8,128)(2,1)S(1)} %collective-permute-done.7.refs_1_.refs_9_.refs_0_, ...), custom_call_target="tpu_custom_call" | custom-call | tf_op jit(solution)/shard_map/coupling/pallas_call | solution.py:188
  31.7 0.4 update.2.refs_3_.own_ref
  32.1 1.9 %collective-permute-start.11 = (bf16[128,256]{1,0:T(8,128)(2,1)S(1)}, bf16[128,256]{1,0:T(8,128)(2,1)S(1)}, u32[]{:S(2)}, u32[]{:S(2)}) collective-permute-start(bf16[128,256]{1,0:T(8,128)(2,1)S(1)} %update.2.refs_3_.own_ref), channel_id=1, source_target_pairs={{0,12},{1,13},{2,14},{3,15},{4,8},{5,9},{6,10},{7,11},{8,4},{9,5},... | collective-permute-start | bytes 196616 | tf_op jit(solution)/shard_map/ppermute | solution.py:349
  34.0 0.0 collective-permute-start.12
  34.0 2.5 %collective-permute-start.13 = (bf16[128,256]{1,0:T(8,128)(2,1)S(1)}, bf16[128,256]{1,0:T(8,128)(2,1)S(1)}, u32[]{:S(2)}, u32[]{:S(2)}) collective-permute-start(bf16[128,256]{1,0:T(8,128)(2,1)S(1)} %update.2.refs_3_.own_ref), channel_id=1, source_target_pairs={{0,4},{1,5},{2,6},{3,7},{4,0},{5,1},{6,2},{7,3},{8,12},{9,13},{10,... | collective-permute-start | bytes 196616 | tf_op jit(solution)/shard_map/ppermute | solution.py:349
  36.5 2.4 %collective-permute-done.11.refs_4_ = bf16[128,256]{1,0:T(8,128)(2,1)S(1)} collective-permute-done((bf16[128,256]{1,0:T(8,128)(2,1)S(1)}, bf16[128,256]{1,0:T(8,128)(2,1)S(1)}, u32[]{:S(2)}, u32[]{:S(2)}) %collective-permute-start.11) | collective-permute-done | bytes 65568 | tf_op jit(solution)/shard_map/ppermute | solution.py:349
  38.9 1.9 %collective-permute-done.12.refs_5_ = bf16[128,256]{1,0:T(8,128)(2,1)S(1)} collective-permute-done((bf16[128,256]{1,0:T(8,128)(2,1)S(1)}, bf16[128,256]{1,0:T(8,128)(2,1)S(1)}, u32[]{:S(2)}, u32[]{:S(2)}) %collective-permute-start.12) | collective-permute-done | bytes 65568 | tf_op jit(solution)/shard_map/ppermute | solution.py:349
  40.9 0.0 collective-permute-done.13.refs_6_
  40.9 2.5 %collective-permute-start.15 = (bf16[384,256]{1,0:T(8,128)(2,1)S(1)}, bf16[384,256]{1,0:T(8,128)(2,1)S(1)}, u32[]{:S(2)}, u32[]{:S(2)}) collective-permute-start(bf16[384,256]{1,0:T(8,128)(2,1)S(1)} %pad_maximum_fusion.5), channel_id=1, source_target_pairs={{0,2},{1,3},{2,0},{3,1},{4,6},{5,7},{6,4},{7,5},{8,10},{9,11},{10,... | collective-permute-start | bytes 589832 | tf_op jit(solution)/shard_map/ppermute | solution.py:349
  43.3 0.1 collective-permute-start.14
  43.4 0.0 copy-done
  43.4 0.0 copy-done.1
  43.4 2.6 %filters.3.ready_ref = bf16[32,128,256]{2,1,0:T(8,128)(2,1)S(1)} custom-call(f32[64,128]{1,0:T(8,128)S(1)} %copy-done.6, bf16[2,64,512]{2,1,0:T(8,128)(2,1)S(1)} %copy-done.1, bf16[2,512,256]{2,1,0:T(8,128)(2,1)S(1)} %copy-done), custom_call_target="tpu_custom_call" | custom-call | tf_op jit(solution)/shard_map/filters/pallas_call | solution.py:235
  46.0 2.2 %collective-permute-start.9 = (bf16[128,256]{1,0:T(8,128)(2,1)S(1)}, bf16[128,256]{1,0:T(8,128)(2,1)S(1)}, u32[]{:S(2)}, u32[]{:S(2)}) collective-permute-start(bf16[128,256]{1,0:T(8,128)(2,1)S(1)} %update.2.refs_3_.own_ref), channel_id=1, source_target_pairs={{0,15},{1,2},{2,1},{3,4},{4,3},{5,6},{6,5},{7,8},{8,7},{9,10},{10,... | collective-permute-start | bytes 196616 | tf_op jit(solution)/shard_map/ppermute | solution.py:390
  48.2 0.0 collective-permute-start.10
  48.2 2.1 %collective-permute-done.14.refs_7_ = bf16[128,256]{1,0:T(8,128)(2,1)S(1)} collective-permute-done((bf16[128,256]{1,0:T(8,128)(2,1)S(1)}, bf16[128,256]{1,0:T(8,128)(2,1)S(1)}, u32[]{:S(2)}, u32[]{:S(2)}) %collective-permute-start.14) | collective-permute-done | bytes 65568 | tf_op jit(solution)/shard_map/ppermute | solution.py:349
  50.3 0.1 collective-permute-start.16
  50.3 0.0 collective-permute-done.15.refs_9_
  50.3 0.5 collective-permute-start.17
  50.8 1.6 %collective-permute-done.9 = bf16[128,256]{1,0:T(8,128)(2,1)S(1)} collective-permute-done((bf16[128,256]{1,0:T(8,128)(2,1)S(1)}, bf16[128,256]{1,0:T(8,128)(2,1)S(1)}, u32[]{:S(2)}, u32[]{:S(2)}) %collective-permute-start.9) | collective-permute-done | bytes 65568 | tf_op jit(solution)/shard_map/ppermute | solution.py:390
  52.4 0.0 collective-permute-done.10.refs_8_
  52.5 4.9 %messages.3.message_ref = bf16[128,256]{1,0:T(8,128)(2,1)S(1)} custom-call(s32[64,128]{1,0:T(8,128)S(1)} %copy-done.7, f32[64,128]{1,0:T(8,128)S(1)} %copy-done.6, s32[64,128]{1,0:T(8,128)S(1)} %copy-done.8, bf16[384,256]{1,0:T(8,128)(2,1)S(1)} %pad_maximum_fusion.4.table_ref, bf16[2,64,512]{2,1,0:T(8,128)(2,1)S(1)} %copy-done.1, ...), custom_call_target="tpu_custom_call" | custom-call | tf_op jit(solution)/shard_map/messages/pallas_call | solution.py:282
  57.4 0.0 collective-permute-done.16.refs_10_
  57.4 0.4 partial.3
  57.9 0.0 collective-permute-done.17.refs_1_
  57.9 1.0 %update.3 = bf16[128,256]{1,0:T(8,128)(2,1)} custom-call(bf16[128,256]{1,0:T(8,128)(2,1)S(1)} %update.2.refs_3_.own_ref, f32[128,256]{1,0:T(8,128)S(1)} %get-tuple-element.28.total_ref, f32[128,256]{1,0:T(8,128)S(1)} %get-tuple-element.29.close_ref, bf16[256,256]{1,0:T(8,128)(2,1)S(1)} %get-tuple-element.30.joint_ref, ...), custom_call_target="tpu_custom_call" | custom-call | tf_op jit(solution)/shard_map/update/pallas_call | solution.py:330
  (10 shorter events, 0.1 us)
Async XLA Ops:
  0.0 22.7 %copy-start.5 = (bf16[128,256]{1,0:T(8,128)(2,1)S(1)}, bf16[128,256]{1,0:T(8,128)(2,1)}, u32[]{:S(2)}) copy-start(bf16[128,256]{1,0:T(8,128)(2,1)} %own_ref.3) | copy-start | bytes 196612
  1.5 21.2 %copy-start.7 = (s32[64,128]{1,0:T(8,128)S(1)}, s32[64,128]{1,0:T(8,128)}, u32[]{:S(2)}) copy-start(s32[64,128]{1,0:T(8,128)} %index_ref.3) | copy-start | bytes 98308
  1.6 21.2 %copy-start.8 = (s32[64,128]{1,0:T(8,128)S(1)}, s32[64,128]{1,0:T(8,128)}, u32[]{:S(2)}) copy-start(s32[64,128]{1,0:T(8,128)} %mask_ref.3) | copy-start | bytes 98308
  1.6 7.8 %collective-permute-start.2 = (bf16[144,256]{1,0:T(8,128)(2,1)S(1)}, bf16[144,256]{1,0:T(8,128)(2,1)S(1)}, u32[]{:S(2)}, u32[]{:S(2)}) collective-permute-start(bf16[144,256]{1,0:T(8,128)(2,1)S(1)} %get-tuple-element.19.refs_0_.refs_2_), channel_id=1, source_target_pairs={{0,12},{1,13},{2,14},{3,15},{4,8},{5,9},{6,10},{7,11},{8,4},{9,5},... | collective-permute-start | bytes 221192 | tf_op jit(solution)/shard_map/ppermute | solution.py:349
  6.7 6.2 %collective-permute-start.3 = (bf16[144,256]{1,0:T(8,128)(2,1)S(1)}, bf16[144,256]{1,0:T(8,128)(2,1)S(1)}, u32[]{:S(2)}, u32[]{:S(2)}) collective-permute-start(bf16[144,256]{1,0:T(8,128)(2,1)S(1)} %get-tuple-element.19.refs_0_.refs_2_), channel_id=1, source_target_pairs={{0,8},{1,9},{2,10},{3,11},{4,12},{5,13},{6,14},{7,15},{8,0},{9,1},... | collective-permute-start | bytes 221192 | tf_op jit(solution)/shard_map/ppermute | solution.py:349
  6.7 6.2 %collective-permute-start.4 = (bf16[144,256]{1,0:T(8,128)(2,1)S(1)}, bf16[144,256]{1,0:T(8,128)(2,1)S(1)}, u32[]{:S(2)}, u32[]{:S(2)}) collective-permute-start(bf16[144,256]{1,0:T(8,128)(2,1)S(1)} %get-tuple-element.19.refs_0_.refs_2_), channel_id=1, source_target_pairs={{0,4},{1,5},{2,6},{3,7},{4,0},{5,1},{6,2},{7,3},{8,12},{9,13},{10,... | collective-permute-start | bytes 221192 | tf_op jit(solution)/shard_map/ppermute | solution.py:349
  12.9 9.2 %collective-permute-start.6 = (bf16[432,256]{1,0:T(8,128)(2,1)S(1)}, bf16[432,256]{1,0:T(8,128)(2,1)S(1)}, u32[]{:S(2)}, u32[]{:S(2)}) collective-permute-start(bf16[432,256]{1,0:T(8,128)(2,1)S(1)} %pad_maximum_fusion.2), channel_id=1, source_target_pairs={{0,2},{1,3},{2,0},{3,1},{4,6},{5,7},{6,4},{7,5},{8,10},{9,11},{10,... | collective-permute-start | bytes 663560 | tf_op jit(solution)/shard_map/ppermute | solution.py:349
  14.5 7.5 %collective-permute-start.5 = (bf16[144,256]{1,0:T(8,128)(2,1)S(1)}, bf16[144,256]{1,0:T(8,128)(2,1)S(1)}, u32[]{:S(2)}, u32[]{:S(2)}) collective-permute-start(bf16[144,256]{1,0:T(8,128)(2,1)S(1)} %get-tuple-element.19.refs_0_.refs_2_), channel_id=1, source_target_pairs={{0,2},{1,3},{2,0},{3,1},{4,6},{5,7},{6,4},{7,5},{8,10},{9,11},{10,... | collective-permute-start | bytes 221192 | tf_op jit(solution)/shard_map/ppermute | solution.py:349
  15.0 7.6 %collective-permute-start = (bf16[128,256]{1,0:T(8,128)(2,1)}, bf16[128,256]{1,0:T(8,128)(2,1)S(1)}, u32[]{:S(2)}, u32[]{:S(2)}) collective-permute-start(bf16[128,256]{1,0:T(8,128)(2,1)} %own_ref.3), channel_id=1, source_target_pairs={{0,15},{1,2},{2,1},{3,4},{4,3},{5,6},{6,5},{7,8},{8,7},{9,10},{10,... | collective-permute-start | bytes 196616 | tf_op jit(solution)/shard_map/ppermute | solution.py:390
  16.3 6.3 %collective-permute-start.1 = (bf16[144,256]{1,0:T(8,128)(2,1)S(1)}, bf16[144,256]{1,0:T(8,128)(2,1)S(1)}, u32[]{:S(2)}, u32[]{:S(2)}) collective-permute-start(bf16[144,256]{1,0:T(8,128)(2,1)S(1)} %get-tuple-element.19.refs_0_.refs_2_), channel_id=1, source_target_pairs={{0,1},{1,0},{2,3},{3,2},{4,5},{5,4},{6,7},{7,6},{8,9},{9,8},{10,11... | collective-permute-start | bytes 221192 | tf_op jit(solution)/shard_map/ppermute | solution.py:349
  22.1 6.9 %collective-permute-start.7 = (bf16[576,256]{1,0:T(8,128)(2,1)S(1)}, bf16[576,256]{1,0:T(8,128)(2,1)S(1)}, u32[]{:S(2)}, u32[]{:S(2)}) collective-permute-start(bf16[576,256]{1,0:T(8,128)(2,1)S(1)} %pad_maximum_fusion), channel_id=1, source_target_pairs={{0,1},{1,0},{2,3},{3,2},{4,5},{5,4},{6,7},{7,6},{8,9},{9,8},{10,11... | collective-permute-start | bytes 884744 | tf_op jit(solution)/shard_map/ppermute | solution.py:349
  22.2 8.5 %collective-permute-start.8 = (bf16[432,256]{1,0:T(8,128)(2,1)S(1)}, bf16[432,256]{1,0:T(8,128)(2,1)S(1)}, u32[]{:S(2)}, u32[]{:S(2)}) collective-permute-start(bf16[432,256]{1,0:T(8,128)(2,1)S(1)} %collective-permute-done.6.refs_0_.refs_8_), channel_id=1, source_target_pairs={{0,1},{1,0},{2,3},{3,2},{4,5},{5,4},{6,7},{7,6},{8,9},{9,8},{10,11... | collective-permute-start | bytes 663560 | tf_op jit(solution)/shard_map/ppermute | solution.py:349
  27.7 2.5 %copy-start.2 = (bf16[2,256,256]{2,1,0:T(8,128)(2,1)S(1)}, bf16[2,256,256]{2,1,0:T(8,128)(2,1)}, u32[]{:S(2)}) copy-start(bf16[2,256,256]{2,1,0:T(8,128)(2,1)} %short_ref.3) | copy-start | bytes 786436
  27.7 2.5 %copy-start.3 = (bf16[2,256,256]{2,1,0:T(8,128)(2,1)S(1)}, bf16[2,256,256]{2,1,0:T(8,128)(2,1)}, u32[]{:S(2)}) copy-start(bf16[2,256,256]{2,1,0:T(8,128)(2,1)} %mixing_ref.3) | copy-start | bytes 786436
  27.7 2.5 %copy-start.4 = (bf16[2,256,256]{2,1,0:T(8,128)(2,1)S(1)}, bf16[2,256,256]{2,1,0:T(8,128)(2,1)}, u32[]{:S(2)}) copy-start(bf16[2,256,256]{2,1,0:T(8,128)(2,1)} %long_ref.3) | copy-start | bytes 786436
  30.6 12.8 %copy-start = (bf16[2,512,256]{2,1,0:T(8,128)(2,1)S(1)}, bf16[2,512,256]{2,1,0:T(8,128)(2,1)}, u32[]{:S(2)}) copy-start(bf16[2,512,256]{2,1,0:T(8,128)(2,1)} %filter_ref.5) | copy-start | bytes 1572868
  30.6 12.8 %copy-start.1 = (bf16[2,64,512]{2,1,0:T(8,128)(2,1)S(1)}, bf16[2,64,512]{2,1,0:T(8,128)(2,1)}, u32[]{:S(2)}) copy-start(bf16[2,64,512]{2,1,0:T(8,128)(2,1)} %rbf_ref.5) | copy-start | bytes 393220
  30.7 12.8 %copy-start.6 = (f32[64,128]{1,0:T(8,128)S(1)}, f32[64,128]{1,0:T(8,128)}, u32[]{:S(2)}) copy-start(f32[64,128]{1,0:T(8,128)} %distance_ref.5) | copy-start | bytes 98308
  32.1 6.8 %collective-permute-start.11 = (bf16[128,256]{1,0:T(8,128)(2,1)S(1)}, bf16[128,256]{1,0:T(8,128)(2,1)S(1)}, u32[]{:S(2)}, u32[]{:S(2)}) collective-permute-start(bf16[128,256]{1,0:T(8,128)(2,1)S(1)} %update.2.refs_3_.own_ref), channel_id=1, source_target_pairs={{0,12},{1,13},{2,14},{3,15},{4,8},{5,9},{6,10},{7,11},{8,4},{9,5},... | collective-permute-start | bytes 196616 | tf_op jit(solution)/shard_map/ppermute | solution.py:349
  34.0 6.8 %collective-permute-start.12 = (bf16[128,256]{1,0:T(8,128)(2,1)S(1)}, bf16[128,256]{1,0:T(8,128)(2,1)S(1)}, u32[]{:S(2)}, u32[]{:S(2)}) collective-permute-start(bf16[128,256]{1,0:T(8,128)(2,1)S(1)} %update.2.refs_3_.own_ref), channel_id=1, source_target_pairs={{0,8},{1,9},{2,10},{3,11},{4,12},{5,13},{6,14},{7,15},{8,0},{9,1},... | collective-permute-start | bytes 196616 | tf_op jit(solution)/shard_map/ppermute | solution.py:349
  34.0 6.8 %collective-permute-start.13 = (bf16[128,256]{1,0:T(8,128)(2,1)S(1)}, bf16[128,256]{1,0:T(8,128)(2,1)S(1)}, u32[]{:S(2)}, u32[]{:S(2)}) collective-permute-start(bf16[128,256]{1,0:T(8,128)(2,1)S(1)} %update.2.refs_3_.own_ref), channel_id=1, source_target_pairs={{0,4},{1,5},{2,6},{3,7},{4,0},{5,1},{6,2},{7,3},{8,12},{9,13},{10,... | collective-permute-start | bytes 196616 | tf_op jit(solution)/shard_map/ppermute | solution.py:349
  40.9 9.5 %collective-permute-start.15 = (bf16[384,256]{1,0:T(8,128)(2,1)S(1)}, bf16[384,256]{1,0:T(8,128)(2,1)S(1)}, u32[]{:S(2)}, u32[]{:S(2)}) collective-permute-start(bf16[384,256]{1,0:T(8,128)(2,1)S(1)} %pad_maximum_fusion.5), channel_id=1, source_target_pairs={{0,2},{1,3},{2,0},{3,1},{4,6},{5,7},{6,4},{7,5},{8,10},{9,11},{10,... | collective-permute-start | bytes 589832 | tf_op jit(solution)/shard_map/ppermute | solution.py:349
  43.3 6.9 %collective-permute-start.14 = (bf16[128,256]{1,0:T(8,128)(2,1)S(1)}, bf16[128,256]{1,0:T(8,128)(2,1)S(1)}, u32[]{:S(2)}, u32[]{:S(2)}) collective-permute-start(bf16[128,256]{1,0:T(8,128)(2,1)S(1)} %update.2.refs_3_.own_ref), channel_id=1, source_target_pairs={{0,2},{1,3},{2,0},{3,1},{4,6},{5,7},{6,4},{7,5},{8,10},{9,11},{10,... | collective-permute-start | bytes 196616 | tf_op jit(solution)/shard_map/ppermute | solution.py:349
  46.0 6.5 %collective-permute-start.9 = (bf16[128,256]{1,0:T(8,128)(2,1)S(1)}, bf16[128,256]{1,0:T(8,128)(2,1)S(1)}, u32[]{:S(2)}, u32[]{:S(2)}) collective-permute-start(bf16[128,256]{1,0:T(8,128)(2,1)S(1)} %update.2.refs_3_.own_ref), channel_id=1, source_target_pairs={{0,15},{1,2},{2,1},{3,4},{4,3},{5,6},{6,5},{7,8},{8,7},{9,10},{10,... | collective-permute-start | bytes 196616 | tf_op jit(solution)/shard_map/ppermute | solution.py:390
  48.2 4.3 %collective-permute-start.10 = (bf16[128,256]{1,0:T(8,128)(2,1)S(1)}, bf16[128,256]{1,0:T(8,128)(2,1)S(1)}, u32[]{:S(2)}, u32[]{:S(2)}) collective-permute-start(bf16[128,256]{1,0:T(8,128)(2,1)S(1)} %update.2.refs_3_.own_ref), channel_id=1, source_target_pairs={{0,1},{1,0},{2,3},{3,2},{4,5},{5,4},{6,7},{7,6},{8,9},{9,8},{10,11... | collective-permute-start | bytes 196616 | tf_op jit(solution)/shard_map/ppermute | solution.py:349
  50.3 7.2 %collective-permute-start.16 = (bf16[512,256]{1,0:T(8,128)(2,1)S(1)}, bf16[512,256]{1,0:T(8,128)(2,1)S(1)}, u32[]{:S(2)}, u32[]{:S(2)}) collective-permute-start(bf16[512,256]{1,0:T(8,128)(2,1)S(1)} %pad_maximum_fusion.1), channel_id=1, source_target_pairs={{0,1},{1,0},{2,3},{3,2},{4,5},{5,4},{6,7},{7,6},{8,9},{9,8},{10,11... | collective-permute-start | bytes 786440 | tf_op jit(solution)/shard_map/ppermute | solution.py:349
  50.3 7.5 %collective-permute-start.17 = (bf16[384,256]{1,0:T(8,128)(2,1)S(1)}, bf16[384,256]{1,0:T(8,128)(2,1)S(1)}, u32[]{:S(2)}, u32[]{:S(2)}) collective-permute-start(bf16[384,256]{1,0:T(8,128)(2,1)S(1)} %collective-permute-done.15.refs_9_), channel_id=1, source_target_pairs={{0,1},{1,0},{2,3},{3,2},{4,5},{5,4},{6,7},{7,6},{8,9},{9,8},{10,11... | collective-permute-start | bytes 589832 | tf_op jit(solution)/shard_map/ppermute | solution.py:349
